TPU v7x, 32 devices: a whole 2x2x4 slice. The times are simulated.
32 devices in a mesh: dp: 4 (over y, core), fsdp: 8 (over z, x).
Axes of the slice: x: 2, y: 2, z: 4, core: 2. Of those that a mesh axis runs over, the one named last changes fastest.
Arguments:
- frames: bfloat16 [16384, 2, 1024], P(('dp', 'fsdp')), may hold values from -6 to 6
- cotangent: bfloat16 [16384, 2, 1024], P(('dp', 'fsdp')), may hold values from -12 to 12
- segment_ids: int32 [16384], replicated, may hold values from 0 to 1023, never falling along the last dimension, each value on 1 to 256 neighbouring positions
- qkv_weight: float32 [2, 1024, 3072], P(None, 'fsdp'), may hold values from -0.1875 to 0.1875
- mix_weight: float32 [2, 1024, 1024], P(None, 'fsdp'), may hold values from -0.25 to 0.25
- inner_weight: float32 [2, 1024, 5632], P(None, 'fsdp'), may hold values from -0.1875 to 0.1875
- down_weight: float32 [2, 2816, 1024], P(None, 'fsdp'), may hold values from -0.109375 to 0.109375
- norm_gains: float32 [2, 1024], P(None, 'fsdp'), may hold values from 0.5 to 1.5
- qkv_moment: float32 [2, 1024, 3072], P(None, 'fsdp'), may hold values from -448 to 448
- mix_moment: float32 [2, 1024, 1024], P(None, 'fsdp'), may hold values from -448 to 448
- inner_moment: float32 [2, 1024, 5632], P(None, 'fsdp'), may hold values from -224 to 224
- down_moment: float32 [2, 2816, 1024], P(None, 'fsdp'), may hold values from -448 to 448
- gains_moment: float32 [2, 1024], P(None, 'fsdp'), may hold values from -1024 to 1024
- qkv_average: float32 [2, 1024, 3072], P(None, 'fsdp'), may hold values from -0.1875 to 0.1875
- mix_average: float32 [2, 1024, 1024], P(None, 'fsdp'), may hold values from -0.25 to 0.25
- inner_average: float32 [2, 1024, 5632], P(None, 'fsdp'), may hold values from -0.1875 to 0.1875
- down_average: float32 [2, 2816, 1024], P(None, 'fsdp'), may hold values from -0.109375 to 0.109375
- gains_average: float32 [2, 1024], P(None, 'fsdp'), may hold values from 0.1 to 1.9
Outputs:
- layer_out: bfloat16 [16384, 2, 1024], P(('dp', 'fsdp'))
- frames_grad: bfloat16 [16384, 2, 1024], P(('dp', 'fsdp'))
- qkv_grad: float32 [2, 1024, 3072], P(None, 'fsdp')
- mix_grad: float32 [2, 1024, 1024], P(None, 'fsdp')
- inner_grad: float32 [2, 1024, 5632], P(None, 'fsdp')
- down_grad: float32 [2, 2816, 1024], P(None, 'fsdp')
- gains_grad: float32 [2, 1024], P(None, 'fsdp')
- qkv_moment_new: float32 [2, 1024, 3072], P(None, 'fsdp')
- mix_moment_new: float32 [2, 1024, 1024], P(None, 'fsdp')
- inner_moment_new: float32 [2, 1024, 5632], P(None, 'fsdp')
- down_moment_new: float32 [2, 2816, 1024], P(None, 'fsdp')
- gains_moment_new: float32 [2, 1024], P(None, 'fsdp')
- qkv_average_new: float32 [2, 1024, 3072], P(None, 'fsdp')
- mix_average_new: float32 [2, 1024, 1024], P(None, 'fsdp')
- inner_average_new: float32 [2, 1024, 5632], P(None, 'fsdp')
- down_average_new: float32 [2, 2816, 1024], P(None, 'fsdp')
- gains_average_new: float32 [2, 1024], P(None, 'fsdp')
- qkv_weight_new: float32 [2, 1024, 3072], P(None, 'fsdp')
- mix_weight_new: float32 [2, 1024, 1024], P(None, 'fsdp')
- inner_weight_new: float32 [2, 1024, 5632], P(None, 'fsdp')
- down_weight_new: float32 [2, 2816, 1024], P(None, 'fsdp')
- gains_new: float32 [2, 1024], P(None, 'fsdp')
Inputs may be any that keep to these rules, and one draw needn't show every extreme that they name: `segment_ids`: ids never fall along the frames and rise by at most 1 from a frame to the next.
All inputs are finite; a program needn't handle non-finite values.
Results may differ from a plain program's by a relative error of at most 0.017.
Values may be sent and summed in bfloat16 or wider, within the bound.
A program may use at most 384 MiB of HBM per device.

v0:
```python
import math

import jax
import jax.numpy as jnp
from jax import lax
from jax.sharding import PartitionSpec as P

HEADS = 16


norm_eps = 1e-05
momentum_rate = 0.5
average_rate = 0.5
step_rate = 0.05


def shifted(value, axis, steps):
    count = lax.axis_size(axis)
    first, last = (max(0, -steps), min(count, count - steps))
    return lax.ppermute(value, axis, [(source, source + steps) for source in range(first, last)])


def scale_rows(values):
    return lax.rsqrt(jnp.mean(values * values, axis=-1, keepdims=True) + norm_eps)


def silu_slope(values):
    squashed = jax.nn.sigmoid(values)
    return squashed * (1.0 + values * (1.0 - squashed))


def norm_back(grad_in, normed, gain_row, inverse):
    scaled = grad_in * gain_row
    return inverse * (scaled - normed * jnp.mean(scaled * normed, axis=-1, keepdims=True))


def owner_update(weight, gradient, moment, average, step_size):
    moment_new = momentum_rate * moment + gradient
    weight_new = weight - step_size * (gradient + momentum_rate * moment_new)
    average_new = average_rate * average + (1.0 - average_rate) * weight_new
    return (moment_new, average_new, weight_new)


def per_device(
    frames,
    cotangent,
    segment_ids,
    qkv_weight,
    mix_weight,
    inner_weight,
    down_weight,
    norm_gains,
    qkv_moment,
    mix_moment,
    inner_moment,
    down_moment,
    gains_moment,
    qkv_average,
    mix_average,
    inner_average,
    down_average,
    gains_average,
):
    frame_count, positions, model_width = frames.shape
    head_count = HEADS
    head_size = model_width // head_count
    hidden_width = inner_weight.shape[2] // 2
    dp_count = lax.axis_size("dp")
    fsdp_count = lax.axis_size("fsdp")
    total_frames = frame_count * dp_count * fsdp_count
    device = lax.axis_index("dp") * fsdp_count + lax.axis_index("fsdp")
    first_frame = device * frame_count
    padded_ids = jnp.concatenate([jnp.full((1,), -1, jnp.int32), segment_ids])
    id_window = lax.dynamic_slice_in_dim(padded_ids, first_frame, frame_count + 1)
    carried = id_window[1:] == id_window[:-1]
    places = jnp.arange(positions)
    causal = places[None, :] <= places[:, None]
    allowed = jnp.concatenate(
        [
            jnp.broadcast_to(carried[:, None, None, None], (frame_count, 1, positions, positions)),
            jnp.broadcast_to(causal[None, None], (frame_count, 1, positions, positions)),
        ],
        axis=-1,
    )
    root_size = math.sqrt(head_size)
    head_shape = (frame_count, positions, head_count, head_size)
    flat_shape = (frame_count, positions, model_width)
    attn_local = (
        norm_gains.astype(jnp.bfloat16),
        qkv_weight.astype(jnp.bfloat16),
        mix_weight.astype(jnp.bfloat16),
    )
    inner_local = (inner_weight.astype(jnp.bfloat16), down_weight.astype(jnp.bfloat16))
    gains_low, qkv_low, mix_low = (
        lax.all_gather(attn_local[0], "fsdp", axis=1, tiled=True),
        lax.all_gather(attn_local[1], "fsdp", axis=1, tiled=True),
        lax.all_gather(attn_local[2], "fsdp", axis=1, tiled=True),
    )
    gains_f32 = gains_low.astype(jnp.float32)
    frames_f32 = frames.astype(jnp.float32)
    first_scale = scale_rows(frames_f32)
    normed_one = frames_f32 * first_scale
    inputs_one = (normed_one * gains_f32[0]).astype(jnp.bfloat16)
    qkv_rows = jnp.einsum(
        "fpd,pde->fpe", inputs_one, qkv_low, preferred_element_type=jnp.float32
    ).astype(jnp.bfloat16)
    kv_rows = qkv_rows[..., model_width:]
    edge_rows = shifted(kv_rows[-1], ("dp", "fsdp"), 1)
    kv_before = jnp.concatenate([edge_rows[None], kv_rows[:-1]], axis=0)
    queries = qkv_rows[..., :model_width].reshape(head_shape)
    key_rows = jnp.concatenate(
        [
            kv_before[..., :model_width].reshape(head_shape),
            kv_rows[..., :model_width].reshape(head_shape),
        ],
        axis=1,
    )
    value_rows = jnp.concatenate(
        [
            kv_before[..., model_width:].reshape(head_shape),
            kv_rows[..., model_width:].reshape(head_shape),
        ],
        axis=1,
    )
    scores = (
        jnp.einsum("fphe,fqhe->fhpq", queries, key_rows, preferred_element_type=jnp.float32)
        / root_size
    )
    masked = jnp.where(allowed, scores, -1e30)
    row_max = jnp.max(masked, axis=-1, keepdims=True)
    exponent = jnp.where(allowed, jnp.exp(masked - row_max), 0.0)
    attn_probs = exponent / jnp.sum(exponent, axis=-1, keepdims=True)
    probs_low = attn_probs.astype(jnp.bfloat16)
    mixed_heads = jnp.einsum(
        "fhpq,fqhe->fphe", probs_low, value_rows, preferred_element_type=jnp.float32
    )
    mixed_low = mixed_heads.reshape(flat_shape).astype(jnp.bfloat16)
    residual = frames_f32 + jnp.einsum(
        "fpd,pde->fpe", mixed_low, mix_low, preferred_element_type=jnp.float32
    )
    inner_full, down_full = (
        lax.all_gather(inner_local[0], "fsdp", axis=1, tiled=True),
        lax.all_gather(inner_local[1], "fsdp", axis=1, tiled=True),
    )
    second_scale = scale_rows(residual)
    normed_two = residual * second_scale
    inputs_two = (normed_two * gains_f32[1]).astype(jnp.bfloat16)
    gate_up = jnp.einsum("fpd,pde->fpe", inputs_two, inner_full, preferred_element_type=jnp.float32)
    gate_part = gate_up[..., :hidden_width]
    up_part = gate_up[..., hidden_width:]
    activated = jax.nn.silu(gate_part)
    hidden = (activated * up_part).astype(jnp.bfloat16)
    layer_out = (
        residual + jnp.einsum("fpk,pkd->fpd", hidden, down_full, preferred_element_type=jnp.float32)
    ).astype(jnp.bfloat16)
    cot_f32 = cotangent.astype(jnp.float32)
    inner_full, down_full = (
        lax.all_gather(inner_local[0], "fsdp", axis=1, tiled=True),
        lax.all_gather(inner_local[1], "fsdp", axis=1, tiled=True),
    )
    down_term = jnp.einsum("fpk,fpd->pkd", hidden, cotangent, preferred_element_type=jnp.float32)
    hidden_grad = jnp.einsum(
        "fpd,pkd->fpk", cotangent, down_full, preferred_element_type=jnp.float32
    )
    gate_up_grad = jnp.concatenate(
        [hidden_grad * up_part * silu_slope(gate_part), hidden_grad * activated], axis=-1
    ).astype(jnp.bfloat16)
    inner_term = jnp.einsum(
        "fpd,fpe->pde", inputs_two, gate_up_grad, preferred_element_type=jnp.float32
    )
    inputs_two_grad = jnp.einsum(
        "fpe,pde->fpd", gate_up_grad, inner_full, preferred_element_type=jnp.float32
    )
    inner_share, down_share = (
        lax.psum_scatter(
            inner_term.astype(jnp.bfloat16), "fsdp", scatter_dimension=1, tiled=True
        ).astype(jnp.float32),
        lax.psum_scatter(
            down_term.astype(jnp.bfloat16), "fsdp", scatter_dimension=1, tiled=True
        ).astype(jnp.float32),
    )
    second_gain = jnp.sum(inputs_two_grad * normed_two, axis=(0, 1))
    residual_grad = cot_f32 + norm_back(inputs_two_grad, normed_two, gains_f32[1], second_scale)
    residual_low = residual_grad.astype(jnp.bfloat16)
    gains_low, qkv_low, mix_low = (
        lax.all_gather(attn_local[0], "fsdp", axis=1, tiled=True),
        lax.all_gather(attn_local[1], "fsdp", axis=1, tiled=True),
        lax.all_gather(attn_local[2], "fsdp", axis=1, tiled=True),
    )
    gains_f32 = gains_low.astype(jnp.float32)
    mix_term = jnp.einsum(
        "fpd,fpe->pde", mixed_low, residual_low, preferred_element_type=jnp.float32
    )
    mixed_grad = (
        jnp.einsum("fpe,pde->fpd", residual_low, mix_low, preferred_element_type=jnp.float32)
        .astype(jnp.bfloat16)
        .reshape(head_shape)
    )
    probs_grad = jnp.einsum(
        "fphe,fqhe->fhpq", mixed_grad, value_rows, preferred_element_type=jnp.float32
    )
    scores_grad = (
        attn_probs * (probs_grad - jnp.sum(attn_probs * probs_grad, axis=-1, keepdims=True))
    ).astype(jnp.bfloat16)
    query_grad = (
        jnp.einsum("fhpq,fqhe->fphe", scores_grad, key_rows, preferred_element_type=jnp.float32)
        / root_size
    )
    key_grad = (
        jnp.einsum("fhpq,fphe->fqhe", scores_grad, queries, preferred_element_type=jnp.float32)
        / root_size
    )
    value_grad = jnp.einsum(
        "fhpq,fphe->fqhe", probs_low, mixed_grad, preferred_element_type=jnp.float32
    )
    kv_grad_before = jnp.concatenate(
        [
            key_grad[:, :positions].reshape(flat_shape),
            value_grad[:, :positions].reshape(flat_shape),
        ],
        axis=-1,
    )
    kv_grad_here = jnp.concatenate(
        [
            key_grad[:, positions:].reshape(flat_shape),
            value_grad[:, positions:].reshape(flat_shape),
        ],
        axis=-1,
    )
    edge_grad = shifted(kv_grad_before[0], ("dp", "fsdp"), -1)
    kv_grad = kv_grad_here + jnp.concatenate([kv_grad_before[1:], edge_grad[None]], axis=0)
    qkv_grad_low = jnp.concatenate([query_grad.reshape(flat_shape), kv_grad], axis=-1).astype(
        jnp.bfloat16
    )
    qkv_term = jnp.einsum(
        "fpd,fpe->pde", inputs_one, qkv_grad_low, preferred_element_type=jnp.float32
    )
    inputs_one_grad = jnp.einsum(
        "fpe,pde->fpd", qkv_grad_low, qkv_low, preferred_element_type=jnp.float32
    )
    first_gain = jnp.sum(inputs_one_grad * normed_one, axis=(0, 1))
    frames_grad = (
        residual_grad + norm_back(inputs_one_grad, normed_one, gains_f32[0], first_scale)
    ).astype(jnp.bfloat16)
    gains_term = jnp.stack([first_gain, second_gain])
    gains_share, qkv_share, mix_share = (
        lax.psum_scatter(
            gains_term.astype(jnp.bfloat16), "fsdp", scatter_dimension=1, tiled=True
        ).astype(jnp.float32),
        lax.psum_scatter(
            qkv_term.astype(jnp.bfloat16), "fsdp", scatter_dimension=1, tiled=True
        ).astype(jnp.float32),
        lax.psum_scatter(
            mix_term.astype(jnp.bfloat16), "fsdp", scatter_dimension=1, tiled=True
        ).astype(jnp.float32),
    )
    gains_grad, qkv_grad, mix_grad, inner_grad, down_grad = (
        lax.psum(gains_share.astype(jnp.bfloat16), "dp").astype(jnp.float32),
        lax.psum(qkv_share.astype(jnp.bfloat16), "dp").astype(jnp.float32),
        lax.psum(mix_share.astype(jnp.bfloat16), "dp").astype(jnp.float32),
        lax.psum(inner_share.astype(jnp.bfloat16), "dp").astype(jnp.float32),
        lax.psum(down_share.astype(jnp.bfloat16), "dp").astype(jnp.float32),
    )
    step_size = step_rate / math.sqrt(total_frames)
    qkv_new = owner_update(qkv_weight, qkv_grad, qkv_moment, qkv_average, step_size)
    mix_new = owner_update(mix_weight, mix_grad, mix_moment, mix_average, step_size)
    inner_new = owner_update(inner_weight, inner_grad, inner_moment, inner_average, step_size)
    down_new = owner_update(down_weight, down_grad, down_moment, down_average, step_size)
    gains_new = owner_update(norm_gains, gains_grad, gains_moment, gains_average, step_size)
    return (
        layer_out,
        frames_grad,
        qkv_grad,
        mix_grad,
        inner_grad,
        down_grad,
        gains_grad,
        qkv_new[0],
        mix_new[0],
        inner_new[0],
        down_new[0],
        gains_new[0],
        qkv_new[1],
        mix_new[1],
        inner_new[1],
        down_new[1],
        gains_new[1],
        qkv_new[2],
        mix_new[2],
        inner_new[2],
        down_new[2],
        gains_new[2],
    )


def solution(mesh):
    placed = (
        P(("dp", "fsdp"), None, None),
        P(("dp", "fsdp"), None, None),
        P(),
        P(None, "fsdp", None),
        P(None, "fsdp", None),
        P(None, "fsdp", None),
        P(None, "fsdp", None),
        P(None, "fsdp"),
        P(None, "fsdp", None),
        P(None, "fsdp", None),
        P(None, "fsdp", None),
        P(None, "fsdp", None),
        P(None, "fsdp"),
        P(None, "fsdp", None),
        P(None, "fsdp", None),
        P(None, "fsdp", None),
        P(None, "fsdp", None),
        P(None, "fsdp"),
    )
    return jax.shard_map(
        per_device,
        mesh=mesh,
        in_specs=placed,
        out_specs=(
            P(("dp", "fsdp"), None, None),
            P(("dp", "fsdp"), None, None),
            P(None, "fsdp", None),
            P(None, "fsdp", None),
            P(None, "fsdp", None),
            P(None, "fsdp", None),
            P(None, "fsdp"),
            P(None, "fsdp", None),
            P(None, "fsdp", None),
            P(None, "fsdp", None),
            P(None, "fsdp", None),
            P(None, "fsdp"),
            P(None, "fsdp", None),
            P(None, "fsdp", None),
            P(None, "fsdp", None),
            P(None, "fsdp", None),
            P(None, "fsdp"),
            P(None, "fsdp", None),
            P(None, "fsdp", None),
            P(None, "fsdp", None),
            P(None, "fsdp", None),
            P(None, "fsdp"),
        ),
        check_vma=False,
    )
```

profile of v0, /device:TPU:0, one launch (start us, length us, event | category | flops | bytes accessed | tf_op | source)
XLA Modules:
  0.0 2027.8 jit_solution(269927858604653945)
XLA Ops:
  20.3 22.4 %all_gather.20 = bf16[2,1024]{1,0:T(2,128)(2,1)S(1)} all-gather(bf16[2,128]{1,0:T(2,128)(2,1)S(1)} %convert_element_type.111), channel_id=1, replica_groups=mesh['dp'=4,'fsdp'=8] {'fsdp'}, dimensions={1}, use_global_device_ids=true | all-gather | bytes 4608 | tf_op jit(solution)/shard_map/all_gather | solution.py:95
  43.4 146.5 %all-gather.5.cloned.1.call-done = bf16[2,1024,3072]{2,1,0:T(8,128)(2,1)} async-done(((bf16[2,128,3072]{2,1,0:T(8,128)(2,1)}), bf16[2,1024,3072]{2,1,0:T(8,128)(2,1)}) %all-gather.5.cloned.1.call-update) | async-done | bytes 12582928 | tf_op jit(solution)/shard_map/all_gather | solution.py:96
  189.9 11.8 convert_bitcast_fusion
  288.7 30.7 %fusion.52 = (f32[512,16,2]{2,1,0:T(8,128)}, f32[512,16,2,4]{3,2,1,0:T(2,128)}) fusion(pred[512,2,4]{2,1,0:T(4,128)(4,1)S(1)} %copy.143, bf16[512,2,16,64]{3,1,2,0:T(2,128)(2,1)} %copy.149, bf16[512,2,16,64]{3,1,2,0:T(2,128)(2,1)} %copy.148, bf16[512,2,16,64]{3,1,2,0:T(2,128)(2,1)} %copy.147), kind=kOutput, calls=%fused_computation.117 | convolution fusion | flops 17104900 | bytes 6623232 | tf_op jit(solution)/shard_map/sub | solution.py:131
  319.4 12.1 broadcast_divide_fusion
  334.9 14.0 fusion.12
  367.4 338.6 %all-gather.9.cloned.1.call-done = bf16[2,1024,5632]{2,1,0:T(8,128)(2,1)} async-done(((bf16[2,128,5632]{2,1,0:T(8,128)(2,1)}), bf16[2,1024,5632]{2,1,0:T(8,128)(2,1)}) %all-gather.9.cloned.1.call-update) | async-done | bytes 23068688 | tf_op jit(solution)/shard_map/all_gather | solution.py:142
  706.0 22.3 %convolution_bitcast_fusion = f32[512,2,5632]{2,0,1:T(8,128)} fusion(bf16[2,1024,5632]{2,1,0:T(8,128)(2,1)} %all-gather.9.cloned.1.call-done, f32[512,2,1024]{2,0,1:T(8,128)} %get-tuple-element.155, f32[1024]{0:T(1024)S(1)} %bitcast.110, f32[512,2]{0,1:T(2,128)S(1)} %add_rsqrt_fusion), kind=kOutput, calls=%fused_computation.3 | convolution fusion | flops 11814305792 | bytes 50339840 | tf_op jit(solution)/shard_map/fpd,pde->fpe/dot_general | solution.py:148
  728.3 143.9 %all-gather.11.cloned.1.call-done = bf16[2,2816,1024]{2,1,0:T(8,128)(2,1)} async-done(((bf16[2,352,1024]{2,1,0:T(8,128)(2,1)}), bf16[2,2816,1024]{2,1,0:T(8,128)(2,1)}) %all-gather.11.cloned.1.call-update) | async-done | bytes 11534352 | tf_op jit(solution)/shard_map/all_gather | solution.py:143
  872.3 21.7 %fusion.2 = (bf16[512,2,2816]{2,0,1:T(8,128)(2,1)}, bf16[512,2,2816]{2,0,1:T(8,128)(2,1)}, bf16[512,2,2816]{2,0,1:T(8,128)(2,1)}) fusion(f32[512,2,5632]{2,0,1:T(8,128)} %convolution_bitcast_fusion, bf16[2,2816,1024]{2,1,0:T(8,128)(2,1)} %all-gather.11.cloned.1.call-done, bf16[512,2,1024]{2,1,0:T(2,128)(2,1)S(1)} %copy-done.19), kind=kOutput, calls=%fused_computation.8 | convolution fusion | flops 5948833792 | bytes 54001664 | tf_op jit(solution)/shard_map/fpd,pkd->fpk/dot_general | solution.py:162
  894.0 22.8 %fusion.22 = (bf16[1024]{0:T(1024)(128)(2,1)}, f32[512,2]{0,1:T(2,128)S(1)}, f32[2,512,1024]{2,1,0:T(8,128)}) fusion(f32[512,2,1024]{2,0,1:T(8,128)} %get-tuple-element.155, f32[512,2]{0,1:T(2,128)S(1)} %add_rsqrt_fusion, f32[1024]{0:T(1024)S(1)} %bitcast.111, bf16[2,1024,5632]{2,1,0:T(8,128)(2,1)} %all-gather.9.cloned.1.call-done, ...), kind=kOutput, calls=%fused_computation.57 | convolution fusion | flops 11840518144 | bytes 43005952 | tf_op jit(solution)/shard_map/fpe,pde->fpd/dot_general | solution.py:171
  927.4 11.7 convolution_convert_fusion.1
  957.3 12.7 convolution_bitcast_fusion.1
  970.1 11.4 fusion.49
  981.5 12.2 copy.165
  1001.1 23.7 %multiply_reduce_fusion = (f32[512,16,2]{2,1,0:T(8,128)}, f32[512,16,2,4]{3,2,1,0:T(2,128)}) fusion(f32[512,16,2,4]{3,2,1,0:T(2,128)} %copy-done.7, bf16[512,2,16,64]{3,1,2,0:T(2,128)(2,1)} %copy.156, bf16[512,2,16,64]{3,1,2,0:T(2,128)(2,1)} %copy.142, bf16[512,2,16,64]{3,1,2,0:T(2,128)(2,1)} %copy.141), kind=kOutput, calls=%fused_computation.21 | convolution fusion | flops 16891904 | bytes 6881280 | tf_op jit(solution)/shard_map/fphe,fqhe->fhpq/dot_general | solution.py:199
  1024.8 22.2 %multiply_convert_fusion.2 = bf16[512,16,2,4]{3,2,1,0:T(2,128)(2,1)S(1)} fusion(f32[512,16,2,4]{3,2,1,0:T(2,128)} %get-tuple-element.158, f32[512,16,2]{2,1,0:T(8,128)} %get-tuple-element.157, f32[512,16,2,4]{3,2,1,0:T(2,128)} %get-tuple-element.153, f32[512,16,2]{2,1,0:T(8,128)} %get-tuple-element.152), kind=kLoop, calls=%fused_computation.20 | loop fusion | flops 262144 | bytes 786432 | tf_op jit(solution)/shard_map/convert_element_type | solution.py:204
  1057.7 11.5 fusion.48
  1069.1 12.3 copy.164
  1092.4 17.5 fusion.13
  1127.2 12.3 copy.161
  1144.9 11.5 copy.168
  1156.4 12.3 copy.159
  1183.7 11.8 convolution_convert_fusion.2
  1196.2 22.6 %convolution_convert_fusion = bf16[2,1024,5632]{2,1,0:T(8,128)(2,1)} fusion(bf16[512,2,2816]{2,0,1:T(8,128)(2,1)} %get-tuple-element.139, bf16[512,2,2816]{2,0,1:T(8,128)(2,1)} %get-tuple-element.138, f32[512,2,1024]{2,0,1:T(8,128)} %get-tuple-element.155, f32[1024]{0:T(1024)S(1)} %bitcast.113, f32[512,2]{0,1:T(2,128)S(1)} %copy-done.26), kind=kOutput, calls=%fused_computation.2 | convolution fusion | flops 11848908800 | bytes 38805504 | tf_op jit(solution)/shard_map/fpd,fpe->pde/dot_general | solution.py:168
  1219.5 15.7 fusion.20
  1236.2 184.1 %reduce-scatter.8.cloned.1.call-done = bf16[2,128,3072]{2,1,0:T(8,128)(2,1)} async-done(((bf16[2,1024,3072]{2,1,0:T(8,128)(2,1)}), bf16[2,128,3072]{2,1,0:T(8,128)(2,1)}) %reduce-scatter.8.cloned.1.call-update) | async-done | bytes 1572880 | tf_op jit(solution)/shard_map/reduce_scatter | solution.py:250
  1420.3 377.0 %reduce-scatter.12.cloned.1.call-done = bf16[2,128,5632]{2,1,0:T(8,128)(2,1)} async-done(((bf16[2,1024,5632]{2,1,0:T(8,128)(2,1)}), bf16[2,128,5632]{2,1,0:T(8,128)(2,1)}) %reduce-scatter.12.cloned.1.call-update) | async-done | bytes 2883600 | tf_op jit(solution)/shard_map/reduce_scatter | solution.py:175
  1797.4 11.9 fusion.23
  1817.6 44.4 %reduce-scatter.16.cloned.1.call-done = bf16[128,2]{1,0:T(8,128)(2,1)} async-done(((bf16[1024,2]{1,0:T(8,128)(2,1)}), bf16[128,2]{1,0:T(8,128)(2,1)}) %reduce-scatter.16.cloned.1.call-update) | async-done | bytes 528
  1869.3 116.7 %all-reduce.3.cloned.1.call-done = (bf16[2,128,3072]{2,1,0:T(8,128)(2,1)}, bf16[2,128,1024]{2,1,0:T(8,128)(2,1)}, bf16[2,128,5632]{2,1,0:T(8,128)(2,1)}, bf16[2,352,1024]{2,1,0:T(8,128)(2,1)}) async-done(((bf16[2,128,3072]{2,1,0:T(8,128)(2,1)}, bf16[2,128,1024]{2,1,0:T(8,128)(2,1)}, bf16[2,128,5632]{2,1,0:T(8,128)(2,1)}, bf16[2,352,1024]{2,1,0:T(8,128)(2,1)}), (bf16[2,128,3072]{2,1,0:T(8,128)(2,1)}, ...) | async-done | bytes 6422544 | tf_op jit(solution)/shard_map/psum | solution.py:259
  2009.2 11.6 add_multiply_fusion
  (165 shorter events, 258.8 us)
Async XLA Ops:
  7.2 182.7 %all-gather.5.cloned.1.call-start = ((), (), s32[]{:S(2)}) async-start(), calls=%async_computation.5 | async-start | bytes 14155776 | tf_op jit(solution)/shard_map/all_gather | solution.py:96
  10.6 348.9 %all-gather.7.cloned.1.call-start = ((), (), s32[]{:S(2)}) async-start(), calls=%async_computation.6 | async-start | bytes 4718592 | tf_op jit(solution)/shard_map/all_gather | solution.py:97
  11.6 694.4 %all-gather.9.cloned.1.call-start = ((), (), s32[]{:S(2)}) async-start(), calls=%async_computation.7 | async-start | bytes 25952256 | tf_op jit(solution)/shard_map/all_gather | solution.py:142
  16.1 26.6 %copy-start.2 = (bf16[512,2,1024]{2,1,0:T(2,128)(2,1)S(1)}, bf16[512,2,1024]{2,1,0:T(2,128)(2,1)}, u32[]{:S(2)}) copy-start(bf16[512,2,1024]{2,1,0:T(2,128)(2,1)} %param.18) | copy-start | bytes 6291460
  16.1 856.1 %all-gather.11.cloned.1.call-start = ((), (), s32[]{:S(2)}) async-start(), calls=%async_computation.8 | async-start | bytes 12976128 | tf_op jit(solution)/shard_map/all_gather | solution.py:143
  19.5 1216.7 %reduce-scatter.10.cloned.1.call-start = ((), (), s32[]{:S(2)}) async-start(), calls=%async_computation.10 | async-start | bytes 4718592 | tf_op jit(solution)/shard_map/reduce_scatter | solution.py:253
  43.3 158.4 %copy-start.20 = (f32[512,2]{0,1:T(2,128)}, f32[512,2]{0,1:T(2,128)S(1)}, u32[]{:S(2)}) copy-start(f32[512,2]{0,1:T(2,128)S(1)} %add_rsqrt_fusion.1) | copy-start | bytes 12292
  43.4 158.4 %copy-start.22 = (f32[1,1024]{1,0:T(1,128)}, f32[1,1024]{1,0:T(1,128)S(1)}, u32[]{:S(2)}) copy-start(f32[1,1024]{1,0:T(1,128)S(1)} %get-tuple-element.151) | copy-start | bytes 12292
  43.4 873.4 %copy-start.27 = (f32[1,1024]{1,0:T(1,128)}, f32[1,1024]{1,0:T(1,128)S(1)}, u32[]{:S(2)}) copy-start(f32[1,1024]{1,0:T(1,128)S(1)} %get-tuple-element.150) | copy-start | bytes 12292
  201.8 52.8 %collective-permute-start = (bf16[2,2048]{1,0:T(2,128)(2,1)S(1)}, bf16[2,2048]{1,0:T(2,128)(2,1)S(1)}, u32[]{:S(2)}, u32[]{:S(2)}) collective-permute-start(bf16[2,2048]{1,0:T(2,128)(2,1)S(1)} %bitcast.114), channel_id=1, source_target_pairs={{0,1},{1,2},{2,3},{3,4},{4,5},{5,6},{6,7},{7,8},{8,9},{9,10},{10,1... | collective-permute-start | bytes 24584 | tf_op jit(solution)/shard_map/ppermute | solution.py:20
  319.4 15.5 copy-start.14
  319.4 15.5 copy-start.15
  367.4 549.4 %copy-start.25 = (f32[512,2]{0,1:T(2,128)}, f32[512,2]{0,1:T(2,128)S(1)}, u32[]{:S(2)}) copy-start(f32[512,2]{0,1:T(2,128)S(1)} %add_rsqrt_fusion) | copy-start | bytes 12292
  706.0 166.3 %copy-start.19 = (bf16[512,2,1024]{2,1,0:T(2,128)(2,1)S(1)}, bf16[512,2,1024]{2,1,0:T(2,128)(2,1)}, u32[]{:S(2)}) copy-start(bf16[512,2,1024]{2,1,0:T(2,128)(2,1)} %param.19) | copy-start | bytes 6291460
  927.3 308.9 %reduce-scatter.14.cloned.1.call-start = ((), (), s32[]{:S(2)}) async-start(), calls=%async_computation.12 | async-start | bytes 12976128 | tf_op jit(solution)/shard_map/reduce_scatter | solution.py:178
  939.1 481.2 %reduce-scatter.8.cloned.1.call-start = ((), (), s32[]{:S(2)}) async-start(), calls=%async_computation.9 | async-start | bytes 14155776 | tf_op jit(solution)/shard_map/reduce_scatter | solution.py:250
  1024.8 22.2 %copy-start.13 = (bf16[512,2,16,64]{3,1,2,0:T(2,128)(2,1)S(1)}, bf16[512,2,16,64]{3,1,2,0:T(2,128)(2,1)}, u32[]{:S(2)}) copy-start(bf16[512,2,16,64]{3,1,2,0:T(2,128)(2,1)} %copy.149) | copy-start | bytes 6291460
  1047.0 10.6 copy-start.9
  1089.7 20.1 copy-start
  1089.7 20.1 copy-start.1
  1089.7 84.5 %collective-permute-start.1 = (f32[2,2048]{1,0:T(2,128)S(1)}, f32[2,2048]{1,0:T(2,128)S(1)}, u32[]{:S(2)}, u32[]{:S(2)}) collective-permute-start(f32[2,2048]{1,0:T(2,128)S(1)} %fusion.38), channel_id=1, source_target_pairs={{1,0},{2,1},{3,2},{4,3},{5,4},{6,5},{7,6},{8,7},{9,8},{10,9},{11,1... | collective-permute-start | bytes 49160 | tf_op jit(solution)/shard_map/ppermute | solution.py:20
  1195.5 601.8 %reduce-scatter.12.cloned.1.call-start = ((), (), s32[]{:S(2)}) async-start(), calls=%async_computation.11 | async-start | bytes 25952256 | tf_op jit(solution)/shard_map/reduce_scatter | solution.py:175
  1218.8 643.2 %reduce-scatter.16.cloned.1.call-start = ((), (), s32[]{:S(2)}) async-start(), calls=%async_computation.13 | async-start | bytes 294912
  1236.1 749.9 %all-reduce.3.cloned.1.call-start = ((), (), s32[]{:S(2)}) async-start(), calls=%async_computation.14 | async-start | bytes 12845056 | tf_op jit(solution)/shard_map/psum | solution.py:259
  1797.4 15.4 copy-start.8
  1814.1 54.6 %copy-start.31 = (f32[2,128]{1,0:T(2,128)S(1)}, f32[2,128]{1,0:T(2,128)}, u32[]{:S(2)}) copy-start(f32[2,128]{1,0:T(2,128)} %param.25) | copy-start | bytes 3076
  1814.1 54.6 %copy-start.32 = (f32[2,128]{1,0:T(2,128)S(1)}, f32[2,128]{1,0:T(2,128)}, u32[]{:S(2)}) copy-start(f32[2,128]{1,0:T(2,128)} %param.35) | copy-start | bytes 3076
  1814.1 54.6 %copy-start.33 = (f32[2,128]{1,0:T(2,128)S(1)}, f32[2,128]{1,0:T(2,128)}, u32[]{:S(2)}) copy-start(f32[2,128]{1,0:T(2,128)} %param.30) | copy-start | bytes 3076
  1817.6 172.9 %copy-start.6 = (f32[2,128,3072]{2,1,0:T(8,128)S(1)}, f32[2,128,3072]{2,1,0:T(8,128)}, u32[]{:S(2)}) copy-start(f32[2,128,3072]{2,1,0:T(8,128)} %param.21) | copy-start | bytes 9437188
  1986.0 23.2 %slice-start = ((s8[5767168]{0:T(1024)(128)(4,1)}), s8[4194304]{0:T(1024)(128)(4,1)S(1)}, s32[]{:S(2)}) async-start(s8[5767168]{0:T(1024)(128)(4,1)} %bitcast.89), calls=%async_computation.15 | async-start | bytes 8388608
  1990.5 18.7 slice-start.1
  1999.7 9.5 copy-start.17
  (16 other events, 63.8 us)
Sparse Core Ops, SparseCore 0:
  10.8 179.0 all-gather.4
  192.7 71.7 all-gather.6
  266.5 439.3 all-gather.8
  708.6 163.6 all-gather.10
  927.5 86.0 reduce-scatter.9
  1017.5 192.4 reduce-scatter.13
  1214.0 206.3 reduce-scatter.7
  1424.7 372.6 reduce-scatter.11
  1801.6 60.3 reduce-scatter.15
  1864.7 121.2 all-reduce.2
where the time goes:
time: 2040 us; the launch traced here: 2030 us
  waiting for transfers between devices  1350 us (66%)
  matrix products  281 us (14%)
  local copies, waits for them, and re-layouts  241 us (12%)
  other arithmetic  106 us (5%)
  blocking collectives  28.2 us (1%)
    reduce_scatter x1, waiting for transfers between devices, per_device(): lax.psum_scatter(inner_term.astype(jnp.bfloat16), 'fsdp', scatter_dimensi...  377 us
    all_gather x1, waiting for transfers between devices, per_device(): lax.all_gather(inner_local[0], 'fsdp', axis=1, tiled=True)  339 us
    reduce_scatter x1, waiting for transfers between devices, per_device(): lax.psum_scatter(qkv_term.astype(jnp.bfloat16), 'fsdp', scatter_dimension...  184 us
    all_gather x1, waiting for transfers between devices, per_device(): lax.all_gather(attn_local[1], 'fsdp', axis=1, tiled=True)  147 us
    all_gather x1, waiting for transfers between devices, per_device(): lax.all_gather(inner_local[1], 'fsdp', axis=1, tiled=True)  144 us
    psum x1, waiting for transfers between devices, per_device(): lax.psum(qkv_share.astype(jnp.bfloat16), 'dp').astype(jnp.float32)  117 us
    unnamed x11, waiting for transfers between devices  44.6 us
  transfers between devices with their start and end apart: 12, of which 7 were waited for; matrix products, arithmetic and copies ran while one was open for 26% of the time, Pallas kernels for 0%

commit v1 on v0

v1 whole, which is shorter than its diff:
```python
import functools
import math

import jax
import jax.numpy as jnp
from jax import lax
from jax.experimental import pallas as pl
from jax.experimental.pallas import tpu as pltpu
from jax.sharding import PartitionSpec as P

HEADS = 16
Z = 4
MESH = pl.DeviceIdType.MESH
ANY = pl.BlockSpec(memory_space=pl.ANY)
BF = jnp.bfloat16
F32 = jnp.float32

norm_eps = 1e-05
momentum_rate = 0.5
average_rate = 0.5
step_rate = 0.05
VMEM_BYTES = 60 * 1024 * 1024


def nn(a, b):
    return lax.dot_general(a, b, (((1,), (0,)), ((), ())), preferred_element_type=F32)


def nt(a, b):
    return lax.dot_general(a, b, (((1,), (1,)), ((), ())), preferred_element_type=F32)


def tn(a, b):
    return lax.dot_general(a, b, (((0,), (0,)), ((), ())), preferred_element_type=F32)


def scale_rows(values):
    return lax.rsqrt(jnp.mean(values * values, axis=-1, keepdims=True) + norm_eps)


def norm_back(grad_in, normed, gain_row, inverse):
    scaled = grad_in * gain_row
    return inverse * (scaled - normed * jnp.mean(scaled * normed, axis=-1, keepdims=True))


def owner_update(weight, gradient, moment, average, step_size):
    moment_new = momentum_rate * moment + gradient
    weight_new = weight - step_size * (gradient + momentum_rate * moment_new)
    average_new = average_rate * average + (1.0 - average_rate) * weight_new
    return (moment_new, average_new, weight_new)


def gather_kernel(
    inner_peers, attn_own, inner_own, down_own, gains_own, attn, inner, down, gains,
    local_sem, send_z, recv_z, send_x, recv_x, send_c, recv_c, send_y, recv_y, send_r, recv_r,
):
    X = inner_peers
    dp = lax.axis_index("dp")
    fs = lax.axis_index("fsdp")
    y, core = dp // 2, dp % 2
    z, x = fs // X, fs % X
    other_core = (y * 2 + 1 - core, fs)
    other_y = ((1 - y) * 2 + core, fs)

    def z_peer(k):
        return (dp, lax.rem(z + k, Z) * X + x)

    def x_peer(i):
        return (dp, z * X + lax.rem(x + i, X))

    owns = (attn_own, inner_own, down_own, gains_own)
    rows = [o.shape[-2] for o in owns]

    def place(array, source, part=None):
        if array == 0:
            return attn.at[dp if part is None else part, :, pl.ds(source * rows[0], rows[0]), :]
        if array == 1:
            return inner.at[core, pl.ds(source * rows[1], rows[1]), :]
        if array == 2:
            return down.at[core, pl.ds(source * rows[2], rows[2]), :]
        return gains.at[source]

    barrier = pltpu.get_barrier_semaphore()
    peers = [z_peer(k) for k in range(1, Z)] + [x_peer(i) for i in range(1, X)]
    peers += [other_core, other_y]
    for peer in peers:
        pl.semaphore_signal(barrier, inc=1, device_id=peer, device_id_type=MESH)
    pl.semaphore_wait(barrier, len(peers))

    started = []

    def remote(src, dst, ss, rs, peer):
        copy = pltpu.make_async_remote_copy(
            src_ref=src, dst_ref=dst, send_sem=ss, recv_sem=rs, device_id=peer, device_id_type=MESH
        )
        copy.start()
        started.append(copy)
        return copy

    local = []
    for n, own in enumerate(owns):
        copy = pltpu.make_async_copy(own, place(n, fs), local_sem.at[n])
        copy.start()
        local.append(copy)

    def chunk_source(k, i):
        return lax.rem(z - k + Z, Z) * X + lax.rem(x - i + X, X)

    def start_array(n):
        for k in range(1, Z):
            remote(owns[n], place(n, fs), send_z.at[n, k], recv_z.at[n, k], z_peer(k))
        for i in range(1, X):
            remote(owns[n], place(n, fs), send_x.at[n, 0, i], recv_x.at[n, 0, i], x_peer(i))

    def share(n, k, i):
        if n == 3:
            return
        source = chunk_source(k, i)
        src = owns[n] if (k == 0 and i == 0) else place(n, source)
        if n == 0:
            remote(src, place(0, source), send_y.at[k, i], recv_y.at[k, i], other_y)
        remote(src, place(n, source), send_c.at[n, k, i], recv_c.at[n, k, i], other_core)

    def wait_recv(dst, rs, ss):
        pltpu.make_async_remote_copy(
            src_ref=dst, dst_ref=dst, send_sem=ss, recv_sem=rs, device_id=other_core, device_id_type=MESH
        ).wait_recv()

    def pass_on(n):
        share(n, 0, 0)
        for i in range(1, X):
            wait_recv(place(n, chunk_source(0, i)), recv_x.at[n, 0, i], send_x.at[n, 0, i])
            share(n, 0, i)
        for k in range(1, Z):
            source = chunk_source(k, 0)
            wait_recv(place(n, source), recv_z.at[n, k], send_z.at[n, k])
            for i in range(1, X):
                remote(place(n, source), place(n, source), send_x.at[n, k, i], recv_x.at[n, k, i], x_peer(i))
            share(n, k, 0)
        for k in range(1, Z):
            for i in range(1, X):
                wait_recv(place(n, chunk_source(k, i)), recv_x.at[n, k, i], send_x.at[n, k, i])
                share(n, k, i)

    start_array(3)
    start_array(0)
    start_array(1)
    start_array(2)
    pass_on(0)
    pass_on(3)
    pass_on(1)
    pass_on(2)
    part = (1 - y) * 2 + core
    for k in range(Z):
        for i in range(X):
            source = chunk_source(k, i)
            wait_recv(place(0, source, part), recv_y.at[k, i], send_y.at[k, i])
            remote(place(0, source, part), place(0, source, part), send_r.at[k, i], recv_r.at[k, i], other_core)
    for k in range(Z):
        for i in range(X):
            source = chunk_source(k, i)
            wait_recv(place(0, source, (1 - y) * 2 + 1 - core), recv_r.at[k, i], send_r.at[k, i])
            for n in range(3):
                half = y * 2 + 1 - core if n == 0 else None
                dst = place(0, source, half) if n == 0 else (
                    inner.at[1 - core, pl.ds(source * rows[1], rows[1]), :] if n == 1
                    else down.at[1 - core, pl.ds(source * rows[2], rows[2]), :]
                )
                wait_recv(dst, recv_c.at[n, k, i], send_c.at[n, k, i])
    for copy in started:
        copy.wait_send()
    for copy in local:
        copy.wait()


def gather_weights(attn_own, inner_own, down_own, gains_own, fsdp_count):
    X = fsdp_count // Z
    _, rows, width = attn_own.shape
    dma = pltpu.SemaphoreType.DMA
    return pl.pallas_call(
        functools.partial(gather_kernel, X),
        out_shape=(
            jax.ShapeDtypeStruct((4, 2, rows * fsdp_count, width), BF),
            jax.ShapeDtypeStruct((2, inner_own.shape[0] * fsdp_count, inner_own.shape[1]), BF),
            jax.ShapeDtypeStruct((2, down_own.shape[0] * fsdp_count, down_own.shape[1]), BF),
            jax.ShapeDtypeStruct((fsdp_count,) + gains_own.shape, F32),
        ),
        in_specs=[ANY] * 4,
        out_specs=(ANY,) * 4,
        scratch_shapes=[
            dma((4,)), dma((4, Z)), dma((4, Z)), dma((4, Z, X)), dma((4, Z, X)),
            dma((3, Z, X)), dma((3, Z, X)), dma((Z, X)), dma((Z, X)), dma((Z, X)), dma((Z, X)),
        ],
        compiler_params=pltpu.CompilerParams(collective_id=0, has_side_effects=True),
        name="gather_weights",
    )(attn_own, inner_own, down_own, gains_own)


def head_ones(lanes, head_size):
    row = lax.broadcasted_iota(jnp.int32, (lanes, lanes), 0) // head_size
    column = lax.broadcasted_iota(jnp.int32, (lanes, lanes), 1) // head_size
    return (row == column).astype(BF)


KEYS = ((0, 1, 2), (0, 1, 2, 3))


def load_heads(q, k, v, edge):
    frames = q.shape[1]
    first = lax.broadcasted_iota(jnp.int32, (frames, q.shape[2]), 0) == 0
    queries = [q[p].astype(F32) for p in range(2)]
    here_k = [k[p].astype(F32) for p in range(2)]
    here_v = [v[p].astype(F32) for p in range(2)]
    before_k = [jnp.where(first, edge[p : p + 1, :], pltpu.roll(here_k[p], 1, 0)) for p in range(2)]
    before_v = [jnp.where(first, edge[2 + p : 3 + p, :], pltpu.roll(here_v[p], 1, 0)) for p in range(2)]
    return queries, before_k + here_k, before_v + here_v


def head_probs(queries, keys, p, allowed, ones, root_size):
    scores = []
    for n in KEYS[p]:
        s = nn((queries[p] * keys[n]).astype(BF), ones) * (1.0 / root_size)
        scores.append(jnp.where(allowed, s, -1e30) if n < 2 else s)
    top = functools.reduce(jnp.maximum, scores)
    exps = [jnp.exp(s - top) for s in scores]
    exps = [jnp.where(allowed, e, 0.0) if n < 2 else e for n, e in zip(KEYS[p], exps)]
    inverse = 1.0 / functools.reduce(jnp.add, exps)
    return [e * inverse for e in exps]


def attend_kernel(head_size, carried, q, k, v, edge, out):
    ones = head_ones(q.shape[2], head_size)
    allowed = jnp.broadcast_to(carried[...], q.shape[1:]) > 0.5
    queries, keys, values = load_heads(q, k, v, edge)
    for p in range(2):
        probs = head_probs(queries, keys, p, allowed, ones, math.sqrt(head_size))
        mixed = [pr.astype(BF).astype(F32) * values[n] for n, pr in zip(KEYS[p], probs)]
        out[p] = functools.reduce(jnp.add, mixed).astype(BF)


def attend_back_kernel(head_size, carried, q, k, v, edge, mixed_grad, dq, dk, dv, edge_out):
    frames = q.shape[1]
    ones = head_ones(q.shape[2], head_size)
    allowed = jnp.broadcast_to(carried[...], q.shape[1:]) > 0.5
    queries, keys, values = load_heads(q, k, v, edge)
    scale = 1.0 / math.sqrt(head_size)
    key_grads = [0.0] * 4
    value_grads = [0.0] * 4
    for p in range(2):
        probs = head_probs(queries, keys, p, allowed, ones, math.sqrt(head_size))
        grad = mixed_grad[p].astype(F32)
        dprobs = [nn((grad * values[n]).astype(BF), ones) for n in KEYS[p]]
        mean = functools.reduce(jnp.add, [a * b for a, b in zip(probs, dprobs)])
        query_grad = 0.0
        for n, pr, dp in zip(KEYS[p], probs, dprobs):
            ds = (pr * (dp - mean)).astype(BF).astype(F32)
            query_grad = query_grad + ds * keys[n]
            key_grads[n] = key_grads[n] + ds * queries[p]
            value_grads[n] = value_grads[n] + pr.astype(BF).astype(F32) * grad
        dq[p] = (query_grad * scale).astype(BF)
    last = lax.broadcasted_iota(jnp.int32, q.shape[1:], 0) == frames - 1
    for kind, (grads, out, factor) in enumerate(((key_grads, dk, scale), (value_grads, dv, 1.0))):
        for p in range(2):
            before = grads[p] * factor
            total = grads[2 + p] * factor + jnp.where(last, 0.0, pltpu.roll(before, frames - 1, 0))
            out[p] = total.astype(BF)
            row = 2 * kind + p
            edge_out[row : row + 1, :] = before[0:1, :]
            edge_out[4 + row : 5 + row, :] = total[frames - 1 : frames, :]


def attention_specs(frames, width, lanes):
    rows = pl.BlockSpec((2, frames, lanes), lambda j: (0, 0, j))
    edge = pl.BlockSpec((8, lanes), lambda j: (0, j))
    mask = pl.BlockSpec((frames, 1), lambda j: (0, 0))
    return rows, edge, mask


def attend(carried, q, k, v, edge, head_size):
    _, frames, width = q.shape
    lanes = 256
    rows, edge_spec, mask = attention_specs(frames, width, lanes)
    return pl.pallas_call(
        functools.partial(attend_kernel, head_size),
        grid=(width // lanes,),
        out_shape=jax.ShapeDtypeStruct(q.shape, BF),
        in_specs=[mask, rows, rows, rows, edge_spec],
        out_specs=rows,
        compiler_params=pltpu.CompilerParams(vmem_limit_bytes=VMEM_BYTES),
        name="attend",
    )(carried, q, k, v, edge)


def attend_back(carried, q, k, v, edge, mixed_grad, head_size):
    _, frames, width = q.shape
    lanes = 256
    rows, edge_spec, mask = attention_specs(frames, width, lanes)
    return pl.pallas_call(
        functools.partial(attend_back_kernel, head_size),
        grid=(width // lanes,),
        out_shape=(jax.ShapeDtypeStruct(q.shape, BF),) * 3 + (jax.ShapeDtypeStruct((8, width), F32),),
        in_specs=[mask, rows, rows, rows, edge_spec, rows],
        out_specs=(rows, rows, rows, edge_spec),
        compiler_params=pltpu.CompilerParams(vmem_limit_bytes=VMEM_BYTES),
        name="attend_back",
    )(carried, q, k, v, edge, mixed_grad)


def feed_forward_kernel(b, c, inner, down, out, back, inner_grad, down_grad):
    half = down.shape[2]

    @pl.when(pl.program_id(0) == 0)
    def _():
        out[...] = jnp.zeros_like(out)
        back[...] = jnp.zeros_like(back)

    rows, cot = b[...], c[...]
    gate = nn(rows, inner[0])
    up = nn(rows, inner[1])
    squashed = jax.nn.sigmoid(gate)
    active = gate * squashed
    hidden = (active * up).astype(BF)
    hidden_grad = nt(cot[:, :half], down[0]) + nt(cot[:, half:], down[1])
    gate_grad = (hidden_grad * up * (squashed * (1.0 + gate * (1.0 - squashed)))).astype(BF)
    up_grad = (hidden_grad * active).astype(BF)
    for n in range(2):
        part = slice(n * half, (n + 1) * half)
        down_grad[n] = tn(hidden, cot[:, part]).astype(BF)
        out[:, part] += nn(hidden, down[n])
    inner_grad[0] = tn(rows, gate_grad).astype(BF)
    inner_grad[1] = tn(rows, up_grad).astype(BF)
    back[...] += nt(gate_grad, inner[0]) + nt(up_grad, inner[1])


def feed_forward(b, c, inner, down):
    rows, width = b.shape
    _, _, hidden = inner.shape
    step = 256
    whole = pl.BlockSpec((rows, width), lambda j: (0, 0))
    inner_spec = pl.BlockSpec((2, width, step), lambda j: (0, 0, j))
    down_spec = pl.BlockSpec((2, step, down.shape[2]), lambda j: (0, j, 0))
    return pl.pallas_call(
        feed_forward_kernel,
        grid=(hidden // step,),
        out_shape=(
            jax.ShapeDtypeStruct((rows, width), F32),
            jax.ShapeDtypeStruct((rows, width), F32),
            jax.ShapeDtypeStruct(inner.shape, BF),
            jax.ShapeDtypeStruct(down.shape, BF),
        ),
        in_specs=[whole, whole, inner_spec, down_spec],
        out_specs=(whole, whole, inner_spec, down_spec),
        compiler_params=pltpu.CompilerParams(vmem_limit_bytes=VMEM_BYTES),
        cost_estimate=pl.CostEstimate(flops=18 * rows * width * hidden, bytes_accessed=60 * 2**20, transcendentals=0),
        name="feed_forward",
    )(b, c, inner, down)


def per_device(
    frames, cotangent, segment_ids,
    qkv_weight, mix_weight, inner_weight, down_weight, norm_gains,
    qkv_moment, mix_moment, inner_moment, down_moment, gains_moment,
    qkv_average, mix_average, inner_average, down_average, gains_average,
):
    frame_count, positions, width = frames.shape
    head_size = width // HEADS
    hidden = inner_weight.shape[2] // 2
    dp_count, fsdp_count = lax.axis_size("dp"), lax.axis_size("fsdp")
    X = fsdp_count // Z
    devices = dp_count * fsdp_count
    total_frames = frame_count * devices
    dp, fs = lax.axis_index("dp"), lax.axis_index("fsdp")
    y, core = dp // 2, dp % 2
    z, x = fs // X, fs % X
    axes = ("dp", "fsdp")

    def permute(value, target):
        pairs = []
        for d in range(dp_count):
            for f in range(fsdp_count):
                to = target(d, f)
                if to is not None:
                    pairs.append((d * fsdp_count + f, to[0] * fsdp_count + to[1]))
        return lax.ppermute(value, axes, pairs)

    def to_core(value):
        return permute(value, lambda d, f: (d ^ 1, f))

    def to_y(value):
        return permute(value, lambda d, f: (d ^ 2, f))

    def to_x(value, i):
        return permute(value, lambda d, f: (d, (f // X) * X + (f % X + i) % X))

    def to_z(value, k):
        return permute(value, lambda d, f: (d, ((f // X + k) % Z) * X + f % X))

    def shifted(value, steps):
        def target(d, f):
            to = d * fsdp_count + f + steps
            return divmod(to, fsdp_count) if 0 <= to < devices else None

        return permute(value, target)

    device = dp * fsdp_count + fs
    padded_ids = jnp.concatenate([jnp.full((1,), -1, jnp.int32), segment_ids])
    window = lax.dynamic_slice_in_dim(padded_ids, device * frame_count, frame_count + 1)
    carried = (window[1:] == window[:-1]).astype(F32)[:, None]

    attn_own = lax.select_n(
        dp, qkv_weight[:, :, :width], qkv_weight[:, :, width : 2 * width], qkv_weight[:, :, 2 * width :], mix_weight
    ).astype(BF)
    inner_own = lax.dynamic_slice(
        inner_weight, (y, 0, core * hidden), (1, inner_weight.shape[1], hidden)
    )[0].astype(BF)
    half_width = width // 2
    down_own = lax.dynamic_slice(
        down_weight, (y, 0, core * half_width), (1, down_weight.shape[1], half_width)
    )[0].astype(BF)
    own_gains = norm_gains.astype(BF).astype(F32)
    gains_own = jnp.zeros((8, 128), F32).at[: own_gains.shape[0], : own_gains.shape[1]].set(own_gains)
    attn, inner, down, gains_all = gather_weights(attn_own, inner_own, down_own, gains_own, fsdp_count)
    gains = gains_all[:, :2, : own_gains.shape[1]].transpose(1, 0, 2).reshape(2, width)

    xf = frames.transpose(1, 0, 2).astype(F32)
    cot = cotangent.transpose(1, 0, 2)
    cot_there = to_y(lax.dynamic_index_in_dim(cot, 1 - y, 0, keepdims=False))
    r1 = scale_rows(xf)
    n1 = xf * r1
    a = (n1 * gains[0]).astype(BF)

    def each(left, right):
        return jnp.einsum("pfd,pde->pfe", left, right, preferred_element_type=F32)

    q, k, v = (each(a, attn[t]).astype(BF) for t in range(3))
    edge_rows = shifted(jnp.concatenate([k[:, -1], v[:, -1]], axis=0), 1)
    edge = jnp.pad(edge_rows.astype(F32), ((0, 4), (0, 0)))
    mixed = attend(carried, q, k, v, edge, head_size)
    hres = xf + each(mixed, attn[3])
    r2 = scale_rows(hres)
    n2 = hres * r2
    b = (n2 * gains[1]).astype(BF)

    b_there = to_y(lax.dynamic_index_in_dim(b, 1 - y, 0, keepdims=False))
    b_rows = jnp.concatenate([lax.dynamic_index_in_dim(b, y, 0, keepdims=False), b_there], axis=0)
    c_rows = jnp.concatenate([lax.dynamic_index_in_dim(cot, y, 0, keepdims=False), cot_there], axis=0)
    out, back, inner_part, down_part = feed_forward(b_rows, c_rows, inner, down)
    both = to_y(jnp.stack([out[frame_count:], back[frame_count:]]).astype(BF)).astype(F32)

    def by_position(mine, theirs):
        return jnp.where(y == 0, jnp.stack([mine, theirs]), jnp.stack([theirs, mine]))

    layer_out = (hres + by_position(out[:frame_count], both[0])).astype(BF).transpose(1, 0, 2)
    db = by_position(back[:frame_count], both[1])

    e2 = jnp.sum(db * n2, axis=(0, 1))
    dh = cot.astype(F32) + norm_back(db, n2, gains[1], r2)
    dhb = dh.astype(BF)

    def back_each(left, right):
        return jnp.einsum("pfe,pde->pfd", left, right, preferred_element_type=F32)

    def grad_each(left, right):
        return jnp.einsum("pfd,pfe->pde", left, right, preferred_element_type=F32).astype(BF)

    mixed_grad = back_each(dhb, attn[3]).astype(BF)
    dq, dk, dv, edges = attend_back(carried, q, k, v, edge, mixed_grad, head_size)
    edge_back = shifted(edges[:4], -1)
    last = (edges[4:] + edge_back).astype(BF)
    dk = lax.dynamic_update_slice(dk, last[:2, None], (0, frame_count - 1, 0))
    dv = lax.dynamic_update_slice(dv, last[2:, None], (0, frame_count - 1, 0))
    attn_part = [grad_each(a, dq), grad_each(a, dk), grad_each(a, dv), grad_each(mixed, dhb)]
    da = back_each(dq, attn[0]) + back_each(dk, attn[1]) + back_each(dv, attn[2])
    e1 = jnp.sum(da * n1, axis=(0, 1))
    frames_grad = (dh + norm_back(da, n1, gains[0], r1)).astype(BF).transpose(1, 0, 2)

    def add(left, right):
        return (left.astype(F32) + right.astype(F32)).astype(BF)

    def at(value, index):
        return lax.dynamic_index_in_dim(value, index, 0, keepdims=False)

    def over_fsdp(value):
        grid = value.reshape((Z, X) + value.shape[1:])
        column = lax.dynamic_index_in_dim(grid, x, 1, keepdims=False)
        for i in range(1, X):
            column = add(column, to_x(lax.dynamic_index_in_dim(grid, lax.rem(x + i, X), 1, keepdims=False), i))
        total = at(column, z).astype(F32)
        for k in range(1, Z):
            total = total + to_z(at(column, lax.rem(z + k, Z)), k).astype(F32)
        return total

    def over_fsdp_rows(value):
        return over_fsdp(value.reshape((fsdp_count, value.shape[0] // fsdp_count) + value.shape[1:]))

    down_half = add(at(down_part, core), to_core(at(down_part, 1 - core)))
    inner_half = add(at(inner_part, core), to_core(at(inner_part, 1 - core)))
    down_mine = over_fsdp_rows(down_half).astype(BF)
    inner_mine = over_fsdp_rows(inner_half).astype(BF)

    parts = jnp.stack(attn_part).reshape(2, 2, 2 * width, width)
    pair = add(
        lax.dynamic_index_in_dim(parts, core, 1, keepdims=False),
        to_core(lax.dynamic_index_in_dim(parts, 1 - core, 1, keepdims=False)),
    )
    quarter = add(at(pair, y), to_y(at(pair, 1 - y)))
    quarter = quarter.reshape(2, fsdp_count, width // fsdp_count, width)
    attn_mine = jnp.stack(
        [over_fsdp(quarter[p]) for p in range(2)]
    ).astype(BF)

    def share_y(value):
        theirs = to_y(value)
        mine = jnp.where(y == 0, jnp.stack([value, theirs]), jnp.stack([theirs, value]))
        return mine

    def share_all(value):
        pair_y = share_y(value)
        others = to_core(pair_y)
        return jnp.where(core == 0, jnp.stack([pair_y, others], 1), jnp.stack([others, pair_y], 1))

    down_all = share_all(down_mine).astype(F32)
    inner_all = share_all(inner_mine).astype(F32)
    attn_all = share_all(attn_mine).astype(F32)
    down_grad = jnp.concatenate([down_all[:, 0], down_all[:, 1]], axis=-1)
    inner_grad = jnp.concatenate([inner_all[:, 0], inner_all[:, 1]], axis=-1)
    qkv_grad = jnp.concatenate([attn_all[0, 0], attn_all[0, 1], attn_all[1, 0]], axis=-1)
    mix_grad = attn_all[1, 1]

    gains_part = jnp.stack([e1, e2])
    gains_part = gains_part + to_core(gains_part)
    gains_part = gains_part + to_y(gains_part)
    gains_grid = gains_part.reshape(2, Z, X, -1).transpose(1, 2, 0, 3)
    column = lax.dynamic_index_in_dim(gains_grid, x, 1, keepdims=False)
    for i in range(1, X):
        column = column + to_x(lax.dynamic_index_in_dim(gains_grid, lax.rem(x + i, X), 1, keepdims=False), i)
    gains_grad = at(column, z)
    for kk in range(1, Z):
        gains_grad = gains_grad + to_z(at(column, lax.rem(z + kk, Z)), kk)

    step_size = step_rate / math.sqrt(total_frames)
    grads = (qkv_grad, mix_grad, inner_grad, down_grad, gains_grad)
    new = [
        owner_update(w, g, m, av, step_size)
        for w, g, m, av in zip(
            (qkv_weight, mix_weight, inner_weight, down_weight, norm_gains),
            grads,
            (qkv_moment, mix_moment, inner_moment, down_moment, gains_moment),
            (qkv_average, mix_average, inner_average, down_average, gains_average),
        )
    ]
    return (
        (layer_out, frames_grad) + grads
        + tuple(n[0] for n in new) + tuple(n[1] for n in new) + tuple(n[2] for n in new)
    )


def solution(mesh):
    rows = P(("dp", "fsdp"), None, None)
    weight = P(None, "fsdp", None)
    gains = P(None, "fsdp")
    weights = (weight,) * 4 + (gains,)
    return jax.shard_map(
        per_device,
        mesh=mesh,
        in_specs=(rows, rows, P()) + weights * 3,
        out_specs=(rows, rows) + weights * 4,
        check_vma=False,
    )
```

time: 2040 us -> 821 us (0.40)
  waiting for transfers between devices: 1350 us -> 237 us
  Pallas kernels: 0 us -> 280 us
  matrix products: 281 us -> 72.6 us
  local copies, waits for them, and re-layouts: 241 us -> 73.8 us
  starting transfers between devices: 4.72 us -> 56.3 us
  blocking collectives: 28.2 us -> 0 us
    all_gather x4 -> x0, waiting for transfers between devices: 629 us -> none  [the longest x1 339 us: per_device(): lax.all_gather(inner_local[0], 'fsdp', axis=1, tiled=True)]
    reduce_scatter x4 -> x0, waiting for transfers between devices: 561 us -> none  [the longest x1 377 us: per_device(): lax.psum_scatter(inner_term.astype(jnp.bfloat16), 'fsdp', scatter_dimensi...]
    pallas_call x0 -> x4, Pallas kernels: none -> 280 us  [the longest x1 179 us: gather_weights(): pl.pallas_call(functools.partial(gather_kernel, X), out_shape=(jax.ShapeD...]
    ppermute x2 -> x37, waiting for transfers between devices: 0.01 us -> 237 us  [permute(): return lax.ppermute(value, axes, pairs)]
    dot_general x17 -> x12, matrix products: 250 us -> 72.6 us  [the longest x4 30.3 us: back_each(): return jnp.einsum('pfe,pde->pfd', left, right, preferred_element_type=F32)]
    psum x1 -> x0, waiting for transfers between devices: 117 us -> none  [per_device(): lax.psum(qkv_share.astype(jnp.bfloat16), 'dp').astype(jnp.float32)]
    slice x16 -> x4, local copies, waits for them, and re-layouts: 109 us -> 3.2 us  [the longest x1 1.99 us: per_device(): db = by_position(back[:frame_count], both[1])]
    reshape x11 -> x1, local copies, waits for them, and re-layouts: 90.6 us -> 0.02 us  [per_device(): gains_grid = gains_part.reshape(2, Z, X, -1).transpose(1, 2, 0, 3)]
  transfers between devices with their start and end apart: 12 -> 37, of which waited for: 7 -> 16; matrix products, arithmetic and copies ran while one was open for 26% -> 23% of each run, Pallas kernels for 0% -> 4%
where the time goes in v1:
time: 821 us; the launch traced here: 816 us
  Pallas kernels  280 us (34%)
  waiting for transfers between devices  237 us (29%)
  other arithmetic  94.1 us (11%)
  local copies, waits for them, and re-layouts  73.8 us (9%)
  matrix products  72.6 us (9%)
  starting transfers between devices  56.3 us (7%)
    ppermute x37, waiting for transfers between devices, permute(): return lax.ppermute(value, axes, pairs)  237 us
    pallas_call x1, Pallas kernels, gather_weights(): pl.pallas_call(functools.partial(gather_kernel, X), out_shape=(jax.ShapeD...  179 us
    pallas_call x1, Pallas kernels, feed_forward(): pl.pallas_call(feed_forward_kernel, grid=(hidden // step,), out_shape=(ja...  71.3 us
    ppermute x37, starting transfers between devices, permute(): return lax.ppermute(value, axes, pairs)  56.3 us
    dot_general x4, matrix products, back_each(): return jnp.einsum('pfe,pde->pfd', left, right, preferred_element_type=F32)  30.3 us
    add x5, other arithmetic, owner_update(): average_new = average_rate * average + (1.0 - average_rate) * weight_new  29.5 us
    convert_element_type x8, other arithmetic, add(): return (left.astype(F32) + right.astype(F32)).astype(BF)  28.8 us
    unnamed x77, local copies, waits for them, and re-layouts  22.3 us
  transfers between devices with their start and end apart: 37, of which 16 were waited for; matrix products, arithmetic and copies ran while one was open for 23% of the time, Pallas kernels for 4%

profile of v1, /device:TPU:0, one launch (start us, length us, event | category | flops | bytes accessed | tf_op | source)
XLA Modules:
  0.0 815.5 jit_solution(15396441776990905964)
XLA Ops:
  9.3 179.0 %gather_weights.1 = (bf16[4,2,1024,1024]{3,2,1,0:T(8,128)(2,1)}, bf16[2,1024,2816]{2,1,0:T(8,128)(2,1)}, bf16[2,2816,512]{2,1,0:T(8,128)(2,1)}, f32[8,8,128]{2,1,0:T(8,128)}) custom-call(bf16[2,128,1024]{2,1,0:T(8,128)(2,1)} %select_convert_fusion.attn_own, bf16[128,2816]{1,0:T(8,128)(2,1)} %fusion.69.inner_own, bf16[352,512]{1,0:T(8,128)(2,1)} %fusion.80.down_own, ...), custom_call_target="tpu_custom_call" | custom-call | tf_op jit(solution)/shard_map/gather_weights/pallas_call | solution.py:180
  218.0 5.9 fusion.52.q
  229.4 10.8 %attend.1 = bf16[2,512,1024]{2,1,0:T(8,128)(2,1)} custom-call(f32[512,1]{1,0:T(8,128)} %copy.65.carried, bf16[2,512,1024]{2,1,0:T(8,128)(2,1)} %fusion.52.q, bf16[2,512,1024]{2,1,0:T(8,128)(2,1)} %copy.66.k, bf16[2,512,1024]{2,1,0:T(8,128)(2,1)} %copy.67.v, f32[8,1024]{1,0:T(8,128)} %pad_convert_fusion.edge), custom_call_target="tpu_custom_call" | custom-call | tf_op jit(solution)/shard_map/attend/pallas_call | solution.py:283
  240.3 5.6 multiply_reduce_fusion.2
  251.0 22.2 %collective-permute-done.1 = bf16[512,1024]{1,0:T(8,128)(2,1)S(1)} collective-permute-done((bf16[512,1024]{1,0:T(8,128)(2,1)S(1)}, bf16[512,1024]{1,0:T(8,128)(2,1)S(1)}, u32[]{:S(2)}, u32[]{:S(2)}) %collective-permute-start.1) | collective-permute-done | bytes 1048608 | tf_op jit(solution)/shard_map/ppermute | solution.py:384
  274.8 71.3 %feed_forward.1 = (f32[1024,1024]{1,0:T(8,128)}, f32[1024,1024]{1,0:T(8,128)}, bf16[2,1024,2816]{2,1,0:T(8,128)(2,1)}, bf16[2,2816,512]{2,1,0:T(8,128)(2,1)}) custom-call(bf16[1024,1024]{1,0:T(8,128)(2,1)} %pad_maximum_fusion.4.b, bf16[1024,1024]{1,0:T(8,128)(2,1)} %pad_maximum_fusion.5.c, bf16[2,1024,2816]{2,1,0:T(8,128)(2,1)} %get-tuple-element.48.inner, ...), custom_call_target="tpu_custom_call" | custom-call | flops 53150220288 | bytes 62914560 | tf_op jit(solution)/shard_map/feed_forward/pallas_call | solution.py:342
  351.5 5.7 dynamic-slice_bitcast_fusion.1
  359.6 38.5 %collective-permute-done.3 = bf16[2,512,1024]{2,1,0:T(8,128)(2,1)} collective-permute-done((bf16[2,512,1024]{2,1,0:T(8,128)(2,1)}, bf16[2,512,1024]{2,1,0:T(8,128)(2,1)}, u32[]{:S(2)}, u32[]{:S(2)}) %collective-permute-start.3) | collective-permute-done | bytes 2097184 | tf_op jit(solution)/shard_map/ppermute | solution.py:384
  404.5 7.4 fusion.55.mixed_grad
  416.3 18.8 %attend_back.1 = (bf16[2,512,1024]{2,1,0:T(8,128)(2,1)}, bf16[2,512,1024]{2,1,0:T(8,128)(2,1)}, bf16[2,512,1024]{2,1,0:T(8,128)(2,1)}, f32[8,1024]{1,0:T(8,128)}) custom-call(f32[512,1]{1,0:T(8,128)} %copy.65.carried, bf16[2,512,1024]{2,1,0:T(8,128)(2,1)} %fusion.52.q, bf16[2,512,1024]{2,1,0:T(8,128)(2,1)} %copy.66.k, bf16[2,512,1024]{2,1,0:T(8,128)(2,1)} %copy.67.v, ...), custom_call_target="tpu_custom_call" | custom-call | tf_op jit(solution)/shard_map/attend_back/pallas_call | solution.py:298
  437.4 6.4 convert_bitcast_fusion.3
  445.3 6.3 convert_bitcast_fusion.1
  457.5 9.7 %pad_maximum_fusion = bf16[4,2,1024,1024]{3,2,1,0:T(8,128)(2,1)} fusion(bf16[1,2,1024,1024]{3,2,1,0:T(8,128)(2,1)S(1)} %copy-done.16, bf16[1,2,1024,1024]{3,2,1,0:T(8,128)(2,1)} %convert_bitcast_fusion.1, bf16[1,2,1024,1024]{3,2,1,0:T(8,128)(2,1)S(1)} %convert_bitcast_fusion.2, bf16[1,2,1024,1024]{3,2,1,0:T(8,128)(2,1)S(1)} %copy-done.17), kind=kLoop, calls=%fused_computation | loop fusion | flops 25165824 | bytes 33554432 | tf_op jit(solution)/shard_map/stack | solution.py:501
  467.2 7.6 dynamic-slice_bitcast_fusion
  474.8 15.1 %collective-permute-start.5 = (bf16[2,2048,1024]{2,1,0:T(8,128)(2,1)}, bf16[2,2048,1024]{2,1,0:T(8,128)(2,1)}, u32[]{:S(2)}, u32[]{:S(2)}) collective-permute-start(bf16[2,2048,1024]{2,1,0:T(8,128)(2,1)} %dynamic-slice_bitcast_fusion), channel_id=1, source_target_pairs={{0,8},{1,9},{2,10},{3,11},{4,12},{5,13},{6,14},{7,15},{8,0},{9,1},... | collective-permute-start | bytes 25165832 | tf_op jit(solution)/shard_map/ppermute | solution.py:384
  492.0 7.4 fusion.11
  499.4 6.7 fusion.15
  510.8 5.7 fusion.1
  521.8 8.8 %fusion.33 = (f32[1024]{0:T(1024)S(1)}, f32[2,512]{1,0:T(2,128)S(1)}, f32[2,512,1024]{2,1,0:T(8,128)}) fusion(f32[2,512]{1,0:T(2,128)S(1)} %add_rsqrt_fusion.1, bf16[512,2,1024]{2,1,0:T(2,128)(2,1)S(1)} %copy-done.11, f32[1024]{0:T(1024)S(1)} %bitcast.329, f32[2,512,1024]{2,1,0:T(8,128)} %fusion.11, f32[2,512,1024]{2,1,0:T(8,128)} %fusion.15, ...), kind=kOutput, calls=%fused_computation.51 | convolution fusion | flops 2156918784 | bytes 20987904 | tf_op jit(solution)/shard_map/pfe,pde->pfd/dot_general | solution.py:461
  552.0 8.4 %fusion = bf16[2,2048,1024]{2,1,0:T(8,128)(2,1)S(1)} fusion(bf16[2,2048,1024]{2,1,0:T(8,128)(2,1)} %collective-permute-done.5, bf16[2,2,2048,1024]{3,2,1,0:T(8,128)(2,1)} %bitcast.283, s32[]{:T(128)S(6)} %select_n.245), kind=kLoop, calls=%fused_computation.2 | loop fusion | flops 16777216 | bytes 25165828 | tf_op jit(solution)/shard_map/convert_element_type | solution.py:478
  563.5 16.7 %collective-permute-done.27 = bf16[352,512]{1,0:T(8,128)(2,1)S(1)} collective-permute-done((bf16[352,512]{1,0:T(8,128)(2,1)S(1)}, bf16[352,512]{1,0:T(8,128)(2,1)S(1)}, u32[]{:S(2)}, u32[]{:S(2)}) %collective-permute-start.27) | collective-permute-done | bytes 360480 | tf_op jit(solution)/shard_map/ppermute | solution.py:384
  581.1 25.7 %collective-permute-done.18 = bf16[4,128,2816]{2,1,0:T(8,128)(2,1)} collective-permute-done((bf16[4,128,2816]{2,1,0:T(8,128)(2,1)}, bf16[4,128,2816]{2,1,0:T(8,128)(2,1)}, u32[]{:S(2)}, u32[]{:S(2)}) %collective-permute-start.18) | collective-permute-done | bytes 2883616 | tf_op jit(solution)/shard_map/ppermute | solution.py:384
  618.9 41.9 %collective-permute-done.29 = bf16[352,512]{1,0:T(8,128)(2,1)S(1)} collective-permute-done((bf16[352,512]{1,0:T(8,128)(2,1)S(1)}, bf16[352,512]{1,0:T(8,128)(2,1)S(1)}, u32[]{:S(2)}, u32[]{:S(2)}) %collective-permute-start.29) | collective-permute-done | bytes 360480 | tf_op jit(solution)/shard_map/ppermute | solution.py:384
  664.4 9.6 %collective-permute-done.20 = bf16[128,2816]{1,0:T(8,128)(2,1)S(1)} collective-permute-done((bf16[128,2816]{1,0:T(8,128)(2,1)S(1)}, bf16[128,2816]{1,0:T(8,128)(2,1)S(1)}, u32[]{:S(2)}, u32[]{:S(2)}) %collective-permute-start.20) | collective-permute-done | bytes 720928 | tf_op jit(solution)/shard_map/ppermute | solution.py:384
  680.8 12.4 %collective-permute-done.22 = bf16[128,2816]{1,0:T(8,128)(2,1)S(1)} collective-permute-done((bf16[128,2816]{1,0:T(8,128)(2,1)S(1)}, bf16[128,2816]{1,0:T(8,128)(2,1)S(1)}, u32[]{:S(2)}, u32[]{:S(2)}) %collective-permute-start.22) | collective-permute-done | bytes 720928 | tf_op jit(solution)/shard_map/ppermute | solution.py:384
  703.5 9.0 %add_multiply_fusion.2 = (f32[2,352,1024]{2,1,0:T(8,128)}, f32[2,352,1024]{2,1,0:T(8,128)}, f32[2,352,1024]{2,1,0:T(8,128)}, f32[2,352,1024]{2,1,0:T(8,128)}) fusion(f32[2,352,1024]{2,1,0:T(8,128)} %param.36, f32[2,352,1024]{2,1,0:T(8,128)} %param.26, f32[2,352,1024]{2,1,0:T(8,128)} %param.31, f32[2,352,512]{2,1,0:T(8,128)S(1)} %get-tuple-element.136, ...), kind=kLoop, calls=%fused_computation.84 | loop fusion | flops 6488064 | bytes 23068672 | tf_op jit(solution)/shard_map/add | solution.py:49
  714.1 12.6 %collective-permute-done.11 = bf16[4,128,1024]{2,1,0:T(8,128)(2,1)} collective-permute-done((bf16[4,128,1024]{2,1,0:T(8,128)(2,1)}, bf16[4,128,1024]{2,1,0:T(8,128)(2,1)}, u32[]{:S(2)}, u32[]{:S(2)}) %collective-permute-start.11) | collective-permute-done | bytes 1048608 | tf_op jit(solution)/shard_map/ppermute | solution.py:384
  733.2 15.6 %collective-permute-done.7 = bf16[4,128,1024]{2,1,0:T(8,128)(2,1)} collective-permute-done((bf16[4,128,1024]{2,1,0:T(8,128)(2,1)}, bf16[4,128,1024]{2,1,0:T(8,128)(2,1)}, u32[]{:S(2)}, u32[]{:S(2)}) %collective-permute-start.7) | collective-permute-done | bytes 1048608 | tf_op jit(solution)/shard_map/ppermute | solution.py:384
  761.0 15.2 %collective-permute-done.9 = bf16[128,1024]{1,0:T(8,128)(2,1)S(1)} collective-permute-done((bf16[128,1024]{1,0:T(8,128)(2,1)S(1)}, bf16[128,1024]{1,0:T(8,128)(2,1)S(1)}, u32[]{:S(2)}, u32[]{:S(2)}) %collective-permute-start.9) | collective-permute-done | bytes 262176 | tf_op jit(solution)/shard_map/ppermute | solution.py:384
  777.8 11.8 %collective-permute-done.15 = bf16[2,128,1024]{2,1,0:T(8,128)(2,1)S(1)} collective-permute-done((bf16[2,128,1024]{2,1,0:T(8,128)(2,1)S(1)}, bf16[2,128,1024]{2,1,0:T(8,128)(2,1)S(1)}, u32[]{:S(2)}, u32[]{:S(2)}) %collective-permute-start.15) | collective-permute-done | bytes 524320 | tf_op jit(solution)/shard_map/ppermute | solution.py:384
  790.7 12.4 %add_multiply_fusion = (f32[2,128,5632]{2,1,0:T(8,128)}, f32[2,128,5632]{2,1,0:T(8,128)}, f32[2,128,5632]{2,1,0:T(8,128)}, f32[2,128,5632]{2,1,0:T(8,128)}) fusion(f32[2,128,5632]{2,1,0:T(8,128)} %param.35, f32[2,128,5632]{2,1,0:T(8,128)} %param.25, f32[2,128,5632]{2,1,0:T(8,128)} %param.30, f32[2,128,2816]{2,1,0:T(8,128)S(1)} %get-tuple-element.127, ...), kind=kLoop, calls=%fused_computation.13 | loop fusion | flops 12976128 | bytes 46137344 | tf_op jit(solution)/shard_map/add | solution.py:49
  810.2 5.1 add_multiply_fusion.1
  (232 shorter events, 178.3 us)
Async XLA Ops:
  204.7 24.1 %collective-permute-start = (bf16[4,1024]{1,0:T(4,128)(2,1)S(1)}, bf16[4,1024]{1,0:T(4,128)(2,1)S(1)}, u32[]{:S(2)}, u32[]{:S(2)}) collective-permute-start(bf16[4,1024]{1,0:T(4,128)(2,1)S(1)} %pad_maximum_fusion.8), channel_id=1, source_target_pairs={{0,1},{1,2},{2,3},{3,4},{4,5},{5,6},{6,7},{7,8},{8,9},{9,10},{10,1... | collective-permute-start | bytes 24584 | tf_op jit(solution)/shard_map/ppermute | solution.py:384
  214.2 34.0 %collective-permute-start.2 = (bf16[512,1024]{1,0:T(8,128)(2,1)}, bf16[512,1024]{1,0:T(8,128)(2,1)}, u32[]{:S(2)}, u32[]{:S(2)}) collective-permute-start(bf16[512,1024]{1,0:T(8,128)(2,1)} %get-tuple-element.143), channel_id=1, source_target_pairs={{0,16},{1,17},{2,18},{3,19},{4,20},{5,21},{6,22},{7,23},{8,24},{9,... | collective-permute-start | bytes 3145736 | tf_op jit(solution)/shard_map/ppermute | solution.py:384
  248.1 25.1 %collective-permute-start.1 = (bf16[512,1024]{1,0:T(8,128)(2,1)S(1)}, bf16[512,1024]{1,0:T(8,128)(2,1)S(1)}, u32[]{:S(2)}, u32[]{:S(2)}) collective-permute-start(bf16[512,1024]{1,0:T(8,128)(2,1)S(1)} %get-tuple-element.145), channel_id=1, source_target_pairs={{0,16},{1,17},{2,18},{3,19},{4,20},{5,21},{6,22},{7,23},{8,24},{9,... | collective-permute-start | bytes 3145736 | tf_op jit(solution)/shard_map/ppermute | solution.py:384
  351.1 46.9 %collective-permute-start.3 = (bf16[2,512,1024]{2,1,0:T(8,128)(2,1)}, bf16[2,512,1024]{2,1,0:T(8,128)(2,1)}, u32[]{:S(2)}, u32[]{:S(2)}) collective-permute-start(bf16[2,512,1024]{2,1,0:T(8,128)(2,1)} %pad_maximum_fusion.6), channel_id=1, source_target_pairs={{0,16},{1,17},{2,18},{3,19},{4,20},{5,21},{6,22},{7,23},{8,24},{9,... | collective-permute-start | bytes 6291464 | tf_op jit(solution)/shard_map/ppermute | solution.py:384
  357.1 153.6 %collective-permute-start.17 = (bf16[1024,2816]{1,0:T(8,128)(2,1)}, bf16[1024,2816]{1,0:T(8,128)(2,1)}, u32[]{:S(2)}, u32[]{:S(2)}) collective-permute-start(bf16[1024,2816]{1,0:T(8,128)(2,1)} %dynamic-slice_bitcast_fusion.1), channel_id=1, source_target_pairs={{0,8},{1,9},{2,10},{3,11},{4,12},{5,13},{6,14},{7,15},{8,0},{9,1},... | collective-permute-start | bytes 17301512 | tf_op jit(solution)/shard_map/ppermute | solution.py:384
  474.8 76.1 %collective-permute-start.5 = (bf16[2,2048,1024]{2,1,0:T(8,128)(2,1)}, bf16[2,2048,1024]{2,1,0:T(8,128)(2,1)}, u32[]{:S(2)}, u32[]{:S(2)}) collective-permute-start(bf16[2,2048,1024]{2,1,0:T(8,128)(2,1)} %dynamic-slice_bitcast_fusion), channel_id=1, source_target_pairs={{0,8},{1,9},{2,10},{3,11},{4,12},{5,13},{6,14},{7,15},{8,0},{9,1},... | collective-permute-start | bytes 25165832 | tf_op jit(solution)/shard_map/ppermute | solution.py:384
  491.9 15.0 %collective-permute-start.24 = (bf16[2816,512]{1,0:T(8,128)(2,1)S(1)}, bf16[2816,512]{1,0:T(8,128)(2,1)}, u32[]{:S(2)}, u32[]{:S(2)}) collective-permute-start(bf16[2816,512]{1,0:T(8,128)(2,1)S(1)} %dynamic-slice_bitcast_fusion.3), channel_id=1, source_target_pairs={{0,8},{1,9},{2,10},{3,11},{4,12},{5,13},{6,14},{7,15},{8,0},{9,1},... | collective-permute-start | bytes 8650760 | tf_op jit(solution)/shard_map/ppermute | solution.py:384
  510.8 34.7 %collective-permute-start.25 = (bf16[4,352,512]{2,1,0:T(8,128)(2,1)}, bf16[4,352,512]{2,1,0:T(8,128)(2,1)}, u32[]{:S(2)}, u32[]{:S(2)}) collective-permute-start(bf16[4,352,512]{2,1,0:T(8,128)(2,1)} %dynamic-slice_bitcast_fusion.5), channel_id=1, source_target_pairs={{0,1},{1,0},{2,3},{3,2},{4,5},{5,4},{6,7},{7,6},{8,9},{9,8},{10,11... | collective-permute-start | bytes 4325384 | tf_op jit(solution)/shard_map/ppermute | solution.py:384
  518.3 88.5 %collective-permute-start.18 = (bf16[4,128,2816]{2,1,0:T(8,128)(2,1)}, bf16[4,128,2816]{2,1,0:T(8,128)(2,1)}, u32[]{:S(2)}, u32[]{:S(2)}) collective-permute-start(bf16[4,128,2816]{2,1,0:T(8,128)(2,1)} %dynamic-slice_bitcast_fusion.4), channel_id=1, source_target_pairs={{0,1},{1,0},{2,3},{3,2},{4,5},{5,4},{6,7},{7,6},{8,9},{9,8},{10,11... | collective-permute-start | bytes 8650760 | tf_op jit(solution)/shard_map/ppermute | solution.py:384
  539.9 73.0 %collective-permute-start.33 = (f32[4,2,128]{2,0,1:T(4,128)S(1)}, f32[4,2,128]{2,0,1:T(4,128)S(1)}, u32[]{:S(2)}, u32[]{:S(2)}) collective-permute-start(f32[4,2,128]{2,0,1:T(4,128)S(1)} %bitcast.333), channel_id=1, source_target_pairs={{0,1},{1,0},{2,3},{3,2},{4,5},{5,4},{6,7},{7,6},{8,9},{9,8},{10,11... | collective-permute-start | bytes 12296 | tf_op jit(solution)/shard_map/ppermute | solution.py:384
  547.4 15.5 %collective-permute-start.28 = (bf16[352,512]{1,0:T(8,128)(2,1)S(1)}, bf16[352,512]{1,0:T(8,128)(2,1)S(1)}, u32[]{:S(2)}, u32[]{:S(2)}) collective-permute-start(bf16[352,512]{1,0:T(8,128)(2,1)S(1)} %get-tuple-element.147), channel_id=1, source_target_pairs={{0,6},{1,7},{2,0},{3,1},{4,2},{5,3},{6,4},{7,5},{8,14},{9,15},{10,... | collective-permute-start | bytes 1081352 | tf_op jit(solution)/shard_map/ppermute | solution.py:384
  550.8 29.3 %collective-permute-start.27 = (bf16[352,512]{1,0:T(8,128)(2,1)S(1)}, bf16[352,512]{1,0:T(8,128)(2,1)S(1)}, u32[]{:S(2)}, u32[]{:S(2)}) collective-permute-start(bf16[352,512]{1,0:T(8,128)(2,1)S(1)} %get-tuple-element.148), channel_id=1, source_target_pairs={{0,4},{1,5},{2,6},{3,7},{4,0},{5,1},{6,2},{7,3},{8,12},{9,13},{10,... | collective-permute-start | bytes 1081352 | tf_op jit(solution)/shard_map/ppermute | solution.py:384
  550.9 29.3 %collective-permute-start.26 = (bf16[352,512]{1,0:T(8,128)(2,1)S(1)}, bf16[352,512]{1,0:T(8,128)(2,1)S(1)}, u32[]{:S(2)}, u32[]{:S(2)}) collective-permute-start(bf16[352,512]{1,0:T(8,128)(2,1)S(1)} %get-tuple-element.146), channel_id=1, source_target_pairs={{0,2},{1,3},{2,4},{3,5},{4,6},{5,7},{6,0},{7,1},{8,10},{9,11},{10,... | collective-permute-start | bytes 1081352 | tf_op jit(solution)/shard_map/ppermute | solution.py:384
  562.8 131.8 %collective-permute-start.6 = (bf16[2048,1024]{1,0:T(8,128)(2,1)}, bf16[2048,1024]{1,0:T(8,128)(2,1)}, u32[]{:S(2)}, u32[]{:S(2)}) collective-permute-start(bf16[2048,1024]{1,0:T(8,128)(2,1)} %dynamic-slice_bitcast_fusion.2), channel_id=1, source_target_pairs={{0,16},{1,17},{2,18},{3,19},{4,20},{5,21},{6,22},{7,23},{8,24},{9,... | collective-permute-start | bytes 12582920 | tf_op jit(solution)/shard_map/ppermute | solution.py:384
  580.4 80.4 %collective-permute-start.29 = (bf16[352,512]{1,0:T(8,128)(2,1)S(1)}, bf16[352,512]{1,0:T(8,128)(2,1)S(1)}, u32[]{:S(2)}, u32[]{:S(2)}) collective-permute-start(bf16[352,512]{1,0:T(8,128)(2,1)S(1)} %fusion.73), channel_id=1, source_target_pairs={{0,16},{1,17},{2,18},{3,19},{4,20},{5,21},{6,22},{7,23},{8,24},{9,... | collective-permute-start | bytes 1081352 | tf_op jit(solution)/shard_map/ppermute | solution.py:384
  609.7 53.8 %collective-permute-start.21 = (bf16[128,2816]{1,0:T(8,128)(2,1)S(1)}, bf16[128,2816]{1,0:T(8,128)(2,1)S(1)}, u32[]{:S(2)}, u32[]{:S(2)}) collective-permute-start(bf16[128,2816]{1,0:T(8,128)(2,1)S(1)} %get-tuple-element.138), channel_id=1, source_target_pairs={{0,6},{1,7},{2,0},{3,1},{4,2},{5,3},{6,4},{7,5},{8,14},{9,15},{10,... | collective-permute-start | bytes 2162696 | tf_op jit(solution)/shard_map/ppermute | solution.py:384
  612.9 61.0 %collective-permute-start.20 = (bf16[128,2816]{1,0:T(8,128)(2,1)S(1)}, bf16[128,2816]{1,0:T(8,128)(2,1)S(1)}, u32[]{:S(2)}, u32[]{:S(2)}) collective-permute-start(bf16[128,2816]{1,0:T(8,128)(2,1)S(1)} %get-tuple-element.139), channel_id=1, source_target_pairs={{0,4},{1,5},{2,6},{3,7},{4,0},{5,1},{6,2},{7,3},{8,12},{9,13},{10,... | collective-permute-start | bytes 2162696 | tf_op jit(solution)/shard_map/ppermute | solution.py:384
  613.0 61.2 %collective-permute-start.19 = (bf16[128,2816]{1,0:T(8,128)(2,1)S(1)}, bf16[128,2816]{1,0:T(8,128)(2,1)S(1)}, u32[]{:S(2)}, u32[]{:S(2)}) collective-permute-start(bf16[128,2816]{1,0:T(8,128)(2,1)S(1)} %get-tuple-element.137), channel_id=1, source_target_pairs={{0,2},{1,3},{2,4},{3,5},{4,6},{5,7},{6,0},{7,1},{8,10},{9,11},{10,... | collective-permute-start | bytes 2162696 | tf_op jit(solution)/shard_map/ppermute | solution.py:384
  660.8 13.9 %collective-permute-start.36 = (f32[2,128]{1,0:T(2,128)S(1)}, f32[2,128]{1,0:T(2,128)S(1)}, u32[]{:S(2)}, u32[]{:S(2)}) collective-permute-start(f32[2,128]{1,0:T(2,128)S(1)} %bitcast.337), channel_id=1, source_target_pairs={{0,6},{1,7},{2,0},{3,1},{4,2},{5,3},{6,4},{7,5},{8,14},{9,15},{10,... | collective-permute-start | bytes 3080 | tf_op jit(solution)/shard_map/ppermute | solution.py:384
  663.6 11.8 %collective-permute-start.35 = (f32[2,128]{1,0:T(2,128)S(1)}, f32[2,128]{1,0:T(2,128)S(1)}, u32[]{:S(2)}, u32[]{:S(2)}) collective-permute-start(f32[2,128]{1,0:T(2,128)S(1)} %bitcast.336), channel_id=1, source_target_pairs={{0,4},{1,5},{2,6},{3,7},{4,0},{5,1},{6,2},{7,3},{8,12},{9,13},{10,... | collective-permute-start | bytes 3080 | tf_op jit(solution)/shard_map/ppermute | solution.py:384
  674.7 18.6 %collective-permute-start.22 = (bf16[128,2816]{1,0:T(8,128)(2,1)S(1)}, bf16[128,2816]{1,0:T(8,128)(2,1)S(1)}, u32[]{:S(2)}, u32[]{:S(2)}) collective-permute-start(bf16[128,2816]{1,0:T(8,128)(2,1)S(1)} %fusion.64), channel_id=1, source_target_pairs={{0,16},{1,17},{2,18},{3,19},{4,20},{5,21},{6,22},{7,23},{8,24},{9,... | collective-permute-start | bytes 2162696 | tf_op jit(solution)/shard_map/ppermute | solution.py:384
  694.6 59.7 %collective-permute-start.23 = (bf16[2,128,2816]{2,1,0:T(8,128)(2,1)}, bf16[2,128,2816]{2,1,0:T(8,128)(2,1)}, u32[]{:S(2)}, u32[]{:S(2)}) collective-permute-start(bf16[2,128,2816]{2,1,0:T(8,128)(2,1)} %maximum_select_fusion.4), channel_id=1, source_target_pairs={{0,8},{1,9},{2,10},{3,11},{4,12},{5,13},{6,14},{7,15},{8,0},{9,1},... | collective-permute-start | bytes 4325384 | tf_op jit(solution)/shard_map/ppermute | solution.py:384
  700.4 26.3 %collective-permute-start.11 = (bf16[4,128,1024]{2,1,0:T(8,128)(2,1)}, bf16[4,128,1024]{2,1,0:T(8,128)(2,1)}, u32[]{:S(2)}, u32[]{:S(2)}) collective-permute-start(bf16[4,128,1024]{2,1,0:T(8,128)(2,1)} %dynamic-slice_bitcast_fusion.6), channel_id=1, source_target_pairs={{0,1},{1,0},{2,3},{3,2},{4,5},{5,4},{6,7},{7,6},{8,9},{9,8},{10,11... | collective-permute-start | bytes 3145736 | tf_op jit(solution)/shard_map/ppermute | solution.py:384
  701.8 46.9 %collective-permute-start.7 = (bf16[4,128,1024]{2,1,0:T(8,128)(2,1)}, bf16[4,128,1024]{2,1,0:T(8,128)(2,1)}, u32[]{:S(2)}, u32[]{:S(2)}) collective-permute-start(bf16[4,128,1024]{2,1,0:T(8,128)(2,1)} %dynamic-slice_bitcast_fusion.7), channel_id=1, source_target_pairs={{0,1},{1,0},{2,3},{3,2},{4,5},{5,4},{6,7},{7,6},{8,9},{9,8},{10,11... | collective-permute-start | bytes 3145736 | tf_op jit(solution)/shard_map/ppermute | solution.py:384
  728.4 25.9 %collective-permute-start.14 = (bf16[128,1024]{1,0:T(8,128)(2,1)S(1)}, bf16[128,1024]{1,0:T(8,128)(2,1)S(1)}, u32[]{:S(2)}, u32[]{:S(2)}) collective-permute-start(bf16[128,1024]{1,0:T(8,128)(2,1)S(1)} %get-tuple-element.153), channel_id=1, source_target_pairs={{0,6},{1,7},{2,0},{3,1},{4,2},{5,3},{6,4},{7,5},{8,14},{9,15},{10,... | collective-permute-start | bytes 786440 | tf_op jit(solution)/shard_map/ppermute | solution.py:384
  732.2 25.7 %collective-permute-start.13 = (bf16[128,1024]{1,0:T(8,128)(2,1)S(1)}, bf16[128,1024]{1,0:T(8,128)(2,1)S(1)}, u32[]{:S(2)}, u32[]{:S(2)}) collective-permute-start(bf16[128,1024]{1,0:T(8,128)(2,1)S(1)} %get-tuple-element.154), channel_id=1, source_target_pairs={{0,4},{1,5},{2,6},{3,7},{4,0},{5,1},{6,2},{7,3},{8,12},{9,13},{10,... | collective-permute-start | bytes 786440 | tf_op jit(solution)/shard_map/ppermute | solution.py:384
  732.2 25.7 %collective-permute-start.12 = (bf16[128,1024]{1,0:T(8,128)(2,1)S(1)}, bf16[128,1024]{1,0:T(8,128)(2,1)S(1)}, u32[]{:S(2)}, u32[]{:S(2)}) collective-permute-start(bf16[128,1024]{1,0:T(8,128)(2,1)S(1)} %get-tuple-element.152), channel_id=1, source_target_pairs={{0,2},{1,3},{2,4},{3,5},{4,6},{5,7},{6,0},{7,1},{8,10},{9,11},{10,... | collective-permute-start | bytes 786440 | tf_op jit(solution)/shard_map/ppermute | solution.py:384
  750.5 10.6 %collective-permute-start.10 = (bf16[128,1024]{1,0:T(8,128)(2,1)S(1)}, bf16[128,1024]{1,0:T(8,128)(2,1)S(1)}, u32[]{:S(2)}, u32[]{:S(2)}) collective-permute-start(bf16[128,1024]{1,0:T(8,128)(2,1)S(1)} %get-tuple-element.150), channel_id=1, source_target_pairs={{0,6},{1,7},{2,0},{3,1},{4,2},{5,3},{6,4},{7,5},{8,14},{9,15},{10,... | collective-permute-start | bytes 786440 | tf_op jit(solution)/shard_map/ppermute | solution.py:384
  754.3 22.0 %collective-permute-start.9 = (bf16[128,1024]{1,0:T(8,128)(2,1)S(1)}, bf16[128,1024]{1,0:T(8,128)(2,1)S(1)}, u32[]{:S(2)}, u32[]{:S(2)}) collective-permute-start(bf16[128,1024]{1,0:T(8,128)(2,1)S(1)} %get-tuple-element.151), channel_id=1, source_target_pairs={{0,4},{1,5},{2,6},{3,7},{4,0},{5,1},{6,2},{7,3},{8,12},{9,13},{10,... | collective-permute-start | bytes 786440 | tf_op jit(solution)/shard_map/ppermute | solution.py:384
  754.3 22.0 %collective-permute-start.8 = (bf16[128,1024]{1,0:T(8,128)(2,1)S(1)}, bf16[128,1024]{1,0:T(8,128)(2,1)S(1)}, u32[]{:S(2)}, u32[]{:S(2)}) collective-permute-start(bf16[128,1024]{1,0:T(8,128)(2,1)S(1)} %get-tuple-element.149), channel_id=1, source_target_pairs={{0,2},{1,3},{2,4},{3,5},{4,6},{5,7},{6,0},{7,1},{8,10},{9,11},{10,... | collective-permute-start | bytes 786440 | tf_op jit(solution)/shard_map/ppermute | solution.py:384
  776.5 13.0 %collective-permute-start.15 = (bf16[2,128,1024]{2,1,0:T(8,128)(2,1)S(1)}, bf16[2,128,1024]{2,1,0:T(8,128)(2,1)S(1)}, u32[]{:S(2)}, u32[]{:S(2)}) collective-permute-start(bf16[2,128,1024]{2,1,0:T(8,128)(2,1)S(1)} %pad_maximum_fusion.7), channel_id=1, source_target_pairs={{0,16},{1,17},{2,18},{3,19},{4,20},{5,21},{6,22},{7,23},{8,24},{9,... | collective-permute-start | bytes 1572872 | tf_op jit(solution)/shard_map/ppermute | solution.py:384
  790.7 12.6 %collective-permute-start.16 = (bf16[2,2,128,1024]{3,2,1,0:T(8,128)(2,1)}, bf16[2,2,128,1024]{3,2,1,0:T(8,128)(2,1)S(1)}, u32[]{:S(2)}, u32[]{:S(2)}) collective-permute-start(bf16[2,2,128,1024]{3,2,1,0:T(8,128)(2,1)} %maximum_select_fusion.7), channel_id=1, source_target_pairs={{0,8},{1,9},{2,10},{3,11},{4,12},{5,13},{6,14},{7,15},{8,0},{9,1},... | collective-permute-start | bytes 3145736 | tf_op jit(solution)/shard_map/ppermute | solution.py:384
  (42 other events, 713.1 us)

commit v2 on v1

--- a/solution.py
+++ b/solution.py
@@ -238,37 +238,6 @@
         out[p] = functools.reduce(jnp.add, mixed).astype(BF)
 
 
-def attend_back_kernel(head_size, carried, q, k, v, edge, mixed_grad, dq, dk, dv, edge_out):
-    frames = q.shape[1]
-    ones = head_ones(q.shape[2], head_size)
-    allowed = jnp.broadcast_to(carried[...], q.shape[1:]) > 0.5
-    queries, keys, values = load_heads(q, k, v, edge)
-    scale = 1.0 / math.sqrt(head_size)
-    key_grads = [0.0] * 4
-    value_grads = [0.0] * 4
-    for p in range(2):
-        probs = head_probs(queries, keys, p, allowed, ones, math.sqrt(head_size))
-        grad = mixed_grad[p].astype(F32)
-        dprobs = [nn((grad * values[n]).astype(BF), ones) for n in KEYS[p]]
-        mean = functools.reduce(jnp.add, [a * b for a, b in zip(probs, dprobs)])
-        query_grad = 0.0
-        for n, pr, dp in zip(KEYS[p], probs, dprobs):
-            ds = (pr * (dp - mean)).astype(BF).astype(F32)
-            query_grad = query_grad + ds * keys[n]
-            key_grads[n] = key_grads[n] + ds * queries[p]
-            value_grads[n] = value_grads[n] + pr.astype(BF).astype(F32) * grad
-        dq[p] = (query_grad * scale).astype(BF)
-    last = lax.broadcasted_iota(jnp.int32, q.shape[1:], 0) == frames - 1
-    for kind, (grads, out, factor) in enumerate(((key_grads, dk, scale), (value_grads, dv, 1.0))):
-        for p in range(2):
-            before = grads[p] * factor
-            total = grads[2 + p] * factor + jnp.where(last, 0.0, pltpu.roll(before, frames - 1, 0))
-            out[p] = total.astype(BF)
-            row = 2 * kind + p
-            edge_out[row : row + 1, :] = before[0:1, :]
-            edge_out[4 + row : 5 + row, :] = total[frames - 1 : frames, :]
-
-
 def attention_specs(frames, width, lanes):
     rows = pl.BlockSpec((2, frames, lanes), lambda j: (0, 0, j))
     edge = pl.BlockSpec((8, lanes), lambda j: (0, j))
@@ -291,69 +260,639 @@
     )(carried, q, k, v, edge)
 
 
-def attend_back(carried, q, k, v, edge, mixed_grad, head_size):
-    _, frames, width = q.shape
-    lanes = 256
-    rows, edge_spec, mask = attention_specs(frames, width, lanes)
-    return pl.pallas_call(
-        functools.partial(attend_back_kernel, head_size),
-        grid=(width // lanes,),
-        out_shape=(jax.ShapeDtypeStruct(q.shape, BF),) * 3 + (jax.ShapeDtypeStruct((8, width), F32),),
-        in_specs=[mask, rows, rows, rows, edge_spec, rows],
-        out_specs=(rows, rows, rows, edge_spec),
-        compiler_params=pltpu.CompilerParams(vmem_limit_bytes=VMEM_BYTES),
-        name="attend_back",
-    )(carried, q, k, v, edge, mixed_grad)
-
-
-def feed_forward_kernel(b, c, inner, down, out, back, inner_grad, down_grad):
+def remote_copy(src, dst, send_sem, recv_sem, peer):
+    return pltpu.make_async_remote_copy(
+        src_ref=src, dst_ref=dst, send_sem=send_sem, recv_sem=recv_sem, device_id=peer, device_id_type=MESH
+    )
+
+
+def feed_forward_kernel(
+    X, J, b, c, inner, down, out_mine, back_mine, out_theirs, back_recv, inner_all, down_sum,
+    out, back, down_here, down_there, down_from_core, mine, other, from_core, summed, from_x, column, from_z, final, staged,
+    s1, r1, s2, r2, s3, r3, s5, r5, s6, r6, s7, r7, local_sem,
+):
+    j = pl.program_id(0)
     half = down.shape[2]
-
-    @pl.when(pl.program_id(0) == 0)
-    def _():
+    rows_here = out_mine.shape[0]
+    R, step = final.shape[1:]
+    dp, fs = lax.axis_index("dp"), lax.axis_index("fsdp")
+    y, core = dp // 2, dp % 2
+    z, x = fs // X, fs % X
+    core_peer = (y * 2 + 1 - core, fs)
+    y_peer = ((1 - y) * 2 + core, fs)
+
+    def z_peer(k):
+        return (dp, lax.rem(z + k, Z) * X + x)
+
+    def x_peer(i):
+        return (dp, z * X + lax.rem(x + i, X))
+
+    def dp_peer(d):
+        return (((y + d // 2) % 2) * 2 + (core + d % 2) % 2, fs)
+
+    def to_core(n):
+        return remote_copy(other.at[n % 2], from_core.at[n], s1.at[n % 2], r1.at[n], core_peer)
+
+    def to_x(n, i):
+        return remote_copy(
+            summed.at[n % 2, :, lax.rem(x + i, X)], from_x.at[n, i - 1], s2.at[n % 2, i - 1], r2.at[n, i - 1], x_peer(i)
+        )
+
+    def to_z(n, k):
+        return remote_copy(
+            column.at[n % 2, lax.rem(z + k, Z)], from_z.at[n, k - 1], s3.at[n % 2, k - 1], r3.at[n, k - 1], z_peer(k)
+        )
+
+    def place(n, owner):
+        return inner_all.at[owner, :, pl.ds(pl.multiple_of(n * step, step), step)]
+
+    def share(n, d):
+        return remote_copy(final.at[n], place(n, dp), s5.at[n, d - 1], r5.at[n, d - 1], dp_peer(d))
+
+    def keep(n):
+        return pltpu.make_async_copy(final.at[n], place(n, dp), local_sem.at[n])
+
+    exchange = remote_copy(staged, back_recv, s6, r6, y_peer)
+
+    def down_to_core(n):
+        return remote_copy(down_there.at[n % 2], down_from_core.at[n], s7.at[n % 2], r7.at[n], core_peer)
+
+    @pl.when(j == 0)
+    def _():
+        barrier = pltpu.get_barrier_semaphore()
+        peers = [z_peer(k) for k in range(1, Z)] + [x_peer(i) for i in range(1, X)]
+        peers += [dp_peer(d) for d in range(1, 4)]
+        for peer in peers:
+            pl.semaphore_signal(barrier, inc=1, device_id=peer, device_id_type=MESH)
+        pl.semaphore_wait(barrier, len(peers))
         out[...] = jnp.zeros_like(out)
         back[...] = jnp.zeros_like(back)
 
-    rows, cot = b[...], c[...]
-    gate = nn(rows, inner[0])
-    up = nn(rows, inner[1])
-    squashed = jax.nn.sigmoid(gate)
-    active = gate * squashed
-    hidden = (active * up).astype(BF)
-    hidden_grad = nt(cot[:, :half], down[0]) + nt(cot[:, half:], down[1])
-    gate_grad = (hidden_grad * up * (squashed * (1.0 + gate * (1.0 - squashed)))).astype(BF)
-    up_grad = (hidden_grad * active).astype(BF)
-    for n in range(2):
-        part = slice(n * half, (n + 1) * half)
-        down_grad[n] = tn(hidden, cot[:, part]).astype(BF)
-        out[:, part] += nn(hidden, down[n])
-    inner_grad[0] = tn(rows, gate_grad).astype(BF)
-    inner_grad[1] = tn(rows, up_grad).astype(BF)
-    back[...] += nt(gate_grad, inner[0]) + nt(up_grad, inner[1])
-
-
-def feed_forward(b, c, inner, down):
+    @pl.when((j >= 1) & (j < J + 1))
+    def _():
+        n = j - 1
+        to_core(n).wait_recv()
+
+        @pl.when(n >= 2)
+        def _():
+            for i in range(1, X):
+                to_x(n - 2, i).wait_send()
+
+        down_to_core(n).wait_recv()
+        down_sum[...] = (down_here[n % 2].astype(F32) + down_from_core[n].astype(F32)).astype(BF)
+        total = (mine[n % 2].astype(F32) + from_core[n].astype(F32)).astype(BF)
+        summed[n % 2] = total.reshape(summed.shape[1:])
+        for i in range(1, X):
+            to_x(n, i).start()
+
+    @pl.when((j >= 2) & (j < J + 2))
+    def _():
+        n = j - 2
+        for i in range(1, X):
+            to_x(n, i).wait_recv()
+
+        @pl.when(n >= 2)
+        def _():
+            for k in range(1, Z):
+                to_z(n - 2, k).wait_send()
+
+        total = summed[n % 2, :, x].astype(F32)
+        for i in range(1, X):
+            total = total + from_x[n, i - 1].astype(F32)
+        column[n % 2] = total.astype(BF)
+        for k in range(1, Z):
+            to_z(n, k).start()
+
+    @pl.when(j >= 3)
+    def _():
+        n = j - 3
+        for k in range(1, Z):
+            to_z(n, k).wait_recv()
+        total = column[n % 2, z].astype(F32)
+        for k in range(1, Z):
+            total = total + from_z[n, k - 1].astype(F32)
+        final[n] = total.astype(BF)
+        keep(n).start()
+        for d in range(1, 4):
+            share(n, d).start()
+
+    @pl.when(j < J)
+    def _():
+        rows, cot = b[...], c[...]
+        gate = nn(rows, inner[0])
+        up = nn(rows, inner[1])
+        squashed = jax.nn.sigmoid(gate)
+        active = gate * squashed
+        hidden = (active * up).astype(BF)
+        hidden_grad = nt(cot[:, :half], down[0]) + nt(cot[:, half:], down[1])
+        gate_grad = (hidden_grad * up * (squashed * (1.0 + gate * (1.0 - squashed)))).astype(BF)
+        up_grad = (hidden_grad * active).astype(BF)
+        gate_term = tn(rows, gate_grad).astype(BF)
+        up_term = tn(rows, up_grad).astype(BF)
+
+        @pl.when(j >= 2)
+        def _():
+            to_core(j - 2).wait_send()
+            down_to_core(j - 2).wait_send()
+
+        mine[j % 2] = jnp.where(core == 0, gate_term, up_term)
+        other[j % 2] = jnp.where(core == 0, up_term, gate_term)
+        to_core(j).start()
+        down_term = tn(hidden, cot).astype(BF)
+        down_here[j % 2] = jnp.where(core == 0, down_term[:, :half], down_term[:, half:])
+        down_there[j % 2] = jnp.where(core == 0, down_term[:, half:], down_term[:, :half])
+        down_to_core(j).start()
+        for n in range(2):
+            part = slice(n * half, (n + 1) * half)
+            out[:, part] += nn(hidden, down[n])
+        back[...] += nt(gate_grad, inner[0]) + nt(up_grad, inner[1])
+
+    @pl.when(j == J - 1)
+    def _():
+        staged[...] = back[rows_here:, :].astype(BF)
+        exchange.start()
+        out_theirs[...] = out[rows_here:, :].astype(BF)
+        out_mine[...] = out[:rows_here, :]
+        back_mine[...] = back[:rows_here, :]
+
+    @pl.when(j == J + 2)
+    def _():
+        for n in (J - 2, J - 1):
+            to_core(n).wait_send()
+            down_to_core(n).wait_send()
+            for i in range(1, X):
+                to_x(n, i).wait_send()
+            for k in range(1, Z):
+                to_z(n, k).wait_send()
+
+        def finish(n, carry):
+            keep(n).wait()
+            for d in range(1, 4):
+                share(n, d).wait()
+            return carry
+
+        lax.fori_loop(0, J, finish, 0)
+        exchange.wait()
+
+
+def feed_forward(b, c, inner, down, fsdp_count):
     rows, width = b.shape
     _, _, hidden = inner.shape
+    half = down.shape[2]
     step = 256
-    whole = pl.BlockSpec((rows, width), lambda j: (0, 0))
-    inner_spec = pl.BlockSpec((2, width, step), lambda j: (0, 0, j))
-    down_spec = pl.BlockSpec((2, step, down.shape[2]), lambda j: (0, j, 0))
+    J = hidden // step
+    X = fsdp_count // Z
+    R = width // fsdp_count
+    whole = pl.BlockSpec((rows, width), lambda j: (0, 0), pipeline_mode=pl.Buffered(1))
+    part = pl.BlockSpec((rows // 2, width), lambda j: (0, 0), pipeline_mode=pl.Buffered(1))
+    inner_spec = pl.BlockSpec((2, width, step), lambda j: (0, 0, jnp.minimum(j, J - 1)))
+    down_spec = pl.BlockSpec((2, step, half), lambda j: (0, jnp.minimum(j, J - 1), 0))
+    sum_spec = pl.BlockSpec((step, half), lambda j: (jnp.clip(j - 1, 0, J - 1), 0))
+    dma, vmem = pltpu.SemaphoreType.DMA, pltpu.VMEM
     return pl.pallas_call(
-        feed_forward_kernel,
-        grid=(hidden // step,),
+        functools.partial(feed_forward_kernel, X, J),
+        grid=(J + 3,),
         out_shape=(
-            jax.ShapeDtypeStruct((rows, width), F32),
-            jax.ShapeDtypeStruct((rows, width), F32),
-            jax.ShapeDtypeStruct(inner.shape, BF),
-            jax.ShapeDtypeStruct(down.shape, BF),
+            jax.ShapeDtypeStruct((rows // 2, width), F32),
+            jax.ShapeDtypeStruct((rows // 2, width), F32),
+            jax.ShapeDtypeStruct((rows // 2, width), BF),
+            jax.ShapeDtypeStruct((rows // 2, width), BF),
+            jax.ShapeDtypeStruct((4, R, hidden), BF),
+            jax.ShapeDtypeStruct((hidden, half), BF),
         ),
         in_specs=[whole, whole, inner_spec, down_spec],
-        out_specs=(whole, whole, inner_spec, down_spec),
-        compiler_params=pltpu.CompilerParams(vmem_limit_bytes=VMEM_BYTES),
+        out_specs=(part, part, part, ANY, ANY, sum_spec),
+        scratch_shapes=[
+            vmem((rows, width), F32), vmem((rows, width), F32),
+            vmem((2, step, half), BF), vmem((2, step, half), BF), vmem((J, step, half), BF),
+            vmem((2, width, step), BF), vmem((2, width, step), BF), vmem((J, width, step), BF),
+            vmem((2, Z, X, R, step), BF), vmem((J, X - 1, Z, R, step), BF),
+            vmem((2, Z, R, step), BF), vmem((J, Z - 1, R, step), BF),
+            vmem((J, R, step), BF), vmem((rows // 2, width), BF),
+            dma((2,)), dma((J,)), dma((2, X - 1)), dma((J, X - 1)), dma((2, Z - 1)), dma((J, Z - 1)),
+            dma((J, 3)), dma((J, 3)), dma, dma, dma((2,)), dma((J,)), dma((J,)),
+        ],
+        compiler_params=pltpu.CompilerParams(
+            vmem_limit_bytes=VMEM_BYTES, collective_id=1, has_side_effects=True
+        ),
         cost_estimate=pl.CostEstimate(flops=18 * rows * width * hidden, bytes_accessed=60 * 2**20, transcendentals=0),
         name="feed_forward",
     )(b, c, inner, down)
+
+
+PAIRS = ((0, 0), (0, 1), (0, 2), (1, 0), (1, 1), (1, 2), (1, 3))
+CHUNK = 32
+
+
+def total_of(values):
+    return functools.reduce(jnp.add, values)
+
+
+def attention_back_kernel(
+    X, groups, head_size, carried, q, k, v, edge, mix, dhb, mixed, inputs, proj, down_sum, out_send,
+    da, attn_all, down_all, out_recv,
+    mixed_grad, before, terms_before, terms_here, tails, grads, edge_send, edge_recv,
+    mine, other, from_core, keep_y, send_y, from_y, summed, from_x, column, from_z, final, plane, from_plane, final_plane,
+    down_column, down_from_x, down_from_z, down_final,
+    s_edge, r_edge, s1, r1, sy, ry, sxa, rxa, sxb, rxb, sz, rz, sf, rf, sp, rp, sc, rc, local_sem,
+    sdx, rdx, sdz, rdz, sdf, rdf, down_sem, s_out, r_out, free,
+):
+    i = pl.program_id(0)
+    frames, step = q.shape[1:]
+    R = final.shape[1]
+    dp, fs = lax.axis_index("dp"), lax.axis_index("fsdp")
+    F = Z * X
+    y, core = dp // 2, dp % 2
+    z, x = fs // X, fs % X
+    me = dp * F + fs
+    devices = 4 * F
+    core_peer = (y * 2 + 1 - core, fs)
+    y_peer = ((1 - y) * 2 + core, fs)
+    before_me = ((me - 1 + devices) % devices // F, (me - 1 + devices) % devices % F)
+    after_me = ((me + 1) % devices // F, (me + 1) % devices % F)
+
+    def z_peer(n):
+        return (dp, lax.rem(z + n, Z) * X + x)
+
+    def x_peer(n):
+        return (dp, z * X + lax.rem(x + n, X))
+
+    def dp_peer(d):
+        return (((y + d // 2) % 2) * 2 + (core + d % 2) % 2, fs)
+
+    def to_before(n):
+        return remote_copy(edge_send.at[n % 2], edge_recv.at[n], s_edge.at[n % 2], r_edge.at[n], before_me)
+
+    def to_core(n):
+        return remote_copy(other, from_core.at[n % 2], s1, r1.at[n % 2], core_peer)
+
+    def to_y(n):
+        return remote_copy(send_y.at[n % 2], from_y.at[n], sy.at[n % 2], ry.at[n], y_peer)
+
+    def to_x_early(n, j):
+        return remote_copy(
+            summed.at[n % 2, pl.ds(1, 2), :, lax.rem(x + j, X)], from_x.at[n, j - 1, pl.ds(1, 2)],
+            sxa.at[n % 2, j - 1], rxa.at[n, j - 1], x_peer(j),
+        )
+
+    def to_x_late(n, j):
+        return remote_copy(
+            summed.at[n % 2, 0, :, lax.rem(x + j, X)], from_x.at[n, j - 1, 0],
+            sxb.at[n % 2, j - 1], rxb.at[n, j - 1], x_peer(j),
+        )
+
+    def to_z(n, j):
+        return remote_copy(
+            column.at[n % 2, :, lax.rem(z + j, Z)], from_z.at[n, j - 1], sz.at[n % 2, j - 1], rz.at[n, j - 1], z_peer(j)
+        )
+
+    def place(n, t):
+        return attn_all.at[t, core, :, pl.ds(pl.multiple_of(n * step, step), step)]
+
+    def share(n, d):
+        return remote_copy(final.at[n], place(n, y), sf.at[n, d - 1], rf.at[n, d - 1], dp_peer(d))
+
+    def to_plane(n):
+        return remote_copy(plane.at[n], from_plane.at[n], sp.at[n], rp.at[n], y_peer)
+
+    def share_core(n, t):
+        return remote_copy(final_plane.at[n, t], place(n, 2 + t), sc.at[n, t], rc.at[n, t], core_peer)
+
+    def keep(n, t):
+        src = final.at[n] if t == 0 else final_plane.at[n, t - 1]
+        return pltpu.make_async_copy(src, place(n, y if t == 0 else 1 + t), local_sem.at[n, t])
+
+    def down_to_x(j):
+        return remote_copy(
+            down_sum.at[:, lax.rem(x + j, X)], down_from_x.at[j - 1], sdx.at[j - 1], rdx.at[j - 1], x_peer(j)
+        )
+
+    def down_to_z(j):
+        return remote_copy(
+            down_column.at[lax.rem(z + j, Z)], down_from_z.at[j - 1], sdz.at[j - 1], rdz.at[j - 1], z_peer(j)
+        )
+
+    def down_share(d):
+        return remote_copy(down_final, down_all.at[dp], sdf.at[d - 1], rdf.at[d - 1], dp_peer(d))
+
+    down_mine = pltpu.make_async_copy(down_sum.at[:, x], down_column, down_sem.at[0])
+    down_keep = pltpu.make_async_copy(down_final, down_all.at[dp], down_sem.at[1])
+    out_copy = remote_copy(out_send, out_recv, s_out, r_out, y_peer)
+
+    @pl.when(i == 0)
+    def _():
+        barrier = pltpu.get_barrier_semaphore()
+        peers = [z_peer(n) for n in range(1, Z)] + [x_peer(n) for n in range(1, X)]
+        peers += [dp_peer(d) for d in range(1, 4)] + [before_me, after_me]
+        for peer in peers:
+            pl.semaphore_signal(barrier, inc=1, device_id=peer, device_id_type=MESH)
+        pl.semaphore_wait(barrier, len(peers))
+        out_copy.start()
+        for j in range(1, X):
+            down_to_x(j).start()
+        down_mine.start()
+        da[...] = jnp.zeros_like(da)
+
+        @pl.when(me == devices - 1)
+        def _():
+            edge_recv[...] = jnp.zeros_like(edge_recv)
+
+    def active(first):
+        return (i >= first) & (i < first + groups)
+
+    @pl.when(active(6))
+    def _():
+        n = i - 6
+        to_plane(n).wait_recv()
+        final_plane[n] = (plane[n].astype(F32) + from_plane[n].astype(F32)).astype(BF)
+        for t in range(2):
+            keep(n, t + 1).start()
+            share_core(n, t).start()
+
+    @pl.when(active(5))
+    def _():
+        n = i - 5
+        for j in range(1, Z):
+            to_z(n, j).wait_recv()
+        total = column[n % 2, :, z].astype(F32) + total_of([from_z[n, j].astype(F32) for j in range(Z - 1)])
+        total = total.astype(BF)
+        final[n] = total[0]
+        plane[n] = total[1:]
+        to_plane(n).start()
+        keep(n, 0).start()
+        for d in range(1, 4):
+            share(n, d).start()
+
+    @pl.when(active(4))
+    def _():
+        n = i - 4
+        for j in range(1, X):
+            to_x_early(n, j).wait_recv()
+            to_x_late(n, j).wait_recv()
+
+        @pl.when(n >= 2)
+        def _():
+            for j in range(1, Z):
+                to_z(n - 2, j).wait_send()
+
+        total = summed[n % 2, :, :, x].astype(F32) + total_of([from_x[n, j].astype(F32) for j in range(X - 1)])
+        column[n % 2] = total.astype(BF)
+        for j in range(1, Z):
+            to_z(n, j).start()
+
+    @pl.when(active(3))
+    def _():
+        n = i - 3
+        to_y(n).wait_recv()
+
+        @pl.when(n >= 2)
+        def _():
+            for j in range(1, X):
+                to_x_late(n - 2, j).wait_send()
+
+        total = (keep_y[n % 2].astype(F32) + from_y[n].astype(F32)).astype(BF)
+        summed[n % 2, 0] = total.reshape(summed.shape[2:])
+        for j in range(1, X):
+            to_x_late(n, j).start()
+
+    @pl.when(active(2))
+    def _():
+        n = i - 2
+        to_core(n).wait_recv()
+
+        @pl.when(n >= 2)
+        def _():
+            to_y(n - 2).wait_send()
+            for j in range(1, X):
+                to_x_early(n - 2, j).wait_send()
+
+        def both(t):
+            return (mine[t].astype(F32) + from_core[n % 2, t].astype(F32)).astype(BF)
+
+        send_y[n % 2] = both(1 - y)
+        to_y(n).start()
+        for t in range(2):
+            summed[n % 2, 1 + t] = both(2 + t).reshape(summed.shape[2:])
+        for j in range(1, X):
+            to_x_early(n, j).start()
+        keep_y[n % 2] = both(y)
+
+        @pl.when(n < groups - 2)
+        def _():
+            pl.semaphore_signal(free, inc=1, device_id=core_peer, device_id_type=MESH)
+
+    @pl.when(i == 2)
+    def _():
+        down_mine.wait()
+        for j in range(1, X):
+            down_to_x(j).wait_recv()
+        for row in range(Z):
+            total = down_column[row].astype(F32) + total_of([down_from_x[j, row].astype(F32) for j in range(X - 1)])
+            down_column[row] = total.astype(BF)
+        for j in range(1, Z):
+            down_to_z(j).start()
+
+    @pl.when(i == 4)
+    def _():
+        for j in range(1, Z):
+            down_to_z(j).wait_recv()
+        total = down_column[z].astype(F32) + total_of([down_from_z[j].astype(F32) for j in range(Z - 1)])
+        down_final[...] = total.astype(BF)
+        down_keep.start()
+        for d in range(1, 4):
+            down_share(d).start()
+
+    @pl.when(i < groups)
+    def _():
+        slot = i % 2
+        ones = head_ones(step, head_size)
+        scale = 1.0 / math.sqrt(head_size)
+        first = lax.broadcasted_iota(jnp.int32, (frames, step), 0) == 0
+        last = lax.broadcasted_iota(jnp.int32, (frames, step), 0) == frames - 1
+        for p in range(2):
+            mixed_grad[p] = nt(dhb[p], mix[0, p]).astype(BF)
+            before[p] = jnp.where(first, edge[p : p + 1, :], pltpu.roll(k[p].astype(F32), 1, 0))
+            before[2 + p] = jnp.where(first, edge[2 + p : 3 + p, :], pltpu.roll(v[p].astype(F32), 1, 0))
+
+        def chunk(c, carry):
+            rows = pl.ds(pl.multiple_of(c * CHUNK, CHUNK), CHUNK)
+            allowed = jnp.broadcast_to(carried[rows, :], (CHUNK, step)) > 0.5
+            queries = [q[p, rows, :].astype(F32) for p in range(2)]
+            cots = [mixed_grad[p, rows, :].astype(F32) for p in range(2)]
+            keys = [before[p, rows, :] for p in range(2)] + [k[p, rows, :].astype(F32) for p in range(2)]
+            values = [before[2 + p, rows, :] for p in range(2)] + [v[p, rows, :].astype(F32) for p in range(2)]
+
+            def per_head(left, right):
+                products = [(left[p] * right[n]).astype(BF) for p, n in PAIRS]
+                sums = nn(jnp.concatenate(products, axis=0), ones)
+                return [sums[m * CHUNK : (m + 1) * CHUNK] for m in range(len(PAIRS))]
+
+            scores = per_head(queries, keys)
+            dprobs = per_head(cots, values)
+            key_grads, value_grads = [[] for _ in range(4)], [[] for _ in range(4)]
+            for p, span in ((0, range(0, 3)), (1, range(3, 7))):
+                s = [jnp.where(allowed, scores[m] * scale, -1e30) if PAIRS[m][1] < 2 else scores[m] * scale for m in span]
+                top = functools.reduce(jnp.maximum, s)
+                e = [jnp.exp(value - top) for value in s]
+                e = [jnp.where(allowed, value, 0.0) if PAIRS[m][1] < 2 else value for m, value in zip(span, e)]
+                inverse = 1.0 / total_of(e)
+                probs = [value * inverse for value in e]
+                mean = total_of([pr * dprobs[m] for m, pr in zip(span, probs)])
+                query_grad = []
+                for m, pr in zip(span, probs):
+                    n = PAIRS[m][1]
+                    ds = (pr * (dprobs[m] - mean)).astype(BF).astype(F32) * scale
+                    query_grad.append(ds * keys[n])
+                    key_grads[n].append(ds * queries[p])
+                    value_grads[n].append(pr.astype(BF).astype(F32) * cots[p])
+                grads[slot, 0, p, rows, :] = total_of(query_grad).astype(BF)
+            for p in range(2):
+                terms_before[p, rows, :] = total_of(key_grads[p])
+                terms_before[2 + p, rows, :] = total_of(value_grads[p])
+                terms_here[p, rows, :] = total_of(key_grads[2 + p])
+                terms_here[2 + p, rows, :] = total_of(value_grads[2 + p])
+            return carry
+
+        lax.fori_loop(0, frames // CHUNK, chunk, 0)
+
+        @pl.when((i >= 2) & (me > 0))
+        def _():
+            to_before(i - 2).wait_send()
+
+        for m in range(4):
+            kind, p = m // 2, m % 2
+            later = terms_before[m]
+            edge_send[slot, m : m + 1, :] = later[0:1, :]
+            total = terms_here[m] + jnp.where(last, 0.0, pltpu.roll(later, frames - 1, 0))
+            grads[slot, 1 + kind, p] = total.astype(BF)
+            tails[slot, m] = total[frames - 16 :, :]
+
+        @pl.when(me > 0)
+        def _():
+            to_before(i).start()
+
+    @pl.when(active(1))
+    def _():
+        n = i - 1
+        slot = n % 2
+
+        @pl.when(me < devices - 1)
+        def _():
+            to_before(n).wait_recv()
+
+        bottom = lax.broadcasted_iota(jnp.int32, (16, step), 0) == 15
+        for m in range(4):
+            fixed = tails[slot, m] + jnp.where(bottom, edge_recv[n, m : m + 1, :], 0.0)
+            grads[slot, 1 + m // 2, m % 2, frames - 16 :, :] = fixed.astype(BF)
+
+        @pl.when(n >= 1)
+        def _():
+            to_core(n - 1).wait_send()
+
+        for t in range(4):
+            pair = []
+            for p in range(2):
+                if t < 3:
+                    pair.append(tn(inputs[p], grads[slot, t, p]).astype(BF))
+                else:
+                    pair.append(tn(mixed[p], dhb[p, :, pl.ds(pl.multiple_of(n * step, step), step)]).astype(BF))
+            mine[t] = jnp.where(core == 0, pair[0], pair[1])
+            other[t] = jnp.where(core == 0, pair[1], pair[0])
+
+        @pl.when(n >= 2)
+        def _():
+            pl.semaphore_wait(free, 1)
+
+        to_core(n).start()
+        for p in range(2):
+            da[p] += total_of([nt(grads[slot, t, p], proj[t, p]) for t in range(3)])
+
+    @pl.when(i == groups + 5)
+    def _():
+        to_core(groups - 1).wait_send()
+        for n in (groups - 2, groups - 1):
+            @pl.when(me > 0)
+            def _():
+                to_before(n).wait_send()
+
+            to_y(n).wait_send()
+            for j in range(1, X):
+                to_x_early(n, j).wait_send()
+                to_x_late(n, j).wait_send()
+            for j in range(1, Z):
+                to_z(n, j).wait_send()
+
+        def finish(n, carry):
+            to_plane(n).wait_send()
+            keep(n, 0).wait()
+            for d in range(1, 4):
+                share(n, d).wait()
+            for t in range(2):
+                keep(n, t + 1).wait()
+                share_core(n, t).wait()
+            return carry
+
+        lax.fori_loop(0, groups, finish, 0)
+        for j in range(1, X):
+            down_to_x(j).wait_send()
+        for j in range(1, Z):
+            down_to_z(j).wait_send()
+        down_keep.wait()
+        for d in range(1, 4):
+            down_share(d).wait()
+        out_copy.wait()
+
+
+def attention_back(carried, q, k, v, edge, attn, dhb, mixed, inputs, down_sum, out_send, head_size, fsdp_count):
+    _, frames, width = q.shape
+    step = 256
+    groups = width // step
+    X = fsdp_count // Z
+    R = width // fsdp_count
+    R2, half = down_sum.shape[2:]
+
+    def early(i):
+        return jnp.minimum(i, groups - 1)
+
+    rows = pl.BlockSpec((2, frames, step), lambda i: (0, 0, early(i)))
+    edge_spec = pl.BlockSpec((8, step), lambda i: (0, early(i)))
+    mask = pl.BlockSpec((frames, 1), lambda i: (0, 0), pipeline_mode=pl.Buffered(1))
+    whole = pl.BlockSpec((2, frames, width), lambda i: (0, 0, 0), pipeline_mode=pl.Buffered(1))
+    mix_spec = pl.BlockSpec((1, 2, step, width), lambda i: (3, 0, early(i), 0))
+    proj_spec = pl.BlockSpec((3, 2, width, step), lambda i: (0, 0, 0, jnp.clip(i - 1, 0, groups - 1)))
+    dma, vmem = pltpu.SemaphoreType.DMA, pltpu.VMEM
+    n = groups
+    return pl.pallas_call(
+        functools.partial(attention_back_kernel, X, groups, head_size),
+        grid=(groups + 6,),
+        out_shape=(
+            jax.ShapeDtypeStruct((2, frames, width), F32),
+            jax.ShapeDtypeStruct((4, 2, R, width), BF),
+            jax.ShapeDtypeStruct((4, R2, half), BF),
+            jax.ShapeDtypeStruct(out_send.shape, BF),
+        ),
+        in_specs=[mask, rows, rows, rows, edge_spec, mix_spec, whole, whole, whole, proj_spec, ANY, ANY],
+        out_specs=(whole, ANY, ANY, ANY),
+        scratch_shapes=[
+            vmem((2, frames, step), BF), vmem((4, frames, step), F32), vmem((4, frames, step), F32),
+            vmem((4, frames, step), F32), vmem((2, 4, 16, step), F32), vmem((2, 3, 2, frames, step), BF),
+            vmem((2, 8, step), F32), vmem((n, 8, step), F32),
+            vmem((4, width, step), BF), vmem((4, width, step), BF), vmem((2, 4, width, step), BF),
+            vmem((2, width, step), BF), vmem((2, width, step), BF), vmem((n, width, step), BF),
+            vmem((2, 3, Z, X, R, step), BF), vmem((n, X - 1, 3, Z, R, step), BF),
+            vmem((2, 3, Z, R, step), BF), vmem((n, Z - 1, 3, R, step), BF),
+            vmem((n, R, step), BF), vmem((n, 2, R, step), BF), vmem((n, 2, R, step), BF), vmem((n, 2, R, step), BF),
+            vmem((Z, R2, half), BF), vmem((X - 1, Z, R2, half), BF), vmem((Z - 1, R2, half), BF), vmem((R2, half), BF),
+            dma((2,)), dma((n,)), dma, dma((2,)), dma((2,)), dma((n,)),
+            dma((2, X - 1)), dma((n, X - 1)), dma((2, X - 1)), dma((n, X - 1)),
+            dma((2, Z - 1)), dma((n, Z - 1)), dma((n, 3)), dma((n, 3)), dma((n,)), dma((n,)),
+            dma((n, 2)), dma((n, 2)), dma((n, 3)),
+            dma((X - 1,)), dma((X - 1,)), dma((Z - 1,)), dma((Z - 1,)), dma((3,)), dma((3,)), dma((2,)),
+            dma, dma, pltpu.SemaphoreType.REGULAR,
+        ],
+        compiler_params=pltpu.CompilerParams(vmem_limit_bytes=63 * 2**20, collective_id=2, has_side_effects=True),
+        name="attention_back",
+    )(carried, q, k, v, edge, attn, dhb, mixed, inputs, attn, down_sum, out_send)
 
 
 def per_device(
@@ -444,88 +983,30 @@
     b_there = to_y(lax.dynamic_index_in_dim(b, 1 - y, 0, keepdims=False))
     b_rows = jnp.concatenate([lax.dynamic_index_in_dim(b, y, 0, keepdims=False), b_there], axis=0)
     c_rows = jnp.concatenate([lax.dynamic_index_in_dim(cot, y, 0, keepdims=False), cot_there], axis=0)
-    out, back, inner_part, down_part = feed_forward(b_rows, c_rows, inner, down)
-    both = to_y(jnp.stack([out[frame_count:], back[frame_count:]]).astype(BF)).astype(F32)
+    out, back, out_there, back_there, inner_shares, down_sum = feed_forward(b_rows, c_rows, inner, down, fsdp_count)
 
     def by_position(mine, theirs):
         return jnp.where(y == 0, jnp.stack([mine, theirs]), jnp.stack([theirs, mine]))
 
-    layer_out = (hres + by_position(out[:frame_count], both[0])).astype(BF).transpose(1, 0, 2)
-    db = by_position(back[:frame_count], both[1])
+    db = by_position(back, back_there.astype(F32))
 
     e2 = jnp.sum(db * n2, axis=(0, 1))
     dh = cot.astype(F32) + norm_back(db, n2, gains[1], r2)
     dhb = dh.astype(BF)
-
-    def back_each(left, right):
-        return jnp.einsum("pfe,pde->pfd", left, right, preferred_element_type=F32)
-
-    def grad_each(left, right):
-        return jnp.einsum("pfd,pfe->pde", left, right, preferred_element_type=F32).astype(BF)
-
-    mixed_grad = back_each(dhb, attn[3]).astype(BF)
-    dq, dk, dv, edges = attend_back(carried, q, k, v, edge, mixed_grad, head_size)
-    edge_back = shifted(edges[:4], -1)
-    last = (edges[4:] + edge_back).astype(BF)
-    dk = lax.dynamic_update_slice(dk, last[:2, None], (0, frame_count - 1, 0))
-    dv = lax.dynamic_update_slice(dv, last[2:, None], (0, frame_count - 1, 0))
-    attn_part = [grad_each(a, dq), grad_each(a, dk), grad_each(a, dv), grad_each(mixed, dhb)]
-    da = back_each(dq, attn[0]) + back_each(dk, attn[1]) + back_each(dv, attn[2])
+    down_sum = down_sum.reshape(Z, X, -1, half_width)
+    da, attn_shares, down_shares, out_here = attention_back(
+        carried, q, k, v, edge, attn, dhb, mixed, a, down_sum, out_there, head_size, fsdp_count
+    )
+    layer_out = (hres + by_position(out, out_here.astype(F32))).astype(BF).transpose(1, 0, 2)
     e1 = jnp.sum(da * n1, axis=(0, 1))
     frames_grad = (dh + norm_back(da, n1, gains[0], r1)).astype(BF).transpose(1, 0, 2)
 
-    def add(left, right):
-        return (left.astype(F32) + right.astype(F32)).astype(BF)
-
-    def at(value, index):
-        return lax.dynamic_index_in_dim(value, index, 0, keepdims=False)
-
-    def over_fsdp(value):
-        grid = value.reshape((Z, X) + value.shape[1:])
-        column = lax.dynamic_index_in_dim(grid, x, 1, keepdims=False)
-        for i in range(1, X):
-            column = add(column, to_x(lax.dynamic_index_in_dim(grid, lax.rem(x + i, X), 1, keepdims=False), i))
-        total = at(column, z).astype(F32)
-        for k in range(1, Z):
-            total = total + to_z(at(column, lax.rem(z + k, Z)), k).astype(F32)
-        return total
-
-    def over_fsdp_rows(value):
-        return over_fsdp(value.reshape((fsdp_count, value.shape[0] // fsdp_count) + value.shape[1:]))
-
-    down_half = add(at(down_part, core), to_core(at(down_part, 1 - core)))
-    inner_half = add(at(inner_part, core), to_core(at(inner_part, 1 - core)))
-    down_mine = over_fsdp_rows(down_half).astype(BF)
-    inner_mine = over_fsdp_rows(inner_half).astype(BF)
-
-    parts = jnp.stack(attn_part).reshape(2, 2, 2 * width, width)
-    pair = add(
-        lax.dynamic_index_in_dim(parts, core, 1, keepdims=False),
-        to_core(lax.dynamic_index_in_dim(parts, 1 - core, 1, keepdims=False)),
-    )
-    quarter = add(at(pair, y), to_y(at(pair, 1 - y)))
-    quarter = quarter.reshape(2, fsdp_count, width // fsdp_count, width)
-    attn_mine = jnp.stack(
-        [over_fsdp(quarter[p]) for p in range(2)]
-    ).astype(BF)
-
-    def share_y(value):
-        theirs = to_y(value)
-        mine = jnp.where(y == 0, jnp.stack([value, theirs]), jnp.stack([theirs, value]))
-        return mine
-
-    def share_all(value):
-        pair_y = share_y(value)
-        others = to_core(pair_y)
-        return jnp.where(core == 0, jnp.stack([pair_y, others], 1), jnp.stack([others, pair_y], 1))
-
-    down_all = share_all(down_mine).astype(F32)
-    inner_all = share_all(inner_mine).astype(F32)
-    attn_all = share_all(attn_mine).astype(F32)
-    down_grad = jnp.concatenate([down_all[:, 0], down_all[:, 1]], axis=-1)
-    inner_grad = jnp.concatenate([inner_all[:, 0], inner_all[:, 1]], axis=-1)
-    qkv_grad = jnp.concatenate([attn_all[0, 0], attn_all[0, 1], attn_all[1, 0]], axis=-1)
-    mix_grad = attn_all[1, 1]
+    inner_grad = inner_shares.reshape((2, 2) + inner_shares.shape[1:])
+    inner_grad = jnp.concatenate([inner_grad[:, 0], inner_grad[:, 1]], axis=-1).astype(F32)
+    down_grad = down_shares.reshape((2, 2) + down_shares.shape[1:])
+    down_grad = jnp.concatenate([down_grad[:, 0], down_grad[:, 1]], axis=-1).astype(F32)
+    qkv_grad = jnp.concatenate([attn_shares[0], attn_shares[1], attn_shares[2]], axis=-1).astype(F32)
+    mix_grad = attn_shares[3].astype(F32)
 
     gains_part = jnp.stack([e1, e2])
     gains_part = gains_part + to_core(gains_part)
@@ -534,9 +1015,9 @@
     column = lax.dynamic_index_in_dim(gains_grid, x, 1, keepdims=False)
     for i in range(1, X):
         column = column + to_x(lax.dynamic_index_in_dim(gains_grid, lax.rem(x + i, X), 1, keepdims=False), i)
-    gains_grad = at(column, z)
+    gains_grad = lax.dynamic_index_in_dim(column, z, 0, keepdims=False)
     for kk in range(1, Z):
-        gains_grad = gains_grad + to_z(at(column, lax.rem(z + kk, Z)), kk)
+        gains_grad = gains_grad + to_z(lax.dynamic_index_in_dim(column, lax.rem(z + kk, Z), 0, keepdims=False), kk)
 
     step_size = step_rate / math.sqrt(total_frames)
     grads = (qkv_grad, mix_grad, inner_grad, down_grad, gains_grad)

time: 821 us -> 679 us (0.83)
  waiting for transfers between devices: 237 us -> 23.7 us
  Pallas kernels: 280 us -> 485 us
  matrix products: 72.6 us -> 21.4 us
  local copies, waits for them, and re-layouts: 73.8 us -> 41 us
  starting transfers between devices: 56.3 us -> 25.1 us
  other arithmetic: 94.1 us -> 72.7 us
    ppermute x37 -> x9, waiting for transfers between devices: 237 us -> 23.7 us  [permute(): return lax.ppermute(value, axes, pairs)]
    pallas_call x2, Pallas kernels: 90.2 us -> 295 us  [the longest x1 161 us: attention_back(): pl.pallas_call(functools.partial(attention_back_kernel, X, groups, head_s...]
    dot_general x8 -> x0, matrix products: 51.8 us -> none  [the longest x4 30.3 us: back_each(): return jnp.einsum('pfe,pde->pfd', left, right, preferred_element_type=F32)]
    ppermute x37 -> x9, starting transfers between devices: 56.3 us -> 25.1 us  [permute(): return lax.ppermute(value, axes, pairs)]
    convert_element_type x14 -> x2, other arithmetic: 32.5 us -> 2.85 us  [the longest x1 2.25 us: per_device(): dhb = dh.astype(BF)]
    squeeze x15 -> x3, local copies, waits for them, and re-layouts: 24.4 us -> 7.3 us  [the longest x1 3.71 us: per_device(): inner_grad[:, 0]]
    unnamed x77 -> x65, local copies, waits for them, and re-layouts: 22.3 us -> 14.8 us
  transfers between devices with their start and end apart: 37 -> 9, of which waited for: 16 -> 2; matrix products, arithmetic and copies ran while one was open for 23% -> 12% of each run, Pallas kernels for 4% -> 2%
where the time goes in v2:
time: 679 us; the launch traced here: 670 us
  Pallas kernels  485 us (71%)
  other arithmetic  72.7 us (11%)
  local copies, waits for them, and re-layouts  41 us (6%)
  starting transfers between devices  25.1 us (4%)
  waiting for transfers between devices  23.7 us (3%)
  matrix products  21.4 us (3%)
    pallas_call x1, Pallas kernels, gather_weights(): pl.pallas_call(functools.partial(gather_kernel, X), out_shape=(jax.ShapeD...  179 us
    pallas_call x1, Pallas kernels, attention_back(): pl.pallas_call(functools.partial(attention_back_kernel, X, groups, head_s...  161 us
    pallas_call x1, Pallas kernels, feed_forward(): pl.pallas_call(functools.partial(feed_forward_kernel, X, J), grid=(J + 3,...  134 us
    add x5, other arithmetic, owner_update(): average_new = average_rate * average + (1.0 - average_rate) * weight_new  35.5 us
    ppermute x9, starting transfers between devices, permute(): return lax.ppermute(value, axes, pairs)  25.1 us
    ppermute x9, waiting for transfers between devices, permute(): return lax.ppermute(value, axes, pairs)  23.7 us
    dot_general x4, matrix products, each(): return jnp.einsum('pfd,pde->pfe', left, right, preferred_element_type=F32)  21.4 us
    unnamed x65, local copies, waits for them, and re-layouts  14.8 us
  transfers between devices with their start and end apart: 9, of which 2 were waited for; matrix products, arithmetic and copies ran while one was open for 12% of the time, Pallas kernels for 2%

profile of v2, /device:TPU:0, one launch (start us, length us, event | category | flops | bytes accessed | tf_op | source)
XLA Modules:
  0.0 670.3 jit_solution(4958818061732822516)
XLA Ops:
  6.3 3.0 select_convert_fusion.attn_own
  9.3 179.0 %gather_weights.1 = (bf16[4,2,1024,1024]{3,2,1,0:T(8,128)(2,1)}, bf16[2,1024,2816]{2,1,0:T(8,128)(2,1)}, bf16[2,2816,512]{2,1,0:T(8,128)(2,1)}, f32[8,8,128]{2,1,0:T(8,128)}) custom-call(bf16[2,128,1024]{2,1,0:T(8,128)(2,1)} %select_convert_fusion.attn_own, bf16[128,2816]{1,0:T(8,128)(2,1)} %fusion.33.inner_own, bf16[352,512]{1,0:T(8,128)(2,1)} %fusion.34.down_own, ...), custom_call_target="tpu_custom_call" | custom-call | tf_op jit(solution)/shard_map/gather_weights/pallas_call | solution.py:180
  190.4 5.3 fusion.6
  195.8 4.6 fusion.4
  206.0 3.3 collective-permute-start
  209.4 3.5 copy.60
  212.9 2.8 dynamic-slice_bitcast_fusion.1
  215.7 3.8 collective-permute-start.2
  219.5 5.9 fusion.30.q
  225.6 3.7 copy.58.k
  232.7 10.7 %attend.1.mixed = bf16[2,512,1024]{2,1,0:T(8,128)(2,1)} custom-call(f32[512,1]{1,0:T(8,128)} %copy.57.carried, bf16[2,512,1024]{2,1,0:T(8,128)(2,1)} %fusion.30.q, bf16[2,512,1024]{2,1,0:T(8,128)(2,1)} %copy.58.k, bf16[2,512,1024]{2,1,0:T(8,128)(2,1)} %copy.59.v, f32[8,1024]{1,0:T(8,128)} %pad_convert_fusion.edge), custom_call_target="tpu_custom_call" | custom-call | tf_op jit(solution)/shard_map/attend/pallas_call | solution.py:252
  243.4 5.7 multiply_reduce_fusion.2
  251.4 2.7 pad_maximum_fusion.1.c
  254.1 22.3 %collective-permute-done.1 = bf16[512,1024]{1,0:T(8,128)(2,1)} collective-permute-done((bf16[512,1024]{1,0:T(8,128)(2,1)S(1)}, bf16[512,1024]{1,0:T(8,128)(2,1)}, u32[]{:S(2)}, u32[]{:S(2)}) %collective-permute-start.1) | collective-permute-done | bytes 1048608 | tf_op jit(solution)/shard_map/ppermute | solution.py:923
  276.4 2.7 pad_maximum_fusion.b
  279.1 133.8 %feed_forward.1 = (f32[512,1024]{1,0:T(8,128)}, f32[512,1024]{1,0:T(8,128)}, bf16[512,1024]{1,0:T(8,128)(2,1)}, bf16[512,1024]{1,0:T(8,128)(2,1)}, bf16[4,128,28...) custom-call(bf16[1024,1024]{1,0:T(8,128)(2,1)} %pad_maximum_fusion.b, bf16[1024,1024]{1,0:T(8,128)(2,1)} %pad_maximum_fusion.1.c, ...), custom_call_target="tpu_custom_call" | custom-call | flops 53150220288 | bytes 62914560 | tf_op jit(solution)/shard_map/feed_forward/pallas_call | solution.py:452
  414.8 3.5 multiply_reduce_fusion
  421.6 161.4 %attention_back.1 = (f32[2,512,1024]{2,1,0:T(8,128)}, bf16[4,2,128,1024]{3,2,1,0:T(8,128)(2,1)}, bf16[4,352,512]{2,1,0:T(8,128)(2,1)}, bf16[512,1024]{1,0:T(8,128)(2,1)}) custom-call(f32[512,1]{1,0:T(8,128)} %copy.57.carried, bf16[2,512,1024]{2,1,0:T(8,128)(2,1)} %fusion.30.q, bf16[2,512,1024]{2,1,0:T(8,128)(2,1)} %copy.58.k, bf16[2,512,1024]{2,1,0:T(8,128)(2,1)} %copy.59.v, ...), custom_call_target="tpu_custom_call" | custom-call | tf_op jit(solution)/shard_map/attention_back/pallas_call | solution.py:865
  583.0 4.4 fusion.20
  588.1 2.9 bitcast_convert_fusion
  591.0 2.6 slice_bitcast_fusion.6
  593.6 3.7 slice_bitcast_fusion.1
  598.3 7.6 %fusion.26 = (bf16[512,2,1024]{2,0,1:T(8,128)(2,1)S(1)}, bf16[512,2,1024]{2,0,1:T(8,128)(2,1)}) fusion(f32[2,512,1024]{2,1,0:T(8,128)S(1)} %copy-done.11, f32[2,512]{1,0:T(2,128)} %broadcast_multiply_fusion, f32[1024]{0:T(1024)S(1)} %bitcast.153, f32[2,512]{1,0:T(2,128)S(1)} %add_rsqrt_fusion.1, bf16[512,2,1024]{2,1,0:T(2,128)(2,1)S(1)} %copy-done.4, ...), kind=kLoop, calls=%fused_computation.48 | loop fusion | flops 24117248 | bytes 25190400 | tf_op jit(solution)/shard_map/transpose | solution.py:1002
  606.0 15.6 %add_multiply_fusion = (f32[2,128,5632]{2,1,0:T(8,128)}, f32[2,128,5632]{2,1,0:T(8,128)}, f32[2,128,5632]{2,1,0:T(8,128)}, f32[2,128,5632]{2,1,0:T(8,128)}) fusion(f32[2,128,5632]{2,1,0:T(8,128)} %param.35, f32[2,128,5632]{2,1,0:T(8,128)} %param.25, f32[2,128,5632]{2,1,0:T(8,128)} %param.30, bf16[2,128,2816]{2,1,0:T(8,128)(2,1)} %get-tuple-element.133, ...), kind=kLoop, calls=%fused_computation | loop fusion | flops 17301504 | bytes 43253760 | tf_op jit(solution)/shard_map/add | solution.py:49
  621.7 6.6 add_multiply_fusion.1
  633.5 4.9 collective-permute-start.5
  638.4 9.3 %add_multiply_fusion.2 = (f32[2,352,1024]{2,1,0:T(8,128)}, f32[2,352,1024]{2,1,0:T(8,128)}, f32[2,352,1024]{2,1,0:T(8,128)}, f32[2,352,1024]{2,1,0:T(8,128)}) fusion(f32[2,352,1024]{2,1,0:T(8,128)} %param.36, f32[2,352,1024]{2,1,0:T(8,128)} %param.26, f32[2,352,1024]{2,1,0:T(8,128)} %param.31, bf16[2,352,512]{2,1,0:T(8,128)(2,1)} %get-tuple-element.142, ...), kind=kLoop, calls=%fused_computation.45 | loop fusion | flops 8650752 | bytes 21626880 | tf_op jit(solution)/shard_map/add | solution.py:49
  647.8 3.9 collective-permute-start.8
  651.7 5.3 collective-permute-start.7
  659.0 3.4 add_multiply_fusion.3
  662.3 3.5 copy.71
  665.8 3.5 copy.72
  (108 shorter events, 33.7 us)
Async XLA Ops:
  2.0 187.2 %copy-start.3 = (bf16[512,2,1024]{2,1,0:T(2,128)(2,1)S(1)}, bf16[512,2,1024]{2,1,0:T(2,128)(2,1)}, u32[]{:S(2)}) copy-start(bf16[512,2,1024]{2,1,0:T(2,128)(2,1)} %param.20) | copy-start | bytes 6291460
  190.4 5.3 copy-start.16
  206.0 26.0 %collective-permute-start = (bf16[4,1024]{1,0:T(4,128)(2,1)S(1)}, bf16[4,1024]{1,0:T(4,128)(2,1)S(1)}, u32[]{:S(2)}, u32[]{:S(2)}) collective-permute-start(bf16[4,1024]{1,0:T(4,128)(2,1)S(1)} %pad_maximum_fusion.2), channel_id=1, source_target_pairs={{0,1},{1,2},{2,3},{3,4},{4,5},{5,6},{6,7},{7,8},{8,9},{9,10},{10,1... | collective-permute-start | bytes 24584 | tf_op jit(solution)/shard_map/ppermute | solution.py:923
  212.9 6.6 copy-start.17
  215.7 9.7 %copy-start.26 = (s32[16384]{0:T(1024)S(1)}, s32[16384]{0:T(1024)}, u32[]{:S(2)}) copy-start(s32[16384]{0:T(1024)} %param.22) | copy-start | bytes 196612
  215.7 35.6 %collective-permute-start.2 = (bf16[512,1024]{1,0:T(8,128)(2,1)}, bf16[512,1024]{1,0:T(8,128)(2,1)}, u32[]{:S(2)}, u32[]{:S(2)}) collective-permute-start(bf16[512,1024]{1,0:T(8,128)(2,1)} %get-tuple-element.138), channel_id=1, source_target_pairs={{0,16},{1,17},{2,18},{3,19},{4,20},{5,21},{6,22},{7,23},{8,24},{9,... | collective-permute-start | bytes 3145736 | tf_op jit(solution)/shard_map/ppermute | solution.py:923
  225.4 3.8 copy-start.14
  251.2 25.2 %collective-permute-start.1 = (bf16[512,1024]{1,0:T(8,128)(2,1)S(1)}, bf16[512,1024]{1,0:T(8,128)(2,1)}, u32[]{:S(2)}, u32[]{:S(2)}) collective-permute-start(bf16[512,1024]{1,0:T(8,128)(2,1)S(1)} %get-tuple-element.140), channel_id=1, source_target_pairs={{0,16},{1,17},{2,18},{3,19},{4,20},{5,21},{6,22},{7,23},{8,24},{9,... | collective-permute-start | bytes 3145736 | tf_op jit(solution)/shard_map/ppermute | solution.py:923
  414.5 3.8 copy-start.5
  414.8 3.9 copy-start.1
  414.8 4.6 copy-start.7
  583.0 15.3 %copy-start.10 = (f32[512,1024]{1,0:T(8,128)S(1)}, f32[512,1024]{1,0:T(8,128)}, u32[]{:S(2)}) copy-start(f32[512,1024]{1,0:T(8,128)} %get-tuple-element.53) | copy-start | bytes 6291460
  583.0 15.3 %copy-start.11 = (f32[2,512,1024]{2,1,0:T(8,128)S(1)}, f32[2,512,1024]{2,1,0:T(8,128)}, u32[]{:S(2)}) copy-start(f32[2,512,1024]{2,1,0:T(8,128)} %get-tuple-element.58) | copy-start | bytes 12582916
  588.1 10.2 %copy-start.8 = (bf16[512,2,1024]{2,1,0:T(2,128)(2,1)S(1)}, bf16[512,2,1024]{2,1,0:T(2,128)(2,1)}, u32[]{:S(2)}) copy-start(bf16[512,2,1024]{2,1,0:T(2,128)(2,1)} %param.21) | copy-start | bytes 6291460
  591.0 7.3 %copy-start.4 = (bf16[512,2,1024]{2,1,0:T(2,128)(2,1)S(1)}, bf16[512,2,1024]{2,1,0:T(2,128)(2,1)}, u32[]{:S(2)}) copy-start(bf16[512,2,1024]{2,1,0:T(2,128)(2,1)} %param.20) | copy-start | bytes 6291460
  591.0 7.3 %copy-start.6 = (f32[1,512,1024]{2,1,0:T(8,128)S(1)}, f32[1,512,1024]{2,1,0:T(8,128)}, u32[]{:S(2)}) copy-start(f32[1,512,1024]{2,1,0:T(8,128)} %copy-done.5) | copy-start | bytes 6291460
  593.6 4.7 copy-start.2
  597.9 30.4 %collective-permute-start.3 = (f32[2,1024]{1,0:T(2,128)}, f32[2,1024]{1,0:T(2,128)}, u32[]{:S(2)}, u32[]{:S(2)}) collective-permute-start(f32[2,1024]{1,0:T(2,128)} %pad_maximum_fusion.3), channel_id=1, source_target_pairs={{0,8},{1,9},{2,10},{3,11},{4,12},{5,13},{6,14},{7,15},{8,0},{9,1},... | collective-permute-start | bytes 24584 | tf_op jit(solution)/shard_map/ppermute | solution.py:923
  606.0 15.7 %copy-start.18 = (f32[2,128,3072]{2,1,0:T(8,128)S(1)}, f32[2,128,3072]{2,1,0:T(8,128)}, u32[]{:S(2)}) copy-start(f32[2,128,3072]{2,1,0:T(8,128)} %param.23) | copy-start | bytes 9437188
  606.0 15.7 %copy-start.20 = (f32[2,128,3072]{2,1,0:T(8,128)S(1)}, f32[2,128,3072]{2,1,0:T(8,128)}, u32[]{:S(2)}) copy-start(f32[2,128,3072]{2,1,0:T(8,128)} %param.33) | copy-start | bytes 9437188
  606.0 15.7 %copy-start.21 = (bf16[2,128,1024]{2,1,0:T(8,128)(2,1)S(1)}, bf16[2,128,1024]{2,1,0:T(8,128)(2,1)}, u32[]{:S(2)}) copy-start(bf16[2,128,1024]{2,1,0:T(8,128)(2,1)} %get-tuple-element.135) | copy-start | bytes 1572868
  606.0 15.7 %copy-start.22 = (bf16[2,128,1024]{2,1,0:T(8,128)(2,1)S(1)}, bf16[2,128,1024]{2,1,0:T(8,128)(2,1)}, u32[]{:S(2)}) copy-start(bf16[2,128,1024]{2,1,0:T(8,128)(2,1)} %get-tuple-element.136) | copy-start | bytes 1572868
  621.7 8.7 %copy-start.23 = (bf16[4,352,512]{2,1,0:T(8,128)(2,1)S(1)}, bf16[4,352,512]{2,1,0:T(8,128)(2,1)}, u32[]{:S(2)}) copy-start(bf16[4,352,512]{2,1,0:T(8,128)(2,1)} %get-tuple-element.61) | copy-start | bytes 4325380
  629.0 3.7 collective-permute-start.4
  633.5 14.2 %collective-permute-start.5 = (f32[4,2,128]{2,0,1:T(4,128)S(1)}, f32[4,2,128]{2,0,1:T(4,128)S(1)}, u32[]{:S(2)}, u32[]{:S(2)}) collective-permute-start(f32[4,2,128]{2,0,1:T(4,128)S(1)} %bitcast.156), channel_id=1, source_target_pairs={{0,1},{1,0},{2,3},{3,2},{4,5},{5,4},{6,7},{7,6},{8,9},{9,8},{10,11... | collective-permute-start | bytes 12296 | tf_op jit(solution)/shard_map/ppermute | solution.py:923
  638.4 20.5 %copy-start.19 = (f32[2,128,1024]{2,1,0:T(8,128)S(1)}, f32[2,128,1024]{2,1,0:T(8,128)}, u32[]{:S(2)}) copy-start(f32[2,128,1024]{2,1,0:T(8,128)} %param.24) | copy-start | bytes 3145732
  638.4 20.5 %copy-start.24 = (f32[2,128,1024]{2,1,0:T(8,128)S(1)}, f32[2,128,1024]{2,1,0:T(8,128)}, u32[]{:S(2)}) copy-start(f32[2,128,1024]{2,1,0:T(8,128)} %param.34) | copy-start | bytes 3145732
  638.4 20.5 %copy-start.25 = (f32[2,128,1024]{2,1,0:T(8,128)S(1)}, f32[2,128,1024]{2,1,0:T(8,128)}, u32[]{:S(2)}) copy-start(f32[2,128,1024]{2,1,0:T(8,128)} %param.29) | copy-start | bytes 3145732
  647.8 21.5 %collective-permute-start.8 = (f32[2,128]{1,0:T(2,128)S(1)}, f32[2,128]{1,0:T(2,128)S(1)}, u32[]{:S(2)}, u32[]{:S(2)}) collective-permute-start(f32[2,128]{1,0:T(2,128)S(1)} %bitcast.160), channel_id=1, source_target_pairs={{0,6},{1,7},{2,0},{3,1},{4,2},{5,3},{6,4},{7,5},{8,14},{9,15},{10,... | collective-permute-start | bytes 3080 | tf_op jit(solution)/shard_map/ppermute | solution.py:923
  651.7 17.6 %collective-permute-start.7 = (f32[2,128]{1,0:T(2,128)S(1)}, f32[2,128]{1,0:T(2,128)S(1)}, u32[]{:S(2)}, u32[]{:S(2)}) collective-permute-start(f32[2,128]{1,0:T(2,128)S(1)} %bitcast.159), channel_id=1, source_target_pairs={{0,4},{1,5},{2,6},{3,7},{4,0},{5,1},{6,2},{7,3},{8,12},{9,13},{10,... | collective-permute-start | bytes 3080 | tf_op jit(solution)/shard_map/ppermute | solution.py:923
  657.0 5.3 copy-start.15
  657.0 12.3 %collective-permute-start.6 = (f32[2,128]{1,0:T(2,128)S(1)}, f32[2,128]{1,0:T(2,128)S(1)}, u32[]{:S(2)}, u32[]{:S(2)}) collective-permute-start(f32[2,128]{1,0:T(2,128)S(1)} %bitcast.158), channel_id=1, source_target_pairs={{0,2},{1,3},{2,4},{3,5},{4,6},{5,7},{6,0},{7,1},{8,10},{9,11},{10,... | collective-permute-start | bytes 3080 | tf_op jit(solution)/shard_map/ppermute | solution.py:923
  (8 other events, 20.2 us)

commit v3 on v2

--- a/solution.py
+++ b/solution.py
@@ -35,7 +35,9 @@
 
 
 def scale_rows(values):
-    return lax.rsqrt(jnp.mean(values * values, axis=-1, keepdims=True) + norm_eps)
+    square = jnp.mean(values * values, axis=-1, keepdims=True) + norm_eps
+    inverse = lax.rsqrt(square)
+    return inverse * (1.5 - 0.5 * square * inverse * inverse)
 
 
 def norm_back(grad_in, normed, gain_row, inverse):
@@ -50,150 +52,20 @@
     return (moment_new, average_new, weight_new)
 
 
-def gather_kernel(
-    inner_peers, attn_own, inner_own, down_own, gains_own, attn, inner, down, gains,
-    local_sem, send_z, recv_z, send_x, recv_x, send_c, recv_c, send_y, recv_y, send_r, recv_r,
-):
-    X = inner_peers
-    dp = lax.axis_index("dp")
-    fs = lax.axis_index("fsdp")
-    y, core = dp // 2, dp % 2
-    z, x = fs // X, fs % X
-    other_core = (y * 2 + 1 - core, fs)
-    other_y = ((1 - y) * 2 + core, fs)
-
-    def z_peer(k):
-        return (dp, lax.rem(z + k, Z) * X + x)
-
-    def x_peer(i):
-        return (dp, z * X + lax.rem(x + i, X))
-
-    owns = (attn_own, inner_own, down_own, gains_own)
-    rows = [o.shape[-2] for o in owns]
-
-    def place(array, source, part=None):
-        if array == 0:
-            return attn.at[dp if part is None else part, :, pl.ds(source * rows[0], rows[0]), :]
-        if array == 1:
-            return inner.at[core, pl.ds(source * rows[1], rows[1]), :]
-        if array == 2:
-            return down.at[core, pl.ds(source * rows[2], rows[2]), :]
-        return gains.at[source]
-
-    barrier = pltpu.get_barrier_semaphore()
-    peers = [z_peer(k) for k in range(1, Z)] + [x_peer(i) for i in range(1, X)]
-    peers += [other_core, other_y]
-    for peer in peers:
-        pl.semaphore_signal(barrier, inc=1, device_id=peer, device_id_type=MESH)
-    pl.semaphore_wait(barrier, len(peers))
-
-    started = []
-
-    def remote(src, dst, ss, rs, peer):
-        copy = pltpu.make_async_remote_copy(
-            src_ref=src, dst_ref=dst, send_sem=ss, recv_sem=rs, device_id=peer, device_id_type=MESH
-        )
-        copy.start()
-        started.append(copy)
-        return copy
-
-    local = []
-    for n, own in enumerate(owns):
-        copy = pltpu.make_async_copy(own, place(n, fs), local_sem.at[n])
-        copy.start()
-        local.append(copy)
-
-    def chunk_source(k, i):
-        return lax.rem(z - k + Z, Z) * X + lax.rem(x - i + X, X)
-
-    def start_array(n):
-        for k in range(1, Z):
-            remote(owns[n], place(n, fs), send_z.at[n, k], recv_z.at[n, k], z_peer(k))
-        for i in range(1, X):
-            remote(owns[n], place(n, fs), send_x.at[n, 0, i], recv_x.at[n, 0, i], x_peer(i))
-
-    def share(n, k, i):
-        if n == 3:
-            return
-        source = chunk_source(k, i)
-        src = owns[n] if (k == 0 and i == 0) else place(n, source)
-        if n == 0:
-            remote(src, place(0, source), send_y.at[k, i], recv_y.at[k, i], other_y)
-        remote(src, place(n, source), send_c.at[n, k, i], recv_c.at[n, k, i], other_core)
-
-    def wait_recv(dst, rs, ss):
-        pltpu.make_async_remote_copy(
-            src_ref=dst, dst_ref=dst, send_sem=ss, recv_sem=rs, device_id=other_core, device_id_type=MESH
-        ).wait_recv()
-
-    def pass_on(n):
-        share(n, 0, 0)
-        for i in range(1, X):
-            wait_recv(place(n, chunk_source(0, i)), recv_x.at[n, 0, i], send_x.at[n, 0, i])
-            share(n, 0, i)
-        for k in range(1, Z):
-            source = chunk_source(k, 0)
-            wait_recv(place(n, source), recv_z.at[n, k], send_z.at[n, k])
-            for i in range(1, X):
-                remote(place(n, source), place(n, source), send_x.at[n, k, i], recv_x.at[n, k, i], x_peer(i))
-            share(n, k, 0)
-        for k in range(1, Z):
-            for i in range(1, X):
-                wait_recv(place(n, chunk_source(k, i)), recv_x.at[n, k, i], send_x.at[n, k, i])
-                share(n, k, i)
-
-    start_array(3)
-    start_array(0)
-    start_array(1)
-    start_array(2)
-    pass_on(0)
-    pass_on(3)
-    pass_on(1)
-    pass_on(2)
-    part = (1 - y) * 2 + core
-    for k in range(Z):
-        for i in range(X):
-            source = chunk_source(k, i)
-            wait_recv(place(0, source, part), recv_y.at[k, i], send_y.at[k, i])
-            remote(place(0, source, part), place(0, source, part), send_r.at[k, i], recv_r.at[k, i], other_core)
-    for k in range(Z):
-        for i in range(X):
-            source = chunk_source(k, i)
-            wait_recv(place(0, source, (1 - y) * 2 + 1 - core), recv_r.at[k, i], send_r.at[k, i])
-            for n in range(3):
-                half = y * 2 + 1 - core if n == 0 else None
-                dst = place(0, source, half) if n == 0 else (
-                    inner.at[1 - core, pl.ds(source * rows[1], rows[1]), :] if n == 1
-                    else down.at[1 - core, pl.ds(source * rows[2], rows[2]), :]
-                )
-                wait_recv(dst, recv_c.at[n, k, i], send_c.at[n, k, i])
-    for copy in started:
-        copy.wait_send()
-    for copy in local:
-        copy.wait()
-
-
-def gather_weights(attn_own, inner_own, down_own, gains_own, fsdp_count):
-    X = fsdp_count // Z
-    _, rows, width = attn_own.shape
-    dma = pltpu.SemaphoreType.DMA
-    return pl.pallas_call(
-        functools.partial(gather_kernel, X),
-        out_shape=(
-            jax.ShapeDtypeStruct((4, 2, rows * fsdp_count, width), BF),
-            jax.ShapeDtypeStruct((2, inner_own.shape[0] * fsdp_count, inner_own.shape[1]), BF),
-            jax.ShapeDtypeStruct((2, down_own.shape[0] * fsdp_count, down_own.shape[1]), BF),
-            jax.ShapeDtypeStruct((fsdp_count,) + gains_own.shape, F32),
-        ),
-        in_specs=[ANY] * 4,
-        out_specs=(ANY,) * 4,
-        scratch_shapes=[
-            dma((4,)), dma((4, Z)), dma((4, Z)), dma((4, Z, X)), dma((4, Z, X)),
-            dma((3, Z, X)), dma((3, Z, X)), dma((Z, X)), dma((Z, X)), dma((Z, X)), dma((Z, X)),
-        ],
-        compiler_params=pltpu.CompilerParams(collective_id=0, has_side_effects=True),
-        name="gather_weights",
-    )(attn_own, inner_own, down_own, gains_own)
+PAIRS = ((0, 0), (0, 1), (0, 2), (1, 0), (1, 1), (1, 2), (1, 3))
+SPANS = ((0, range(0, 3)), (1, range(3, 7)))
+CHUNK = 128
+STEP = 256
+
+
+def total_of(values):
+    return functools.reduce(jnp.add, values)
+
+
+def remote_copy(src, dst, send_sem, recv_sem, peer):
+    return pltpu.make_async_remote_copy(
+        src_ref=src, dst_ref=dst, send_sem=send_sem, recv_sem=recv_sem, device_id=peer, device_id_type=MESH
+    )
 
 
 def head_ones(lanes, head_size):
@@ -202,68 +74,414 @@
     return (row == column).astype(BF)
 
 
-KEYS = ((0, 1, 2), (0, 1, 2, 3))
-
-
-def load_heads(q, k, v, edge):
-    frames = q.shape[1]
-    first = lax.broadcasted_iota(jnp.int32, (frames, q.shape[2]), 0) == 0
-    queries = [q[p].astype(F32) for p in range(2)]
-    here_k = [k[p].astype(F32) for p in range(2)]
-    here_v = [v[p].astype(F32) for p in range(2)]
-    before_k = [jnp.where(first, edge[p : p + 1, :], pltpu.roll(here_k[p], 1, 0)) for p in range(2)]
-    before_v = [jnp.where(first, edge[2 + p : 3 + p, :], pltpu.roll(here_v[p], 1, 0)) for p in range(2)]
-    return queries, before_k + here_k, before_v + here_v
-
-
-def head_probs(queries, keys, p, allowed, ones, root_size):
-    scores = []
-    for n in KEYS[p]:
-        s = nn((queries[p] * keys[n]).astype(BF), ones) * (1.0 / root_size)
-        scores.append(jnp.where(allowed, s, -1e30) if n < 2 else s)
-    top = functools.reduce(jnp.maximum, scores)
-    exps = [jnp.exp(s - top) for s in scores]
-    exps = [jnp.where(allowed, e, 0.0) if n < 2 else e for n, e in zip(KEYS[p], exps)]
-    inverse = 1.0 / functools.reduce(jnp.add, exps)
-    return [e * inverse for e in exps]
-
-
-def attend_kernel(head_size, carried, q, k, v, edge, out):
-    ones = head_ones(q.shape[2], head_size)
-    allowed = jnp.broadcast_to(carried[...], q.shape[1:]) > 0.5
-    queries, keys, values = load_heads(q, k, v, edge)
-    for p in range(2):
-        probs = head_probs(queries, keys, p, allowed, ones, math.sqrt(head_size))
-        mixed = [pr.astype(BF).astype(F32) * values[n] for n, pr in zip(KEYS[p], probs)]
-        out[p] = functools.reduce(jnp.add, mixed).astype(BF)
-
-
-def attention_specs(frames, width, lanes):
-    rows = pl.BlockSpec((2, frames, lanes), lambda j: (0, 0, j))
-    edge = pl.BlockSpec((8, lanes), lambda j: (0, j))
-    mask = pl.BlockSpec((frames, 1), lambda j: (0, 0))
-    return rows, edge, mask
-
-
-def attend(carried, q, k, v, edge, head_size):
-    _, frames, width = q.shape
-    lanes = 256
-    rows, edge_spec, mask = attention_specs(frames, width, lanes)
+def per_head(left, right, ones):
+    rows = left[0].shape[0]
+    products = [(left[p] * right[n]).astype(BF) for p, n in PAIRS]
+    sums = nn(jnp.concatenate(products, axis=0), ones)
+    return [sums[m * rows : (m + 1) * rows] for m in range(len(PAIRS))]
+
+
+def head_probs(scores, span, allowed, scale):
+    s = [jnp.where(allowed, scores[m] * scale, -1e30) if PAIRS[m][1] < 2 else scores[m] * scale for m in span]
+    top = functools.reduce(jnp.maximum, s)
+    e = [jnp.exp(value - top) for value in s]
+    e = [jnp.where(allowed, value, 0.0) if PAIRS[m][1] < 2 else value for m, value in zip(span, e)]
+    inverse = 1.0 / total_of(e)
+    return [value * inverse for value in e]
+
+
+def forward_kernel(
+    X, groups, head_size, frames, carried, cot, attn_own, inner_own, down_own, gains_own,
+    attn, inner, down, gains_out, inputs_out, rows_out, mixed_out, edge_out, hres_out, b_rows, c_rows,
+    gains, inputs, rows_in, mixed, before, hres, b, proj, mix, edge_send, edge_recv,
+    send_up, recv_up, send_down, recv_down, send_x, recv_x, send_y, recv_y, send_c, recv_c, send_r, recv_r,
+    send_g, recv_g, send_e, recv_e, send_b, recv_b, send_q, recv_q, local_sem, out_sem,
+):
+    dp, fs = lax.axis_index("dp"), lax.axis_index("fsdp")
+    F = Z * X
+    y, core = dp // 2, dp % 2
+    z, x = fs // X, fs % X
+    me = dp * F + fs
+    devices = 4 * F
+    count = frames.shape[1]
+    core_peer = (y * 2 + 1 - core, fs)
+    y_peer = ((1 - y) * 2 + core, fs)
+    up_peer = (dp, lax.rem(z + 1, Z) * X + x)
+    down_peer = (dp, lax.rem(z + Z - 1, Z) * X + x)
+    before_me = ((me - 1 + devices) % devices // F, (me - 1 + devices) % devices % F)
+    after_me = ((me + 1) % devices // F, (me + 1) % devices % F)
+
+    def z_peer(k):
+        return (dp, lax.rem(z + k, Z) * X + x)
+
+    def x_peer(i):
+        return (dp, z * X + lax.rem(x + i, X))
+
+    UNITS = unit_list(groups, inner_own.shape[1], down_own.shape[1])
+
+    def own(u):
+        kind, n, columns = UNITS[u]
+        if kind in ("quarter", "low", "high"):
+            return attn_own.at[n if kind != "high" else n + 1]
+        return (down_own if kind == "down" else inner_own).at[:, columns]
+
+    def part_of(u, core_index, plane):
+        kind = UNITS[u][0]
+        if kind == "quarter":
+            return plane * 2 + core_index
+        return 2 + core_index if kind == "high" else core_index
+
+    def whole(u, part):
+        kind, n, columns = UNITS[u]
+        if kind == "down":
+            return down.at[part, :, columns]
+        if kind == "inner":
+            return inner.at[part, :, columns]
+        return attn.at[n, part]
+
+    def place(u, source, part=None):
+        kind, n, columns = UNITS[u]
+        part = part_of(u, core, y) if part is None else part
+        if kind == "down":
+            R = down_own.shape[0]
+            return down.at[part, pl.ds(source * R, R), columns]
+        if kind == "inner":
+            R = inner_own.shape[0]
+            return inner.at[part, pl.ds(source * R, R), columns]
+        R = attn_own.shape[2]
+        return attn.at[n, part, :, pl.ds(source * R, R), :]
+
+    barrier = pltpu.get_barrier_semaphore()
+    peers = [z_peer(k) for k in range(1, Z)] + [x_peer(i) for i in range(1, X)]
+    peers += [core_peer, y_peer, before_me, after_me]
+    for peer in peers:
+        pl.semaphore_signal(barrier, inc=1, device_id=peer, device_id_type=MESH)
+    pl.semaphore_wait(barrier, len(peers))
+
+    sent, local = [], []
+
+    def send(condition, make):
+        remote_copy(*make()).start()
+        sent.append((condition, make))
+
+    def wait_send(condition, make):
+        def action():
+            remote_copy(*make()).wait_send()
+
+        if condition is None:
+            action()
+        else:
+            pl.when(condition())(action)
+
+    def wait_recv(dst, recv_sem, send_sem):
+        remote_copy(dst, dst, send_sem, recv_sem, core_peer).wait_recv()
+
+    def store(src, dst):
+        copy = pltpu.make_async_copy(src, dst, out_sem.at[len(local)])
+        copy.start()
+        local.append(copy)
+
+    def spread(u, row, mine, condition):
+        def src():
+            return own(u) if mine else place(u, row() * X + x)
+
+        for i in range(1, X):
+            send(
+                condition,
+                lambda i=i: (
+                    src(), place(u, row() * X + x), send_x.at[u, row(), i], recv_x.at[u, row(), i], x_peer(i)
+                ),
+            )
+        to_plane(u, lambda: row() * X + x, src, condition)
+
+    def to_plane(u, source, src, condition):
+        if UNITS[u][0] == "quarter":
+            send(
+                condition,
+                lambda: (src(), place(u, source()), send_y.at[u, source()], recv_y.at[u, source()], y_peer),
+            )
+
+    def start_unit(u):
+        def below_top():
+            return z < Z - 1
+
+        def above_bottom():
+            return z > 0
+
+        def upward():
+            return (own(u), place(u, fs), send_up.at[u, 1], recv_up.at[u, 1], up_peer)
+
+        def downward():
+            return (own(u), place(u, fs), send_down.at[u, 1], recv_down.at[u, 1], down_peer)
+
+        pl.when(below_top())(lambda: send(below_top, upward))
+        pl.when(above_bottom())(lambda: send(above_bottom, downward))
+        spread(u, lambda: z, True, None)
+        store(own(u), place(u, fs))
+
+    def hop(u, k):
+        def side(reached, row, further, send_sem, recv_sem, peer):
+            def here():
+                return place(u, row() * X + x)
+
+            def both():
+                return reached() & further()
+
+            def action():
+                wait_recv(here(), recv_sem.at[u, k], send_sem.at[u, k])
+                if k < Z - 1:
+                    pl.when(further())(
+                        lambda: send(
+                            both, lambda: (here(), here(), send_sem.at[u, k + 1], recv_sem.at[u, k + 1], peer)
+                        )
+                    )
+                spread(u, row, False, reached)
+
+            pl.when(reached())(action)
+
+        side(lambda: z >= k, lambda: z - k, lambda: z < Z - 1, send_up, recv_up, up_peer)
+        side(lambda: z + k < Z, lambda: z + k, lambda: z > 0, send_down, recv_down, down_peer)
+
+    def arrivals(u):
+        for row in range(Z):
+            for i in range(1, X):
+                column = lax.rem(x - i + X, X)
+                source = row * X + column
+                wait_recv(place(u, source), recv_x.at[u, row, i], send_x.at[u, row, i])
+                to_plane(u, lambda source=source: source, lambda source=source: place(u, source), None)
+        local[own_store[u]].wait()
+        mine = whole(u, part_of(u, core, y))
+        send(None, lambda: (mine, mine, send_c.at[u], recv_c.at[u], core_peer))
+
+    def relay(u):
+        if UNITS[u][0] != "quarter":
+            return
+        part = (1 - y) * 2 + core
+        for source in range(F):
+            wait_recv(place(u, source, part), recv_y.at[u, source], send_y.at[u, source])
+        theirs = whole(u, part)
+        send(None, lambda: (theirs, theirs, send_r.at[u], recv_r.at[u], core_peer))
+
+    def complete(u):
+        wait_recv(whole(u, part_of(u, 1 - core, y)), recv_c.at[u], send_c.at[u])
+        if UNITS[u][0] == "quarter":
+            wait_recv(whole(u, (1 - y) * 2 + 1 - core), recv_r.at[u], send_r.at[u])
+
+    scale = 1.0 / math.sqrt(head_size)
+
+    def gather_gains():
+        keep = pltpu.make_async_copy(gains_own, gains.at[fs], local_sem.at[0])
+        keep.start()
+        for k in range(1, Z):
+            send(None, lambda k=k: (gains_own, gains.at[fs], send_g.at[0, k], recv_g.at[0, k], z_peer(k)))
+        for i in range(1, X):
+            send(None, lambda i=i: (gains_own, gains.at[fs], send_g.at[i, 0], recv_g.at[i, 0], x_peer(i)))
+        keep.wait()
+
+    def chunk_source(k, i):
+        return lax.rem(z - k + Z, Z) * X + lax.rem(x - i + X, X)
+
+    def pass_gains():
+        for k in range(1, Z):
+            here = gains.at[chunk_source(k, 0)]
+            wait_recv(here, recv_g.at[0, k], send_g.at[0, k])
+            for i in range(1, X):
+                send(
+                    None,
+                    lambda here=here, i=i, k=k: (here, here, send_g.at[i, k], recv_g.at[i, k], x_peer(i)),
+                )
+
+    def take_gains():
+        for k in range(Z):
+            for i in range(1, X):
+                wait_recv(gains.at[chunk_source(k, i)], recv_g.at[i, k], send_g.at[i, k])
+        total = gains[0]
+        for source in range(1, F):
+            total = total + gains[source]
+        gains_out[...] = total
+
+    def norm_rows():
+        def chunk(c, carry):
+            rows = pl.ds(pl.multiple_of(c * CHUNK, CHUNK), CHUNK)
+            for p in range(2):
+                value = frames[p, rows, :].astype(F32)
+                inputs[p, rows, :] = (value * scale_rows(value) * gains_out[0:1, :]).astype(BF)
+            return carry
+
+        lax.fori_loop(0, count // CHUNK, chunk, 0)
+        store(inputs, inputs_out)
+
+    def heads(m):
+        columns = slice(m * STEP, (m + 1) * STEP)
+        load = pltpu.make_async_copy(attn.at[m, pl.ds(0, 3)], proj, local_sem.at[0])
+        load.start()
+        load.wait()
+        for t in (1, 2, 0):
+            for p in range(2):
+                rows_in[t, p, :, columns] = nn(inputs[p], proj[t, p]).astype(BF)
+                if t > 0:
+                    tail = rows_in[t, p, count - 16 :, columns].astype(F32)
+                    row = 2 * (t - 1) + p
+                    edge_send[m, row : row + 1, :] = tail[15:16, :]
+            if t == 2:
+                to_after = remote_copy(edge_send.at[m], edge_recv.at[m], send_e.at[m], recv_e.at[m], after_me)
+                pl.when(me < devices - 1)(to_after.start)
+        pl.when(me > 0)(to_after.wait_recv)
+        first = lax.broadcasted_iota(jnp.int32, (count, STEP), 0) == 0
+        for t in range(2):
+            for p in range(2):
+                n = 2 * t + p
+                shifted = pltpu.roll(rows_in[1 + t, p, :, columns].astype(F32), 1, 0)
+                before[n] = jnp.where(first, edge_recv[m, n : n + 1, :], shifted)
+        ones = head_ones(STEP, head_size)
+
+        def chunk(c, carry):
+            rows = pl.ds(pl.multiple_of(c * CHUNK, CHUNK), CHUNK)
+            allowed = jnp.broadcast_to(carried[rows, :], (CHUNK, STEP)) > 0.5
+            queries, here_k, here_v = (
+                [rows_in[t, p, rows, columns].astype(F32) for p in range(2)] for t in range(3)
+            )
+            keys = [before[p, rows, :] for p in range(2)] + here_k
+            values = [before[2 + p, rows, :] for p in range(2)] + here_v
+            scores = per_head(queries, keys, ones)
+            for p, span in SPANS:
+                probs = head_probs(scores, span, allowed, scale)
+                terms = [pr.astype(BF).astype(F32) * values[PAIRS[n][1]] for n, pr in zip(span, probs)]
+                mixed[p, rows, columns] = total_of(terms).astype(BF)
+            return carry
+
+        lax.fori_loop(0, count // CHUNK, chunk, 0)
+
+    def load_mix():
+        return pltpu.make_async_copy(attn.at[:, 3], mix, local_sem.at[1])
+
+    def finish_rows():
+        load_mix().wait()
+        for turn in range(2):
+            p = 1 - y if turn == 0 else y
+            for m in range(groups):
+                columns = slice(m * STEP, (m + 1) * STEP)
+                hres[p, :, columns] = frames[p, :, columns].astype(F32) + nn(mixed[p], mix[m, p])
+
+            def chunk(c, carry):
+                rows = pl.ds(pl.multiple_of(c * CHUNK, CHUNK), CHUNK)
+                value = hres[p, rows, :]
+                b[turn, rows, :] = (value * scale_rows(value) * gains_out[1:2, :]).astype(BF)
+                return carry
+
+            lax.fori_loop(0, count // CHUNK, chunk, 0)
+            if turn == 0:
+                send(None, lambda: (b.at[0], b_rows.at[1], send_b, recv_b, y_peer))
+            else:
+                store(b.at[1], b_rows.at[0])
+        store(hres, hres_out)
+
+    @pl.when(me == 0)
+    def _():
+        edge_recv[...] = jnp.zeros_like(edge_recv)
+
+    own_store = {}
+    last_of = {kind_n[1]: u for u, kind_n in enumerate(UNITS) if kind_n[0] in ("quarter", "low", "high")}
+    last_plane = max(u for u, kind_n in enumerate(UNITS) if kind_n[0] == "quarter")
+    store(cot.at[y], c_rows.at[0])
+    gather_gains()
+    for tick in range(len(UNITS) + Z + 2):
+        if tick < len(UNITS):
+            own_store[tick] = len(local)
+            start_unit(tick)
+        for k in range(1, Z):
+            if 0 <= tick - k < len(UNITS):
+                hop(tick - k, k)
+        if tick == 1:
+            pass_gains()
+        if tick == 2:
+            take_gains()
+            norm_rows()
+        u = tick - Z
+        if 0 <= u < len(UNITS):
+            arrivals(u)
+            if u == last_plane:
+                send(None, lambda: (cot.at[1 - y], c_rows.at[1], send_q, recv_q, y_peer))
+        u = tick - Z - 1
+        if 0 <= u < len(UNITS):
+            relay(u)
+            complete(u)
+            for m in range(groups):
+                if last_of[m] == u:
+                    if m == groups - 1:
+                        load_mix().start()
+                    heads(m)
+                    if m == groups - 1:
+                        store(rows_in, rows_out)
+                        store(mixed, mixed_out)
+                        store(edge_recv, edge_out)
+                        finish_rows()
+    wait_recv(b_rows.at[1], recv_b, send_b)
+    wait_recv(c_rows.at[1], recv_q, send_q)
+    for condition, make in sent:
+        wait_send(condition, make)
+    for n, copy in enumerate(local):
+        if n not in own_store.values():
+            copy.wait()
+
+    @pl.when(me < devices - 1)
+    def _():
+        for m in range(groups):
+            remote_copy(edge_send.at[m], edge_recv.at[m], send_e.at[m], recv_e.at[m], after_me).wait_send()
+
+
+def unit_list(groups, inner_width, down_width):
+    units = [("quarter", n, None) for n in range(groups - 1)]
+    units += [("low", groups - 1, None), ("high", groups - 1, None)]
+    units += [("down", 0, slice(0, down_width // 2)), ("down", 0, slice(down_width // 2, down_width))]
+    tiles = inner_width // 128
+    cuts = [128 * (tiles * n // 4) for n in range(5)]
+    return units + [("inner", 0, slice(lo, hi)) for lo, hi in zip(cuts, cuts[1:])]
+
+
+def forward(frames, carried, cot, attn_own, inner_own, down_own, gains_own, head_size, fsdp_count):
+    X = fsdp_count // Z
+    _, count, width = frames.shape
+    _, _, R, _ = attn_own.shape
+    groups = width // STEP
+    units = len(unit_list(groups, inner_own.shape[1], down_own.shape[1]))
+    dma, vmem = pltpu.SemaphoreType.DMA, pltpu.VMEM
+    whole = pl.BlockSpec(memory_space=pltpu.VMEM)
+    act = jax.ShapeDtypeStruct((2, count, width), BF)
     return pl.pallas_call(
-        functools.partial(attend_kernel, head_size),
-        grid=(width // lanes,),
-        out_shape=jax.ShapeDtypeStruct(q.shape, BF),
-        in_specs=[mask, rows, rows, rows, edge_spec],
-        out_specs=rows,
-        compiler_params=pltpu.CompilerParams(vmem_limit_bytes=VMEM_BYTES),
-        name="attend",
-    )(carried, q, k, v, edge)
-
-
-def remote_copy(src, dst, send_sem, recv_sem, peer):
-    return pltpu.make_async_remote_copy(
-        src_ref=src, dst_ref=dst, send_sem=send_sem, recv_sem=recv_sem, device_id=peer, device_id_type=MESH
-    )
+        functools.partial(forward_kernel, X, groups, head_size),
+        out_shape=(
+            jax.ShapeDtypeStruct((groups, 4, 2, R * fsdp_count, STEP), BF),
+            jax.ShapeDtypeStruct((2, inner_own.shape[0] * fsdp_count, inner_own.shape[1]), BF),
+            jax.ShapeDtypeStruct((2, down_own.shape[0] * fsdp_count, down_own.shape[1]), BF),
+            jax.ShapeDtypeStruct(gains_own.shape, F32),
+            act,
+            jax.ShapeDtypeStruct((3, 2, count, width), BF),
+            act,
+            jax.ShapeDtypeStruct((groups, 8, STEP), F32),
+            jax.ShapeDtypeStruct((2, count, width), F32),
+            act,
+            act,
+        ),
+        in_specs=[whole] * 7,
+        out_specs=(ANY,) * 3 + (whole,) + (ANY,) * 7,
+        scratch_shapes=[
+            vmem((fsdp_count,) + gains_own.shape, F32),
+            vmem((2, count, width), BF), vmem((3, 2, count, width), BF), vmem((2, count, width), BF),
+            vmem((4, count, STEP), F32), vmem((2, count, width), F32), vmem((2, count, width), BF),
+            vmem((3, 2, width, STEP), BF), vmem((groups, 2, width, STEP), BF),
+            vmem((groups, 8, STEP), F32), vmem((groups, 8, STEP), F32),
+            dma((units, Z)), dma((units, Z)), dma((units, Z)), dma((units, Z)),
+            dma((units, Z, X)), dma((units, Z, X)), dma((groups, fsdp_count)), dma((groups, fsdp_count)),
+            dma((units,)), dma((units,)), dma((groups,)), dma((groups,)),
+            dma((X, Z)), dma((X, Z)), dma((groups,)), dma((groups,)), dma, dma, dma, dma,
+            dma((2,)), dma((units + 8,)),
+        ],
+        compiler_params=pltpu.CompilerParams(
+            vmem_limit_bytes=VMEM_BYTES, collective_id=0, has_side_effects=True
+        ),
+        name="attention_forward",
+    )(frames, carried, cot, attn_own, inner_own, down_own, gains_own)
 
 
 def feed_forward_kernel(
@@ -480,10 +698,6 @@
     )(b, c, inner, down)
 
 
-PAIRS = ((0, 0), (0, 1), (0, 2), (1, 0), (1, 1), (1, 2), (1, 3))
-CHUNK = 32
-
-
 def total_of(values):
     return functools.reduce(jnp.add, values)
 
@@ -498,7 +712,7 @@
     sdx, rdx, sdz, rdz, sdf, rdf, down_sem, s_out, r_out, free,
 ):
     i = pl.program_id(0)
-    frames, step = q.shape[1:]
+    frames, step = q.shape[2:]
     R = final.shape[1]
     dp, fs = lax.axis_index("dp"), lax.axis_index("fsdp")
     F = Z * X
@@ -710,33 +924,25 @@
         first = lax.broadcasted_iota(jnp.int32, (frames, step), 0) == 0
         last = lax.broadcasted_iota(jnp.int32, (frames, step), 0) == frames - 1
         for p in range(2):
-            mixed_grad[p] = nt(dhb[p], mix[0, p]).astype(BF)
-            before[p] = jnp.where(first, edge[p : p + 1, :], pltpu.roll(k[p].astype(F32), 1, 0))
-            before[2 + p] = jnp.where(first, edge[2 + p : 3 + p, :], pltpu.roll(v[p].astype(F32), 1, 0))
+            mixed_grad[p] = total_of(
+                [nt(dhb[p, :, g * step : (g + 1) * step], mix[g, 0, p]) for g in range(groups)]
+            ).astype(BF)
+            before[p] = jnp.where(first, edge[0, p : p + 1, :], pltpu.roll(k[0, p].astype(F32), 1, 0))
+            before[2 + p] = jnp.where(first, edge[0, 2 + p : 3 + p, :], pltpu.roll(v[0, p].astype(F32), 1, 0))
 
         def chunk(c, carry):
             rows = pl.ds(pl.multiple_of(c * CHUNK, CHUNK), CHUNK)
             allowed = jnp.broadcast_to(carried[rows, :], (CHUNK, step)) > 0.5
-            queries = [q[p, rows, :].astype(F32) for p in range(2)]
+            queries = [q[0, p, rows, :].astype(F32) for p in range(2)]
             cots = [mixed_grad[p, rows, :].astype(F32) for p in range(2)]
-            keys = [before[p, rows, :] for p in range(2)] + [k[p, rows, :].astype(F32) for p in range(2)]
-            values = [before[2 + p, rows, :] for p in range(2)] + [v[p, rows, :].astype(F32) for p in range(2)]
-
-            def per_head(left, right):
-                products = [(left[p] * right[n]).astype(BF) for p, n in PAIRS]
-                sums = nn(jnp.concatenate(products, axis=0), ones)
-                return [sums[m * CHUNK : (m + 1) * CHUNK] for m in range(len(PAIRS))]
-
-            scores = per_head(queries, keys)
-            dprobs = per_head(cots, values)
+            keys = [before[p, rows, :] for p in range(2)] + [k[0, p, rows, :].astype(F32) for p in range(2)]
+            values = [before[2 + p, rows, :] for p in range(2)] + [v[0, p, rows, :].astype(F32) for p in range(2)]
+
+            scores = per_head(queries, keys, ones)
+            dprobs = per_head(cots, values, ones)
             key_grads, value_grads = [[] for _ in range(4)], [[] for _ in range(4)]
-            for p, span in ((0, range(0, 3)), (1, range(3, 7))):
-                s = [jnp.where(allowed, scores[m] * scale, -1e30) if PAIRS[m][1] < 2 else scores[m] * scale for m in span]
-                top = functools.reduce(jnp.maximum, s)
-                e = [jnp.exp(value - top) for value in s]
-                e = [jnp.where(allowed, value, 0.0) if PAIRS[m][1] < 2 else value for m, value in zip(span, e)]
-                inverse = 1.0 / total_of(e)
-                probs = [value * inverse for value in e]
+            for p, span in SPANS:
+                probs = head_probs(scores, span, allowed, scale)
                 mean = total_of([pr * dprobs[m] for m, pr in zip(span, probs)])
                 query_grad = []
                 for m, pr in zip(span, probs):
@@ -805,7 +1011,7 @@
 
         to_core(n).start()
         for p in range(2):
-            da[p] += total_of([nt(grads[slot, t, p], proj[t, p]) for t in range(3)])
+            da[p] += total_of([nt(grads[slot, t, p], proj[0, t, p]) for t in range(3)])
 
     @pl.when(i == groups + 5)
     def _():
@@ -843,9 +1049,9 @@
         out_copy.wait()
 
 
-def attention_back(carried, q, k, v, edge, attn, dhb, mixed, inputs, down_sum, out_send, head_size, fsdp_count):
-    _, frames, width = q.shape
-    step = 256
+def attention_back(carried, qkv_rows, edge, attn, dhb, mixed, inputs, down_sum, out_send, head_size, fsdp_count):
+    _, frames, width = dhb.shape
+    step = STEP
     groups = width // step
     X = fsdp_count // Z
     R = width // fsdp_count
@@ -854,12 +1060,12 @@
     def early(i):
         return jnp.minimum(i, groups - 1)
 
-    rows = pl.BlockSpec((2, frames, step), lambda i: (0, 0, early(i)))
-    edge_spec = pl.BlockSpec((8, step), lambda i: (0, early(i)))
+    rows = [pl.BlockSpec((1, 2, frames, step), lambda i, t=t: (t, 0, 0, early(i))) for t in range(3)]
+    edge_spec = pl.BlockSpec((1, 8, step), lambda i: (early(i), 0, 0))
     mask = pl.BlockSpec((frames, 1), lambda i: (0, 0), pipeline_mode=pl.Buffered(1))
     whole = pl.BlockSpec((2, frames, width), lambda i: (0, 0, 0), pipeline_mode=pl.Buffered(1))
-    mix_spec = pl.BlockSpec((1, 2, step, width), lambda i: (3, 0, early(i), 0))
-    proj_spec = pl.BlockSpec((3, 2, width, step), lambda i: (0, 0, 0, jnp.clip(i - 1, 0, groups - 1)))
+    mix_spec = pl.BlockSpec((groups, 1, 2, step, step), lambda i: (0, 3, 0, early(i), 0))
+    proj_spec = pl.BlockSpec((1, 3, 2, width, step), lambda i: (jnp.clip(i - 1, 0, groups - 1), 0, 0, 0, 0))
     dma, vmem = pltpu.SemaphoreType.DMA, pltpu.VMEM
     n = groups
     return pl.pallas_call(
@@ -871,7 +1077,7 @@
             jax.ShapeDtypeStruct((4, R2, half), BF),
             jax.ShapeDtypeStruct(out_send.shape, BF),
         ),
-        in_specs=[mask, rows, rows, rows, edge_spec, mix_spec, whole, whole, whole, proj_spec, ANY, ANY],
+        in_specs=[mask, *rows, edge_spec, mix_spec, whole, whole, whole, proj_spec, ANY, ANY],
         out_specs=(whole, ANY, ANY, ANY),
         scratch_shapes=[
             vmem((2, frames, step), BF), vmem((4, frames, step), F32), vmem((4, frames, step), F32),
@@ -892,7 +1098,7 @@
         ],
         compiler_params=pltpu.CompilerParams(vmem_limit_bytes=63 * 2**20, collective_id=2, has_side_effects=True),
         name="attention_back",
-    )(carried, q, k, v, edge, attn, dhb, mixed, inputs, attn, down_sum, out_send)
+    )(carried, qkv_rows, qkv_rows, qkv_rows, edge, attn, dhb, mixed, inputs, attn, down_sum, out_send)
 
 
 def per_device(
@@ -934,21 +1140,24 @@
     def to_z(value, k):
         return permute(value, lambda d, f: (d, ((f // X + k) % Z) * X + f % X))
 
-    def shifted(value, steps):
-        def target(d, f):
-            to = d * fsdp_count + f + steps
-            return divmod(to, fsdp_count) if 0 <= to < devices else None
-
-        return permute(value, target)
-
     device = dp * fsdp_count + fs
     padded_ids = jnp.concatenate([jnp.full((1,), -1, jnp.int32), segment_ids])
     window = lax.dynamic_slice_in_dim(padded_ids, device * frame_count, frame_count + 1)
     carried = (window[1:] == window[:-1]).astype(F32)[:, None]
 
-    attn_own = lax.select_n(
-        dp, qkv_weight[:, :, :width], qkv_weight[:, :, width : 2 * width], qkv_weight[:, :, 2 * width :], mix_weight
+    quarters = (
+        qkv_weight[:, :, :width], qkv_weight[:, :, width : 2 * width], qkv_weight[:, :, 2 * width :], mix_weight
+    )
+    last = width - STEP
+    own_rows = jnp.concatenate(
+        [
+            lax.select_n(dp, *(m[:, :, :last] for m in quarters)),
+            lax.select_n(core > 0, *(m[:, :, last:] for m in quarters[:2])),
+            lax.select_n(core > 0, *(m[:, :, last:] for m in quarters[2:])),
+        ],
+        axis=-1,
     ).astype(BF)
+    attn_own = own_rows.reshape(positions, -1, width // STEP + 1, STEP).transpose(2, 0, 1, 3)
     inner_own = lax.dynamic_slice(
         inner_weight, (y, 0, core * hidden), (1, inner_weight.shape[1], hidden)
     )[0].astype(BF)
@@ -957,32 +1166,19 @@
         down_weight, (y, 0, core * half_width), (1, down_weight.shape[1], half_width)
     )[0].astype(BF)
     own_gains = norm_gains.astype(BF).astype(F32)
-    gains_own = jnp.zeros((8, 128), F32).at[: own_gains.shape[0], : own_gains.shape[1]].set(own_gains)
-    attn, inner, down, gains_all = gather_weights(attn_own, inner_own, down_own, gains_own, fsdp_count)
-    gains = gains_all[:, :2, : own_gains.shape[1]].transpose(1, 0, 2).reshape(2, width)
-
-    xf = frames.transpose(1, 0, 2).astype(F32)
+    gains_own = lax.dynamic_update_slice(jnp.zeros((8, width), F32), own_gains, (0, fs * own_gains.shape[1]))
+    frames_by = frames.transpose(1, 0, 2)
     cot = cotangent.transpose(1, 0, 2)
-    cot_there = to_y(lax.dynamic_index_in_dim(cot, 1 - y, 0, keepdims=False))
+    attn, inner, down, gains, a, qkv_rows, mixed, edge, hres, b_rows, c_rows = forward(
+        frames_by, carried, cot, attn_own, inner_own, down_own, gains_own, head_size, fsdp_count
+    )
+    xf = frames_by.astype(F32)
     r1 = scale_rows(xf)
     n1 = xf * r1
-    a = (n1 * gains[0]).astype(BF)
-
-    def each(left, right):
-        return jnp.einsum("pfd,pde->pfe", left, right, preferred_element_type=F32)
-
-    q, k, v = (each(a, attn[t]).astype(BF) for t in range(3))
-    edge_rows = shifted(jnp.concatenate([k[:, -1], v[:, -1]], axis=0), 1)
-    edge = jnp.pad(edge_rows.astype(F32), ((0, 4), (0, 0)))
-    mixed = attend(carried, q, k, v, edge, head_size)
-    hres = xf + each(mixed, attn[3])
     r2 = scale_rows(hres)
     n2 = hres * r2
-    b = (n2 * gains[1]).astype(BF)
-
-    b_there = to_y(lax.dynamic_index_in_dim(b, 1 - y, 0, keepdims=False))
-    b_rows = jnp.concatenate([lax.dynamic_index_in_dim(b, y, 0, keepdims=False), b_there], axis=0)
-    c_rows = jnp.concatenate([lax.dynamic_index_in_dim(cot, y, 0, keepdims=False), cot_there], axis=0)
+    b_rows = b_rows.reshape(2 * frame_count, width)
+    c_rows = c_rows.reshape(2 * frame_count, width)
     out, back, out_there, back_there, inner_shares, down_sum = feed_forward(b_rows, c_rows, inner, down, fsdp_count)
 
     def by_position(mine, theirs):
@@ -995,7 +1191,7 @@
     dhb = dh.astype(BF)
     down_sum = down_sum.reshape(Z, X, -1, half_width)
     da, attn_shares, down_shares, out_here = attention_back(
-        carried, q, k, v, edge, attn, dhb, mixed, a, down_sum, out_there, head_size, fsdp_count
+        carried, qkv_rows, edge, attn, dhb, mixed, a, down_sum, out_there, head_size, fsdp_count
     )
     layer_out = (hres + by_position(out, out_here.astype(F32))).astype(BF).transpose(1, 0, 2)
     e1 = jnp.sum(da * n1, axis=(0, 1))

time: 679 us -> 605 us (0.89)
  waiting for transfers between devices: 23.7 us -> 0.85 us
  matrix products: 21.4 us -> 0 us
  Pallas kernels: 485 us -> 472 us
  other arithmetic: 72.7 us -> 65.5 us
    ppermute x9 -> x6, waiting for transfers between devices: 23.7 us -> 0.85 us  [permute(): return lax.ppermute(value, axes, pairs)]
    dot_general x4 -> x0, matrix products: 21.4 us -> none  [each(): return jnp.einsum('pfd,pde->pfe', left, right, preferred_element_type=F32)]
    pallas_call x2 -> x1, Pallas kernels: 190 us -> 181 us  [forward(): pl.pallas_call(functools.partial(forward_kernel, X, groups, head_size), o...]
    slice x1 -> x5, local copies, waits for them, and re-layouts: 0.01 us -> 6.93 us  [the longest x2 3.39 us: per_device(): m[:, :, :last]]
    ppermute x9 -> x6, starting transfers between devices: 25.1 us -> 19.3 us  [permute(): return lax.ppermute(value, axes, pairs)]
    unnamed x65 -> x68, local copies, waits for them, and re-layouts: 14.8 us -> 13.7 us
  transfers between devices with their start and end apart: 9 -> 6, of which waited for: 2 -> 1; matrix products, arithmetic and copies ran while one was open for 12% -> 10% of each run, Pallas kernels for 2% -> 0%
where the time goes in v3:
time: 605 us; the launch traced here: 597 us
  Pallas kernels  472 us (78%)
  other arithmetic  65.5 us (11%)
  local copies, waits for them, and re-layouts  37.5 us (6%)
  starting transfers between devices  19.3 us (3%)
    pallas_call x1, Pallas kernels, forward(): pl.pallas_call(functools.partial(forward_kernel, X, groups, head_size), o...  181 us
    pallas_call x1, Pallas kernels, attention_back(): pl.pallas_call(functools.partial(attention_back_kernel, X, groups, head_s...  161 us
    pallas_call x1, Pallas kernels, feed_forward(): pl.pallas_call(functools.partial(feed_forward_kernel, X, J), grid=(J + 3,...  131 us
    add x5, other arithmetic, owner_update(): average_new = average_rate * average + (1.0 - average_rate) * weight_new  36.5 us
    ppermute x6, starting transfers between devices, permute(): return lax.ppermute(value, axes, pairs)  19.3 us
    unnamed x68, local copies, waits for them, and re-layouts  13.7 us
  transfers between devices with their start and end apart: 6, of which 1 were waited for; matrix products, arithmetic and copies ran while one was open for 10% of the time, Pallas kernels for 0%

profile of v3, /device:TPU:0, one launch (start us, length us, event | category | flops | bytes accessed | tf_op | source)
XLA Modules:
  0.0 597.0 jit_solution(15514409109277537296)
XLA Ops:
  0.7 2.0 fusion.25
  2.7 2.6 fusion.24
  10.1 3.3 copy_bitcast_fusion
  13.6 1.0 copy.75
  14.6 1.0 copy.72
  16.0 1.2 copy.71
  17.9 1.1 copy.58
  19.0 2.3 fusion.14.inner_own
  21.3 1.9 fusion.15.down_own
  23.8 180.6 %attention_forward.1 = (bf16[4,4,2,1024,256]{4,3,2,1,0:T(8,128)(2,1)}, bf16[2,1024,2816]{2,1,0:T(8,128)(2,1)}, bf16[2,2816,512]{2,1,0:T(8,128)(2,1)}, f32[8,1024...) custom-call(bf16[2,512,1024]{2,1,0:T(8,128)(2,1)} %get-tuple-element, ...), custom_call_target="tpu_custom_call" | custom-call | tf_op jit(solution)/shard_map/attention_forward/pallas_call | solution.py:451
  204.4 2.5 multiply_reduce_fusion.2
  206.9 130.8 %feed_forward.1 = (f32[512,1024]{1,0:T(8,128)}, f32[512,1024]{1,0:T(8,128)}, bf16[512,1024]{1,0:T(8,128)(2,1)}, bf16[512,1024]{1,0:T(8,128)(2,1)}, bf16[4,128,28...) custom-call(bf16[1024,1024]{1,0:T(8,128)(2,1)} %bitcast.111, bf16[1024,1024]{1,0:T(8,128)(2,1)} %bitcast.112, ...), custom_call_target="tpu_custom_call" | custom-call | flops 53150220288 | bytes 62914560 | tf_op jit(solution)/shard_map/feed_forward/pallas_call | solution.py:670
  337.8 1.6 bitcast_convert_fusion.1
  340.3 3.2 multiply_reduce_fusion
  344.4 2.3 fusion.23.dhb
  346.7 160.8 %attention_back.1 = (f32[2,512,1024]{2,1,0:T(8,128)}, bf16[4,2,128,1024]{3,2,1,0:T(8,128)(2,1)}, bf16[4,352,512]{2,1,0:T(8,128)(2,1)}, bf16[512,1024]{1,0:T(8,128)(2,1)}) custom-call(f32[512,1]{1,0:T(8,128)} %copy.59.carried, bf16[3,2,512,1024]{3,2,1,0:T(8,128)(2,1)} %get-tuple-element.49.q.k.v, bf16[3,2,512,1024]{3,2,1,0:T(8,128)(2,1)} %get-tuple-element.49.q.k.v, ...), custom_call_target="tpu_custom_call" | custom-call | tf_op jit(solution)/shard_map/attention_back/pallas_call | solution.py:1071
  507.6 4.4 fusion.8
  513.5 2.9 bitcast_convert_fusion
  516.5 2.6 slice_bitcast_fusion.6
  519.1 3.7 slice_bitcast_fusion.1
  522.8 7.9 %fusion.13 = (bf16[512,2,1024]{2,0,1:T(8,128)(2,1)S(1)}, bf16[512,2,1024]{2,0,1:T(8,128)(2,1)}) fusion(f32[2,512,1024]{2,1,0:T(8,128)S(1)} %copy-done.11, f32[2,512]{1,0:T(2,128)} %broadcast_multiply_fusion, f32[1024]{0:T(1024)} %bitcast.103, f32[2,512]{1,0:T(2,128)S(1)} %fusion.19, bf16[512,2,1024]{2,1,0:T(2,128)(2,1)S(1)} %copy-done.3, ...), kind=kLoop, calls=%fused_computation.31 | loop fusion | flops 24117248 | bytes 25190400 | tf_op jit(solution)/shard_map/transpose | solution.py:1198
  530.7 15.6 %add_multiply_fusion = (f32[2,128,5632]{2,1,0:T(8,128)}, f32[2,128,5632]{2,1,0:T(8,128)}, f32[2,128,5632]{2,1,0:T(8,128)}, f32[2,128,5632]{2,1,0:T(8,128)}) fusion(f32[2,128,5632]{2,1,0:T(8,128)} %param.33, f32[2,128,5632]{2,1,0:T(8,128)} %param.23, f32[2,128,5632]{2,1,0:T(8,128)} %param.28, bf16[2,128,2816]{2,1,0:T(8,128)(2,1)} %get-tuple-element.141, ...), kind=kLoop, calls=%fused_computation | loop fusion | flops 17301504 | bytes 43253760 | tf_op jit(solution)/shard_map/add | solution.py:51
  546.4 6.6 %add_multiply_fusion.1 = (f32[2,128,3072]{2,1,0:T(8,128)}, f32[2,128,3072]{2,1,0:T(8,128)}, f32[2,128,3072]{2,1,0:T(8,128)}, f32[2,128,3072]{2,1,0:T(8,128)}) fusion(f32[2,128,3072]{2,1,0:T(8,128)S(1)} %copy-done.14, f32[2,128,3072]{2,1,0:T(8,128)S(1)} %copy-done.13, f32[2,128,3072]{2,1,0:T(8,128)} %param.26, bf16[2,128,1024]{2,1,0:T(8,128)(2,1)S(1)} %copy-done.16, ...), kind=kLoop, calls=%fused_computation.23 | loop fusion | flops 11010048 | bytes 23592960 | tf_op jit(solution)/shard_map/add | solution.py:51
  553.8 1.9 collective-permute-start.1
  558.2 6.0 %collective-permute-start.2 = (f32[4,2,128]{2,0,1:T(4,128)S(1)}, f32[4,2,128]{2,0,1:T(4,128)S(1)}, u32[]{:S(2)}, u32[]{:S(2)}) collective-permute-start(f32[4,2,128]{2,0,1:T(4,128)S(1)} %bitcast.106), channel_id=1, source_target_pairs={{0,1},{1,0},{2,3},{3,2},{4,5},{5,4},{6,7},{7,6},{8,9},{9,8},{10,11... | collective-permute-start | bytes 12296 | tf_op jit(solution)/shard_map/ppermute | solution.py:1129
  564.3 9.3 %add_multiply_fusion.2 = (f32[2,352,1024]{2,1,0:T(8,128)}, f32[2,352,1024]{2,1,0:T(8,128)}, f32[2,352,1024]{2,1,0:T(8,128)}, f32[2,352,1024]{2,1,0:T(8,128)}) fusion(f32[2,352,1024]{2,1,0:T(8,128)} %param.34, f32[2,352,1024]{2,1,0:T(8,128)} %param.24, f32[2,352,1024]{2,1,0:T(8,128)} %param.29, bf16[2,352,512]{2,1,0:T(8,128)(2,1)} %get-tuple-element.146, ...), kind=kLoop, calls=%fused_computation.27 | loop fusion | flops 8650752 | bytes 21626880 | tf_op jit(solution)/shard_map/add | solution.py:51
  573.6 3.5 collective-permute-start.5
  577.1 5.5 collective-permute-start.4
  582.6 1.9 collective-permute-start.3
  584.6 4.4 add_multiply_fusion.3
  588.9 3.5 copy.66
  592.4 3.5 copy.67
  (95 shorter events, 13.8 us)
Async XLA Ops:
  0.7 4.7 copy-start.15
  0.7 7.8 %copy-start.2 = (bf16[512,2,1024]{2,1,0:T(2,128)(2,1)S(1)}, bf16[512,2,1024]{2,1,0:T(2,128)(2,1)}, u32[]{:S(2)}) copy-start(bf16[512,2,1024]{2,1,0:T(2,128)(2,1)} %param.18) | copy-start | bytes 6291460
  10.1 3.4 copy-start.21
  10.1 5.5 copy-start.22
  10.1 5.7 copy-start.19
  10.1 7.1 %copy-start.18 = (bf16[2,128,768]{2,1,0:T(8,128)(2,1)S(1)}, bf16[2,128,768]{2,1,0:T(8,128)(2,1)}, u32[]{:S(2)}) copy-start(bf16[2,128,768]{2,1,0:T(8,128)(2,1)} %get-tuple-element.136) | copy-start | bytes 1179652
  17.7 5.4 copy-start.25
  339.4 4.1 copy-start.4
  340.3 167.3 %copy-start.24 = (f32[1,1024]{1,0:T(1,128)}, f32[1,1024]{1,0:T(1,128)S(1)}, u32[]{:S(2)}) copy-start(f32[1,1024]{1,0:T(1,128)S(1)} %get-tuple-element.147) | copy-start | bytes 12292
  340.3 3.5 copy-start
  340.3 4.1 copy-start.7
  507.5 15.2 %copy-start.10 = (f32[512,1024]{1,0:T(8,128)S(1)}, f32[512,1024]{1,0:T(8,128)}, u32[]{:S(2)}) copy-start(f32[512,1024]{1,0:T(8,128)} %get-tuple-element.52) | copy-start | bytes 6291460
  507.6 15.2 %copy-start.11 = (f32[2,512,1024]{2,1,0:T(8,128)S(1)}, f32[2,512,1024]{2,1,0:T(8,128)}, u32[]{:S(2)}) copy-start(f32[2,512,1024]{2,1,0:T(8,128)} %get-tuple-element.60) | copy-start | bytes 12582916
  512.6 40.5 %collective-permute-start = (f32[2,1024]{1,0:T(2,128)}, f32[2,1024]{1,0:T(2,128)}, u32[]{:S(2)}, u32[]{:S(2)}) collective-permute-start(f32[2,1024]{1,0:T(2,128)} %pad_maximum_fusion.1), channel_id=1, source_target_pairs={{0,8},{1,9},{2,10},{3,11},{4,12},{5,13},{6,14},{7,15},{8,0},{9,1},... | collective-permute-start | bytes 24584 | tf_op jit(solution)/shard_map/ppermute | solution.py:1129
  513.5 9.3 %copy-start.8 = (bf16[512,2,1024]{2,1,0:T(2,128)(2,1)S(1)}, bf16[512,2,1024]{2,1,0:T(2,128)(2,1)}, u32[]{:S(2)}) copy-start(bf16[512,2,1024]{2,1,0:T(2,128)(2,1)} %param.19) | copy-start | bytes 6291460
  516.5 6.3 %copy-start.3 = (bf16[512,2,1024]{2,1,0:T(2,128)(2,1)S(1)}, bf16[512,2,1024]{2,1,0:T(2,128)(2,1)}, u32[]{:S(2)}) copy-start(bf16[512,2,1024]{2,1,0:T(2,128)(2,1)} %param.18) | copy-start | bytes 6291460
  516.5 6.3 %copy-start.5 = (f32[1,512,1024]{2,1,0:T(8,128)S(1)}, f32[1,512,1024]{2,1,0:T(8,128)}, u32[]{:S(2)}) copy-start(f32[1,512,1024]{2,1,0:T(8,128)} %copy-done.4) | copy-start | bytes 6291460
  519.1 3.7 copy-start.1
  530.7 15.7 %copy-start.13 = (f32[2,128,3072]{2,1,0:T(8,128)S(1)}, f32[2,128,3072]{2,1,0:T(8,128)}, u32[]{:S(2)}) copy-start(f32[2,128,3072]{2,1,0:T(8,128)} %param.21) | copy-start | bytes 9437188
  530.7 15.7 %copy-start.14 = (f32[2,128,3072]{2,1,0:T(8,128)S(1)}, f32[2,128,3072]{2,1,0:T(8,128)}, u32[]{:S(2)}) copy-start(f32[2,128,3072]{2,1,0:T(8,128)} %param.31) | copy-start | bytes 9437188
  530.7 15.7 %copy-start.16 = (bf16[2,128,1024]{2,1,0:T(8,128)(2,1)S(1)}, bf16[2,128,1024]{2,1,0:T(8,128)(2,1)}, u32[]{:S(2)}) copy-start(bf16[2,128,1024]{2,1,0:T(8,128)(2,1)} %get-tuple-element.143) | copy-start | bytes 1572868
  530.7 15.7 %copy-start.17 = (bf16[2,128,1024]{2,1,0:T(8,128)(2,1)S(1)}, bf16[2,128,1024]{2,1,0:T(8,128)(2,1)}, u32[]{:S(2)}) copy-start(bf16[2,128,1024]{2,1,0:T(8,128)(2,1)} %get-tuple-element.144) | copy-start | bytes 1572868
  546.4 9.2 %copy-start.20 = (bf16[4,352,512]{2,1,0:T(8,128)(2,1)S(1)}, bf16[4,352,512]{2,1,0:T(8,128)(2,1)}, u32[]{:S(2)}) copy-start(bf16[4,352,512]{2,1,0:T(8,128)(2,1)} %get-tuple-element.63) | copy-start | bytes 4325380
  553.8 3.7 collective-permute-start.1
  558.2 15.3 %collective-permute-start.2 = (f32[4,2,128]{2,0,1:T(4,128)S(1)}, f32[4,2,128]{2,0,1:T(4,128)S(1)}, u32[]{:S(2)}, u32[]{:S(2)}) collective-permute-start(f32[4,2,128]{2,0,1:T(4,128)S(1)} %bitcast.106), channel_id=1, source_target_pairs={{0,1},{1,0},{2,3},{3,2},{4,5},{5,4},{6,7},{7,6},{8,9},{9,8},{10,11... | collective-permute-start | bytes 12296 | tf_op jit(solution)/shard_map/ppermute | solution.py:1129
  573.6 22.3 %collective-permute-start.5 = (f32[2,128]{1,0:T(2,128)S(1)}, f32[2,128]{1,0:T(2,128)S(1)}, u32[]{:S(2)}, u32[]{:S(2)}) collective-permute-start(f32[2,128]{1,0:T(2,128)S(1)} %bitcast.110), channel_id=1, source_target_pairs={{0,6},{1,7},{2,0},{3,1},{4,2},{5,3},{6,4},{7,5},{8,14},{9,15},{10,... | collective-permute-start | bytes 3080 | tf_op jit(solution)/shard_map/ppermute | solution.py:1129
  577.1 18.8 %collective-permute-start.4 = (f32[2,128]{1,0:T(2,128)S(1)}, f32[2,128]{1,0:T(2,128)S(1)}, u32[]{:S(2)}, u32[]{:S(2)}) collective-permute-start(f32[2,128]{1,0:T(2,128)S(1)} %bitcast.109), channel_id=1, source_target_pairs={{0,4},{1,5},{2,6},{3,7},{4,0},{5,1},{6,2},{7,3},{8,12},{9,13},{10,... | collective-permute-start | bytes 3080 | tf_op jit(solution)/shard_map/ppermute | solution.py:1129
  582.6 6.3 %copy-start.12 = (bf16[512,2,1024]{2,0,1:T(8,128)(2,1)S(1)}, bf16[512,2,1024]{2,0,1:T(8,128)(2,1)}, u32[]{:S(2)}) copy-start(bf16[512,2,1024]{2,0,1:T(8,128)(2,1)} %get-tuple-element.133) | copy-start | bytes 6291460
  582.6 13.3 %collective-permute-start.3 = (f32[2,128]{1,0:T(2,128)S(1)}, f32[2,128]{1,0:T(2,128)S(1)}, u32[]{:S(2)}, u32[]{:S(2)}) collective-permute-start(f32[2,128]{1,0:T(2,128)S(1)} %bitcast.108), channel_id=1, source_target_pairs={{0,2},{1,3},{2,4},{3,5},{4,6},{5,7},{6,0},{7,1},{8,10},{9,11},{10,... | collective-permute-start | bytes 3080 | tf_op jit(solution)/shard_map/ppermute | solution.py:1129
  592.4 3.5 copy-start.26
  592.4 3.5 copy-start.27
  592.4 3.5 copy-start.28
  (3 other events, 4.7 us)

commit v4 on v3

--- a/solution.py
+++ b/solution.py
@@ -485,9 +485,10 @@
 
 
 def feed_forward_kernel(
-    X, J, b, c, inner, down, out_mine, back_mine, out_theirs, back_recv, inner_all, down_sum,
-    out, back, down_here, down_there, down_from_core, mine, other, from_core, summed, from_x, column, from_z, final, staged,
+    X, J, b, c, inner, down, out_mine, back_mine, out_theirs, back_recv, inner_all, down_columns, down_sum,
+    out, back, down_here, down_there, down_from_core, down_stage, down_column, down_from_x, mine, other, from_core, summed, from_x, column, from_z, final, staged,
     s1, r1, s2, r2, s3, r3, s5, r5, s6, r6, s7, r7, local_sem,
+    s_stage, s_own, sdx, rdx, s_column,
 ):
     j = pl.program_id(0)
     half = down.shape[2]
@@ -532,6 +533,28 @@
 
     exchange = remote_copy(staged, back_recv, s6, r6, y_peer)
 
+    R2 = down_column.shape[1]
+    ends = [-(-(g + 1) * X * R2 // step) - 1 for g in range(Z)]
+
+    def down_rows(g, column):
+        return down_sum.at[pl.ds((g * X + column) * R2, R2), :]
+
+    def down_store(n):
+        return pltpu.make_async_copy(
+            down_stage.at[n % 2], down_sum.at[pl.ds(pl.multiple_of(n * step, step), step), :], s_stage.at[n % 2]
+        )
+
+    def down_load(g):
+        return pltpu.make_async_copy(down_rows(g, x), down_column.at[g], s_own.at[g])
+
+    def down_to_x(g, i):
+        return remote_copy(
+            down_rows(g, lax.rem(x + i, X)), down_from_x.at[g, i - 1], sdx.at[g, i - 1], rdx.at[g, i - 1], x_peer(i)
+        )
+
+    def down_keep(g):
+        return pltpu.make_async_copy(down_column.at[g], down_columns.at[g], s_column.at[g])
+
     def down_to_core(n):
         return remote_copy(down_there.at[n % 2], down_from_core.at[n], s7.at[n % 2], r7.at[n], core_peer)
 
@@ -546,6 +569,17 @@
         out[...] = jnp.zeros_like(out)
         back[...] = jnp.zeros_like(back)
 
+    @pl.when((j >= 2) & (j < J + 2))
+    def _():
+        down_store(j - 2).wait()
+
+    for g in range(Z):
+        @pl.when(j == ends[g] + 2)
+        def _():
+            for i in range(1, X):
+                down_to_x(g, i).start()
+            down_load(g).start()
+
     @pl.when((j >= 1) & (j < J + 1))
     def _():
         n = j - 1
@@ -557,7 +591,8 @@
                 to_x(n - 2, i).wait_send()
 
         down_to_core(n).wait_recv()
-        down_sum[...] = (down_here[n % 2].astype(F32) + down_from_core[n].astype(F32)).astype(BF)
+        down_stage[n % 2] = (down_here[n % 2].astype(F32) + down_from_core[n].astype(F32)).astype(BF)
+        down_store(n).start()
         total = (mine[n % 2].astype(F32) + from_core[n].astype(F32)).astype(BF)
         summed[n % 2] = total.reshape(summed.shape[1:])
         for i in range(1, X):
@@ -581,7 +616,17 @@
         for k in range(1, Z):
             to_z(n, k).start()
 
-    @pl.when(j >= 3)
+    for g in range(Z):
+        @pl.when(j == ends[g] + 3)
+        def _():
+            down_load(g).wait()
+            for i in range(1, X):
+                down_to_x(g, i).wait_recv()
+            total = down_column[g].astype(F32) + total_of([down_from_x[g, i].astype(F32) for i in range(X - 1)])
+            down_column[g] = total.astype(BF)
+            down_keep(g).start()
+
+    @pl.when((j >= 3) & (j < J + 3))
     def _():
         n = j - 3
         for k in range(1, Z):
@@ -651,6 +696,10 @@
 
         lax.fori_loop(0, J, finish, 0)
         exchange.wait()
+        for g in range(Z):
+            down_keep(g).wait()
+            for i in range(1, X):
+                down_to_x(g, i).wait_send()
 
 
 def feed_forward(b, c, inner, down, fsdp_count):
@@ -660,12 +709,11 @@
     step = 256
     J = hidden // step
     X = fsdp_count // Z
-    R = width // fsdp_count
+    R, R2 = width // fsdp_count, hidden // fsdp_count
     whole = pl.BlockSpec((rows, width), lambda j: (0, 0), pipeline_mode=pl.Buffered(1))
     part = pl.BlockSpec((rows // 2, width), lambda j: (0, 0), pipeline_mode=pl.Buffered(1))
     inner_spec = pl.BlockSpec((2, width, step), lambda j: (0, 0, jnp.minimum(j, J - 1)))
     down_spec = pl.BlockSpec((2, step, half), lambda j: (0, jnp.minimum(j, J - 1), 0))
-    sum_spec = pl.BlockSpec((step, half), lambda j: (jnp.clip(j - 1, 0, J - 1), 0))
     dma, vmem = pltpu.SemaphoreType.DMA, pltpu.VMEM
     return pl.pallas_call(
         functools.partial(feed_forward_kernel, X, J),
@@ -676,19 +724,22 @@
             jax.ShapeDtypeStruct((rows // 2, width), BF),
             jax.ShapeDtypeStruct((rows // 2, width), BF),
             jax.ShapeDtypeStruct((4, R, hidden), BF),
+            jax.ShapeDtypeStruct((Z, R2, half), BF),
             jax.ShapeDtypeStruct((hidden, half), BF),
         ),
         in_specs=[whole, whole, inner_spec, down_spec],
-        out_specs=(part, part, part, ANY, ANY, sum_spec),
+        out_specs=(part, part, part, ANY, ANY, ANY, ANY),
         scratch_shapes=[
             vmem((rows, width), F32), vmem((rows, width), F32),
             vmem((2, step, half), BF), vmem((2, step, half), BF), vmem((J, step, half), BF),
+            vmem((2, step, half), BF), vmem((Z, R2, half), BF), vmem((Z, X - 1, R2, half), BF),
             vmem((2, width, step), BF), vmem((2, width, step), BF), vmem((J, width, step), BF),
             vmem((2, Z, X, R, step), BF), vmem((J, X - 1, Z, R, step), BF),
             vmem((2, Z, R, step), BF), vmem((J, Z - 1, R, step), BF),
             vmem((J, R, step), BF), vmem((rows // 2, width), BF),
             dma((2,)), dma((J,)), dma((2, X - 1)), dma((J, X - 1)), dma((2, Z - 1)), dma((J, Z - 1)),
             dma((J, 3)), dma((J, 3)), dma, dma, dma((2,)), dma((J,)), dma((J,)),
+            dma((2,)), dma((Z,)), dma((Z, X - 1)), dma((Z, X - 1)), dma((Z,)),
         ],
         compiler_params=pltpu.CompilerParams(
             vmem_limit_bytes=VMEM_BYTES, collective_id=1, has_side_effects=True
@@ -703,17 +754,19 @@
 
 
 def attention_back_kernel(
-    X, groups, head_size, carried, q, k, v, edge, mix, dhb, mixed, inputs, proj, down_sum, out_send,
-    da, attn_all, down_all, out_recv,
-    mixed_grad, before, terms_before, terms_here, tails, grads, edge_send, edge_recv,
+    X, groups, head_size, carried, q, k, v, edge, mix, dhb, mixed, inputs, proj, gains, second_gain, frames_in, down_in, out_send,
+    frames_grad, gains_sum, attn_all, down_all, out_recv,
+    da, gain_terms, gain_from, mixed_grad, before, terms_before, terms_here, tails, grads, edge_send, edge_recv,
     mine, other, from_core, keep_y, send_y, from_y, summed, from_x, column, from_z, final, plane, from_plane, final_plane,
-    down_column, down_from_x, down_from_z, down_final,
+    down_mine, down_from_z, down_final,
     s_edge, r_edge, s1, r1, sy, ry, sxa, rxa, sxb, rxb, sz, rz, sf, rf, sp, rp, sc, rc, local_sem,
-    sdx, rdx, sdz, rdz, sdf, rdf, down_sem, s_out, r_out, free,
+    s_out, r_out, sg, rg, frame_sem, sdz, rdz, sdf, rdf, down_sem, free,
 ):
     i = pl.program_id(0)
     frames, step = q.shape[2:]
-    R = final.shape[1]
+    R, thin = final.shape[1:]
+    subs = 2 * groups
+    slots = from_core.shape[0]
     dp, fs = lax.axis_index("dp"), lax.axis_index("fsdp")
     F = Z * X
     y, core = dp // 2, dp % 2
@@ -738,21 +791,21 @@
         return remote_copy(edge_send.at[n % 2], edge_recv.at[n], s_edge.at[n % 2], r_edge.at[n], before_me)
 
     def to_core(n):
-        return remote_copy(other, from_core.at[n % 2], s1, r1.at[n % 2], core_peer)
+        return remote_copy(other.at[n % 2], from_core.at[n % slots], s1.at[n % 2], r1.at[n % slots], core_peer)
 
     def to_y(n):
         return remote_copy(send_y.at[n % 2], from_y.at[n], sy.at[n % 2], ry.at[n], y_peer)
 
     def to_x_early(n, j):
         return remote_copy(
-            summed.at[n % 2, pl.ds(1, 2), :, lax.rem(x + j, X)], from_x.at[n, j - 1, pl.ds(1, 2)],
-            sxa.at[n % 2, j - 1], rxa.at[n, j - 1], x_peer(j),
+            summed.at[n % 3, pl.ds(1, 2), :, lax.rem(x + j, X)], from_x.at[n, j - 1, pl.ds(1, 2)],
+            sxa.at[n % 3, j - 1], rxa.at[n, j - 1], x_peer(j),
         )
 
     def to_x_late(n, j):
         return remote_copy(
-            summed.at[n % 2, 0, :, lax.rem(x + j, X)], from_x.at[n, j - 1, 0],
-            sxb.at[n % 2, j - 1], rxb.at[n, j - 1], x_peer(j),
+            summed.at[n % 3, 0, :, lax.rem(x + j, X)], from_x.at[n, j - 1, 0],
+            sxb.at[n % 3, j - 1], rxb.at[n, j - 1], x_peer(j),
         )
 
     def to_z(n, j):
@@ -761,10 +814,25 @@
         )
 
     def place(n, t):
-        return attn_all.at[t, core, :, pl.ds(pl.multiple_of(n * step, step), step)]
+        return attn_all.at[t, core, :, pl.ds(pl.multiple_of(n * thin, thin), thin)]
 
     def share(n, d):
         return remote_copy(final.at[n], place(n, y), sf.at[n, d - 1], rf.at[n, d - 1], dp_peer(d))
+
+    def relay(n):
+        return remote_copy(place(n, 1 - y), place(n, 1 - y), sf.at[n, 2], rf.at[n, 2], core_peer)
+
+    def down_to_z(k):
+        return remote_copy(
+            down_in.at[lax.rem(z + k, Z)], down_from_z.at[k - 1], sdz.at[k - 1], rdz.at[k - 1], z_peer(k)
+        )
+
+    def down_share(d):
+        return remote_copy(down_final, down_all.at[dp], sdf.at[d - 1], rdf.at[d - 1], dp_peer(d))
+
+    def down_relay():
+        part = down_all.at[(1 - y) * 2 + core]
+        return remote_copy(part, part, sdf.at[2], rdf.at[2], core_peer)
 
     def to_plane(n):
         return remote_copy(plane.at[n], from_plane.at[n], sp.at[n], rp.at[n], y_peer)
@@ -776,20 +844,15 @@
         src = final.at[n] if t == 0 else final_plane.at[n, t - 1]
         return pltpu.make_async_copy(src, place(n, y if t == 0 else 1 + t), local_sem.at[n, t])
 
-    def down_to_x(j):
-        return remote_copy(
-            down_sum.at[:, lax.rem(x + j, X)], down_from_x.at[j - 1], sdx.at[j - 1], rdx.at[j - 1], x_peer(j)
-        )
-
-    def down_to_z(j):
-        return remote_copy(
-            down_column.at[lax.rem(z + j, Z)], down_from_z.at[j - 1], sdz.at[j - 1], rdz.at[j - 1], z_peer(j)
-        )
-
-    def down_share(d):
-        return remote_copy(down_final, down_all.at[dp], sdf.at[d - 1], rdf.at[d - 1], dp_peer(d))
-
-    down_mine = pltpu.make_async_copy(down_sum.at[:, x], down_column, down_sem.at[0])
+    def load_frames(g):
+        dst = grads.at[g] if g < 3 else mixed_grad
+        return pltpu.make_async_copy(frames_in.at[:, :, pl.ds(g * step, step)], dst, frame_sem.at[g])
+
+    def gain_copy(level, n):
+        peer = (core_peer, y_peer, x_peer(n + 1), z_peer(n + 1))[level]
+        return remote_copy(gain_terms.at[level], gain_from.at[level, n], sg.at[level, n], rg.at[level, n], peer)
+
+    down_load = pltpu.make_async_copy(down_in.at[z], down_mine, down_sem.at[0])
     down_keep = pltpu.make_async_copy(down_final, down_all.at[dp], down_sem.at[1])
     out_copy = remote_copy(out_send, out_recv, s_out, r_out, y_peer)
 
@@ -802,26 +865,78 @@
             pl.semaphore_signal(barrier, inc=1, device_id=peer, device_id_type=MESH)
         pl.semaphore_wait(barrier, len(peers))
         out_copy.start()
+        for k in range(1, Z):
+            down_to_z(k).start()
+        down_load.start()
+        da[...] = jnp.zeros_like(da)
+
+        @pl.when(me == devices - 1)
+        def _():
+            edge_recv[...] = jnp.zeros_like(edge_recv)
+
+    def active(first):
+        return (i >= first) & (i < first + subs)
+
+    @pl.when(active(2))
+    def _():
+        n = i - 2
+        to_core(n).wait_recv()
+
+        @pl.when(n >= 2)
+        def _():
+            to_y(n - 2).wait_send()
+
+        @pl.when(n >= 3)
+        def _():
+            for j in range(1, X):
+                to_x_early(n - 3, j).wait_send()
+
+        def both(t):
+            return (mine[n % 2, t].astype(F32) + from_core[n % slots, t].astype(F32)).astype(BF)
+
+        send_y[n % 2] = both(1 - y)
+        to_y(n).start()
+        for t in range(2):
+            summed[n % 3, 1 + t] = both(2 + t).reshape(summed.shape[2:])
         for j in range(1, X):
-            down_to_x(j).start()
-        down_mine.start()
-        da[...] = jnp.zeros_like(da)
-
-        @pl.when(me == devices - 1)
-        def _():
-            edge_recv[...] = jnp.zeros_like(edge_recv)
-
-    def active(first):
-        return (i >= first) & (i < first + groups)
-
-    @pl.when(active(6))
-    def _():
-        n = i - 6
-        to_plane(n).wait_recv()
-        final_plane[n] = (plane[n].astype(F32) + from_plane[n].astype(F32)).astype(BF)
-        for t in range(2):
-            keep(n, t + 1).start()
-            share_core(n, t).start()
+            to_x_early(n, j).start()
+        keep_y[n % 2] = both(y)
+
+        @pl.when(n < subs - slots)
+        def _():
+            pl.semaphore_signal(free, inc=1, device_id=core_peer, device_id_type=MESH)
+
+    @pl.when(active(3))
+    def _():
+        n = i - 3
+        to_y(n).wait_recv()
+
+        @pl.when(n >= 3)
+        def _():
+            for j in range(1, X):
+                to_x_late(n - 3, j).wait_send()
+
+        total = (keep_y[n % 2].astype(F32) + from_y[n].astype(F32)).astype(BF)
+        summed[n % 3, 0] = total.reshape(summed.shape[2:])
+        for j in range(1, X):
+            to_x_late(n, j).start()
+
+    @pl.when(active(4))
+    def _():
+        n = i - 4
+        for j in range(1, X):
+            to_x_early(n, j).wait_recv()
+            to_x_late(n, j).wait_recv()
+
+        @pl.when(n >= 2)
+        def _():
+            for j in range(1, Z):
+                to_z(n - 2, j).wait_send()
+
+        total = summed[n % 3, :, :, x].astype(F32) + total_of([from_x[n, j].astype(F32) for j in range(X - 1)])
+        column[n % 2] = total.astype(BF)
+        for j in range(1, Z):
+            to_z(n, j).start()
 
     @pl.when(active(5))
     def _():
@@ -834,91 +949,40 @@
         plane[n] = total[1:]
         to_plane(n).start()
         keep(n, 0).start()
-        for d in range(1, 4):
+        for d in range(1, 3):
             share(n, d).start()
 
-    @pl.when(active(4))
-    def _():
-        n = i - 4
-        for j in range(1, X):
-            to_x_early(n, j).wait_recv()
-            to_x_late(n, j).wait_recv()
-
-        @pl.when(n >= 2)
-        def _():
-            for j in range(1, Z):
-                to_z(n - 2, j).wait_send()
-
-        total = summed[n % 2, :, :, x].astype(F32) + total_of([from_x[n, j].astype(F32) for j in range(X - 1)])
-        column[n % 2] = total.astype(BF)
-        for j in range(1, Z):
-            to_z(n, j).start()
-
-    @pl.when(active(3))
-    def _():
-        n = i - 3
-        to_y(n).wait_recv()
-
-        @pl.when(n >= 2)
-        def _():
-            for j in range(1, X):
-                to_x_late(n - 2, j).wait_send()
-
-        total = (keep_y[n % 2].astype(F32) + from_y[n].astype(F32)).astype(BF)
-        summed[n % 2, 0] = total.reshape(summed.shape[2:])
-        for j in range(1, X):
-            to_x_late(n, j).start()
-
-    @pl.when(active(2))
-    def _():
-        n = i - 2
-        to_core(n).wait_recv()
-
-        @pl.when(n >= 2)
-        def _():
-            to_y(n - 2).wait_send()
-            for j in range(1, X):
-                to_x_early(n - 2, j).wait_send()
-
-        def both(t):
-            return (mine[t].astype(F32) + from_core[n % 2, t].astype(F32)).astype(BF)
-
-        send_y[n % 2] = both(1 - y)
-        to_y(n).start()
+    @pl.when(active(6))
+    def _():
+        n = i - 6
+        to_plane(n).wait_recv()
+        share(n, 2).wait_recv()
+        relay(n).start()
+        final_plane[n] = (plane[n].astype(F32) + from_plane[n].astype(F32)).astype(BF)
         for t in range(2):
-            summed[n % 2, 1 + t] = both(2 + t).reshape(summed.shape[2:])
-        for j in range(1, X):
-            to_x_early(n, j).start()
-        keep_y[n % 2] = both(y)
-
-        @pl.when(n < groups - 2)
-        def _():
-            pl.semaphore_signal(free, inc=1, device_id=core_peer, device_id_type=MESH)
-
-    @pl.when(i == 2)
-    def _():
-        down_mine.wait()
-        for j in range(1, X):
-            down_to_x(j).wait_recv()
-        for row in range(Z):
-            total = down_column[row].astype(F32) + total_of([down_from_x[j, row].astype(F32) for j in range(X - 1)])
-            down_column[row] = total.astype(BF)
-        for j in range(1, Z):
-            down_to_z(j).start()
+            keep(n, t + 1).start()
+            share_core(n, t).start()
 
     @pl.when(i == 4)
     def _():
-        for j in range(1, Z):
-            down_to_z(j).wait_recv()
-        total = down_column[z].astype(F32) + total_of([down_from_z[j].astype(F32) for j in range(Z - 1)])
+        down_load.wait()
+        for k in range(1, Z):
+            down_to_z(k).wait_recv()
+        total = down_mine[...].astype(F32) + total_of([down_from_z[k].astype(F32) for k in range(Z - 1)])
         down_final[...] = total.astype(BF)
         down_keep.start()
-        for d in range(1, 4):
+        for d in range(1, 3):
             down_share(d).start()
 
-    @pl.when(i < groups)
-    def _():
-        slot = i % 2
+    @pl.when(i == 6)
+    def _():
+        down_share(2).wait_recv()
+        down_relay().start()
+
+    @pl.when((i < subs) & (i % 2 == 0))
+    def _():
+        m = i // 2
+        slot = m % 2
         ones = head_ones(step, head_size)
         scale = 1.0 / math.sqrt(head_size)
         first = lax.broadcasted_iota(jnp.int32, (frames, step), 0) == 0
@@ -951,7 +1015,7 @@
                     query_grad.append(ds * keys[n])
                     key_grads[n].append(ds * queries[p])
                     value_grads[n].append(pr.astype(BF).astype(F32) * cots[p])
-                grads[slot, 0, p, rows, :] = total_of(query_grad).astype(BF)
+                grads[0, p, rows, :] = total_of(query_grad).astype(BF)
             for p in range(2):
                 terms_before[p, rows, :] = total_of(key_grads[p])
                 terms_before[2 + p, rows, :] = total_of(value_grads[p])
@@ -961,144 +1025,232 @@
 
         lax.fori_loop(0, frames // CHUNK, chunk, 0)
 
-        @pl.when((i >= 2) & (me > 0))
-        def _():
-            to_before(i - 2).wait_send()
-
-        for m in range(4):
-            kind, p = m // 2, m % 2
-            later = terms_before[m]
-            edge_send[slot, m : m + 1, :] = later[0:1, :]
-            total = terms_here[m] + jnp.where(last, 0.0, pltpu.roll(later, frames - 1, 0))
-            grads[slot, 1 + kind, p] = total.astype(BF)
-            tails[slot, m] = total[frames - 16 :, :]
+        @pl.when((m >= 2) & (me > 0))
+        def _():
+            to_before(m - 2).wait_send()
+
+        for row in range(4):
+            edge_send[slot, row : row + 1, :] = terms_before[row, 0:1, :]
 
         @pl.when(me > 0)
         def _():
-            to_before(i).start()
-
-    @pl.when(active(1))
-    def _():
-        n = i - 1
-        slot = n % 2
+            to_before(m).start()
+
+        for row in range(4):
+            total = terms_here[row] + jnp.where(last, 0.0, pltpu.roll(terms_before[row], frames - 1, 0))
+            grads[1 + row // 2, row % 2] = total.astype(BF)
+            tails[row] = total[frames - 16 :, :]
+
+    @pl.when((i < subs) & (i % 2 == 1))
+    def _():
+        m = i // 2
 
         @pl.when(me < devices - 1)
         def _():
-            to_before(n).wait_recv()
+            to_before(m).wait_recv()
 
         bottom = lax.broadcasted_iota(jnp.int32, (16, step), 0) == 15
-        for m in range(4):
-            fixed = tails[slot, m] + jnp.where(bottom, edge_recv[n, m : m + 1, :], 0.0)
-            grads[slot, 1 + m // 2, m % 2, frames - 16 :, :] = fixed.astype(BF)
-
-        @pl.when(n >= 1)
-        def _():
-            to_core(n - 1).wait_send()
+        for row in range(4):
+            fixed = tails[row] + jnp.where(bottom, edge_recv[m, row : row + 1, :], 0.0)
+            grads[1 + row // 2, row % 2, frames - 16 :, :] = fixed.astype(BF)
+
+        @pl.when(m >= 1)
+        def _():
+            for h in range(2):
+                to_core(2 * m - 2 + h).wait_send()
 
         for t in range(4):
             pair = []
             for p in range(2):
                 if t < 3:
-                    pair.append(tn(inputs[p], grads[slot, t, p]).astype(BF))
+                    pair.append(tn(inputs[p], grads[t, p]).astype(BF))
                 else:
-                    pair.append(tn(mixed[p], dhb[p, :, pl.ds(pl.multiple_of(n * step, step), step)]).astype(BF))
-            mine[t] = jnp.where(core == 0, pair[0], pair[1])
-            other[t] = jnp.where(core == 0, pair[1], pair[0])
-
-        @pl.when(n >= 2)
-        def _():
-            pl.semaphore_wait(free, 1)
-
-        to_core(n).start()
+                    pair.append(tn(mixed[p], dhb[p, :, pl.ds(pl.multiple_of(m * step, step), step)]).astype(BF))
+            here = jnp.where(core == 0, pair[0], pair[1])
+            there = jnp.where(core == 0, pair[1], pair[0])
+            for h in range(2):
+                mine[h, t] = here[:, h * thin : (h + 1) * thin]
+                other[h, t] = there[:, h * thin : (h + 1) * thin]
+
+        @pl.when(m >= slots // 2)
+        def _():
+            pl.semaphore_wait(free, 2)
+
+        for h in range(2):
+            to_core(2 * m + h).start()
         for p in range(2):
-            da[p] += total_of([nt(grads[slot, t, p], proj[0, t, p]) for t in range(3)])
-
-    @pl.when(i == groups + 5)
-    def _():
-        to_core(groups - 1).wait_send()
-        for n in (groups - 2, groups - 1):
-            @pl.when(me > 0)
-            def _():
+            da[p] += total_of([nt(grads[t, p], proj[0, t, p]) for t in range(3)])
+
+        @pl.when(m == groups - 1)
+        def _():
+            for g in range(groups):
+                load_frames(g).start()
+
+    @pl.when(i == subs)
+    def _():
+        for g in range(groups):
+            load_frames(g).wait()
+
+        def chunk(c, term):
+            rows = pl.ds(pl.multiple_of(c * CHUNK, CHUNK), CHUNK)
+            for p in range(2):
+                pieces = [grads[g, p, rows, :] if g < 3 else mixed_grad[p, rows, :] for g in range(groups)]
+                value = jnp.concatenate(pieces, axis=1).astype(F32)
+                inverse = scale_rows(value)
+                normed = value * inverse
+                grad = da[p, rows, :]
+                term = term + jnp.sum(grad * normed, axis=0, keepdims=True)
+                total = dhb[p, rows, :].astype(F32) + norm_back(grad, normed, gains[0:1, :], inverse)
+                frames_grad[p, rows, :] = total.astype(BF)
+            return term
+
+        term = lax.fori_loop(0, frames // CHUNK, chunk, jnp.zeros((1, da.shape[2]), F32))
+        gain_terms[0] = second_gain[...]
+        gain_terms[0, 0:1, :] = term
+        gain_copy(0, 0).start()
+
+    for level in range(1, 4):
+        @pl.when(i == subs + level)
+        def _():
+            count = X - 1 if level == 3 else 1
+            total = gain_terms[level - 1]
+            for n in range(count):
+                gain_copy(level - 1, n).wait()
+                total = total + gain_from[level - 1, n]
+            gain_terms[level] = total
+            for n in range(Z - 1 if level == 3 else X - 1 if level == 2 else 1):
+                gain_copy(level, n).start()
+
+    @pl.when(i == subs + 4)
+    def _():
+        total = gain_terms[3]
+        for n in range(Z - 1):
+            gain_copy(3, n).wait()
+            total = total + gain_from[3, n]
+        gains_sum[...] = total
+
+    @pl.when(i == subs + 5)
+    def _():
+        @pl.when(me > 0)
+        def _():
+            for n in (groups - 2, groups - 1):
                 to_before(n).wait_send()
 
-            to_y(n).wait_send()
+        for n in (subs - 3, subs - 2, subs - 1):
             for j in range(1, X):
                 to_x_early(n, j).wait_send()
                 to_x_late(n, j).wait_send()
+
+        for n in (subs - 2, subs - 1):
+            to_core(n).wait_send()
+            to_y(n).wait_send()
             for j in range(1, Z):
                 to_z(n, j).wait_send()
 
         def finish(n, carry):
             to_plane(n).wait_send()
             keep(n, 0).wait()
-            for d in range(1, 4):
-                share(n, d).wait()
+            share(n, 1).wait()
+            share(n, 2).wait_send()
+            relay(n).wait()
             for t in range(2):
                 keep(n, t + 1).wait()
                 share_core(n, t).wait()
             return carry
 
-        lax.fori_loop(0, groups, finish, 0)
-        for j in range(1, X):
-            down_to_x(j).wait_send()
-        for j in range(1, Z):
-            down_to_z(j).wait_send()
+        lax.fori_loop(0, subs, finish, 0)
+        out_copy.wait()
+        for k in range(1, Z):
+            down_to_z(k).wait_send()
         down_keep.wait()
-        for d in range(1, 4):
-            down_share(d).wait()
-        out_copy.wait()
-
-
-def attention_back(carried, qkv_rows, edge, attn, dhb, mixed, inputs, down_sum, out_send, head_size, fsdp_count):
+        down_share(1).wait()
+        down_share(2).wait_send()
+        down_relay().wait()
+
+
+def attention_back(
+    carried, qkv_rows, edge, attn, dhb, mixed, inputs, gains, second_gain, frames_in, down_in, out_send, head_size, fsdp_count
+):
     _, frames, width = dhb.shape
     step = STEP
     groups = width // step
     X = fsdp_count // Z
     R = width // fsdp_count
-    R2, half = down_sum.shape[2:]
 
     def early(i):
-        return jnp.minimum(i, groups - 1)
+        return jnp.minimum(i // 2, groups - 1)
 
     rows = [pl.BlockSpec((1, 2, frames, step), lambda i, t=t: (t, 0, 0, early(i))) for t in range(3)]
     edge_spec = pl.BlockSpec((1, 8, step), lambda i: (early(i), 0, 0))
     mask = pl.BlockSpec((frames, 1), lambda i: (0, 0), pipeline_mode=pl.Buffered(1))
     whole = pl.BlockSpec((2, frames, width), lambda i: (0, 0, 0), pipeline_mode=pl.Buffered(1))
     mix_spec = pl.BlockSpec((groups, 1, 2, step, step), lambda i: (0, 3, 0, early(i), 0))
-    proj_spec = pl.BlockSpec((1, 3, 2, width, step), lambda i: (jnp.clip(i - 1, 0, groups - 1), 0, 0, 0, 0))
+    proj_spec = pl.BlockSpec((1, 3, 2, width, step), lambda i: (jnp.clip((i - 1) // 2, 0, groups - 1), 0, 0, 0, 0))
+    line = pl.BlockSpec((8, width), lambda i: (0, 0), pipeline_mode=pl.Buffered(1))
     dma, vmem = pltpu.SemaphoreType.DMA, pltpu.VMEM
-    n = groups
+    thin = step // 2
+    n, slots, peers = 2 * groups, 4, max(X, Z) - 1
     return pl.pallas_call(
         functools.partial(attention_back_kernel, X, groups, head_size),
-        grid=(groups + 6,),
+        grid=(n + 6,),
         out_shape=(
-            jax.ShapeDtypeStruct((2, frames, width), F32),
+            jax.ShapeDtypeStruct((2, frames, width), BF),
+            jax.ShapeDtypeStruct((8, width), F32),
             jax.ShapeDtypeStruct((4, 2, R, width), BF),
-            jax.ShapeDtypeStruct((4, R2, half), BF),
+            jax.ShapeDtypeStruct((4,) + down_in.shape[1:], BF),
             jax.ShapeDtypeStruct(out_send.shape, BF),
         ),
-        in_specs=[mask, *rows, edge_spec, mix_spec, whole, whole, whole, proj_spec, ANY, ANY],
-        out_specs=(whole, ANY, ANY, ANY),
+        in_specs=[mask, *rows, edge_spec, mix_spec, whole, whole, whole, proj_spec, line, line, ANY, ANY, ANY],
+        out_specs=(whole, line, ANY, ANY, ANY),
         scratch_shapes=[
+            vmem((2, frames, width), F32), vmem((4, 8, width), F32), vmem((4, peers, 8, width), F32),
             vmem((2, frames, step), BF), vmem((4, frames, step), F32), vmem((4, frames, step), F32),
-            vmem((4, frames, step), F32), vmem((2, 4, 16, step), F32), vmem((2, 3, 2, frames, step), BF),
-            vmem((2, 8, step), F32), vmem((n, 8, step), F32),
-            vmem((4, width, step), BF), vmem((4, width, step), BF), vmem((2, 4, width, step), BF),
-            vmem((2, width, step), BF), vmem((2, width, step), BF), vmem((n, width, step), BF),
-            vmem((2, 3, Z, X, R, step), BF), vmem((n, X - 1, 3, Z, R, step), BF),
-            vmem((2, 3, Z, R, step), BF), vmem((n, Z - 1, 3, R, step), BF),
-            vmem((n, R, step), BF), vmem((n, 2, R, step), BF), vmem((n, 2, R, step), BF), vmem((n, 2, R, step), BF),
-            vmem((Z, R2, half), BF), vmem((X - 1, Z, R2, half), BF), vmem((Z - 1, R2, half), BF), vmem((R2, half), BF),
-            dma((2,)), dma((n,)), dma, dma((2,)), dma((2,)), dma((n,)),
-            dma((2, X - 1)), dma((n, X - 1)), dma((2, X - 1)), dma((n, X - 1)),
+            vmem((4, frames, step), F32), vmem((4, 16, step), F32), vmem((3, 2, frames, step), BF),
+            vmem((2, 8, step), F32), vmem((groups, 8, step), F32),
+            vmem((2, 4, width, thin), BF), vmem((2, 4, width, thin), BF), vmem((slots, 4, width, thin), BF),
+            vmem((2, width, thin), BF), vmem((2, width, thin), BF), vmem((n, width, thin), BF),
+            vmem((3, 3, Z, X, R, thin), BF), vmem((n, X - 1, 3, Z, R, thin), BF),
+            vmem((2, 3, Z, R, thin), BF), vmem((n, Z - 1, 3, R, thin), BF),
+            vmem((n, R, thin), BF), vmem((n, 2, R, thin), BF), vmem((n, 2, R, thin), BF), vmem((n, 2, R, thin), BF),
+            vmem(down_in.shape[1:], BF), vmem((Z - 1,) + down_in.shape[1:], BF), vmem(down_in.shape[1:], BF),
+            dma((2,)), dma((groups,)), dma((2,)), dma((slots,)), dma((2,)), dma((n,)),
+            dma((3, X - 1)), dma((n, X - 1)), dma((3, X - 1)), dma((n, X - 1)),
             dma((2, Z - 1)), dma((n, Z - 1)), dma((n, 3)), dma((n, 3)), dma((n,)), dma((n,)),
             dma((n, 2)), dma((n, 2)), dma((n, 3)),
-            dma((X - 1,)), dma((X - 1,)), dma((Z - 1,)), dma((Z - 1,)), dma((3,)), dma((3,)), dma((2,)),
-            dma, dma, pltpu.SemaphoreType.REGULAR,
+            dma, dma, dma((4, peers)), dma((4, peers)), dma((groups,)),
+            dma((Z - 1,)), dma((Z - 1,)), dma((3,)), dma((3,)), dma((2,)), pltpu.SemaphoreType.REGULAR,
         ],
         compiler_params=pltpu.CompilerParams(vmem_limit_bytes=63 * 2**20, collective_id=2, has_side_effects=True),
         name="attention_back",
-    )(carried, qkv_rows, qkv_rows, qkv_rows, edge, attn, dhb, mixed, inputs, attn, down_sum, out_send)
+    )(
+        carried, qkv_rows, qkv_rows, qkv_rows, edge, attn, dhb, mixed, inputs, attn,
+        gains, second_gain, frames_in, down_in, out_send,
+    )
+
+
+def update_kernel(step_size, share, weight, moment, average, grad_out, moment_out, average_out, weight_out):
+    gradient = share[...].reshape(weight.shape).astype(F32)
+    moment_new, average_new, weight_new = owner_update(
+        weight[...], gradient, moment[...], average[...], step_size
+    )
+    grad_out[...] = gradient
+    moment_out[...] = moment_new
+    average_out[...] = average_new
+    weight_out[...] = weight_new
+
+
+def update(shares, share_block, share_at, grid, block, at, weight, moment, average, step_size, name):
+    share_spec = pl.BlockSpec(share_block, share_at)
+    spec = pl.BlockSpec(block, at)
+    return pl.pallas_call(
+        functools.partial(update_kernel, step_size),
+        grid=grid,
+        out_shape=(jax.ShapeDtypeStruct(weight.shape, F32),) * 4,
+        in_specs=[share_spec, spec, spec, spec],
+        out_specs=(spec,) * 4,
+        compiler_params=pltpu.CompilerParams(vmem_limit_bytes=VMEM_BYTES),
+        name=name,
+    )(shares, weight, moment, average)
 
 
 def per_device(
@@ -1118,27 +1270,6 @@
     y, core = dp // 2, dp % 2
     z, x = fs // X, fs % X
     axes = ("dp", "fsdp")
-
-    def permute(value, target):
-        pairs = []
-        for d in range(dp_count):
-            for f in range(fsdp_count):
-                to = target(d, f)
-                if to is not None:
-                    pairs.append((d * fsdp_count + f, to[0] * fsdp_count + to[1]))
-        return lax.ppermute(value, axes, pairs)
-
-    def to_core(value):
-        return permute(value, lambda d, f: (d ^ 1, f))
-
-    def to_y(value):
-        return permute(value, lambda d, f: (d ^ 2, f))
-
-    def to_x(value, i):
-        return permute(value, lambda d, f: (d, (f // X) * X + (f % X + i) % X))
-
-    def to_z(value, k):
-        return permute(value, lambda d, f: (d, ((f // X + k) % Z) * X + f % X))
 
     device = dp * fsdp_count + fs
     padded_ids = jnp.concatenate([jnp.full((1,), -1, jnp.int32), segment_ids])
@@ -1172,14 +1303,11 @@
     attn, inner, down, gains, a, qkv_rows, mixed, edge, hres, b_rows, c_rows = forward(
         frames_by, carried, cot, attn_own, inner_own, down_own, gains_own, head_size, fsdp_count
     )
-    xf = frames_by.astype(F32)
-    r1 = scale_rows(xf)
-    n1 = xf * r1
     r2 = scale_rows(hres)
     n2 = hres * r2
     b_rows = b_rows.reshape(2 * frame_count, width)
     c_rows = c_rows.reshape(2 * frame_count, width)
-    out, back, out_there, back_there, inner_shares, down_sum = feed_forward(b_rows, c_rows, inner, down, fsdp_count)
+    out, back, out_there, back_there, inner_shares, down_columns, _ = feed_forward(b_rows, c_rows, inner, down, fsdp_count)
 
     def by_position(mine, theirs):
         return jnp.where(y == 0, jnp.stack([mine, theirs]), jnp.stack([theirs, mine]))
@@ -1189,47 +1317,37 @@
     e2 = jnp.sum(db * n2, axis=(0, 1))
     dh = cot.astype(F32) + norm_back(db, n2, gains[1], r2)
     dhb = dh.astype(BF)
-    down_sum = down_sum.reshape(Z, X, -1, half_width)
-    da, attn_shares, down_shares, out_here = attention_back(
-        carried, qkv_rows, edge, attn, dhb, mixed, a, down_sum, out_there, head_size, fsdp_count
+    second_gain = jnp.zeros((8, width), F32).at[1].set(e2)
+    frames_grad, gains_sum, attn_shares, down_shares, out_here = attention_back(
+        carried, qkv_rows, edge, attn, dhb, mixed, a, gains, second_gain, frames_by, down_columns, out_there, head_size, fsdp_count
     )
+    frames_grad = frames_grad.transpose(1, 0, 2)
     layer_out = (hres + by_position(out, out_here.astype(F32))).astype(BF).transpose(1, 0, 2)
-    e1 = jnp.sum(da * n1, axis=(0, 1))
-    frames_grad = (dh + norm_back(da, n1, gains[0], r1)).astype(BF).transpose(1, 0, 2)
-
-    inner_grad = inner_shares.reshape((2, 2) + inner_shares.shape[1:])
-    inner_grad = jnp.concatenate([inner_grad[:, 0], inner_grad[:, 1]], axis=-1).astype(F32)
-    down_grad = down_shares.reshape((2, 2) + down_shares.shape[1:])
-    down_grad = jnp.concatenate([down_grad[:, 0], down_grad[:, 1]], axis=-1).astype(F32)
-    qkv_grad = jnp.concatenate([attn_shares[0], attn_shares[1], attn_shares[2]], axis=-1).astype(F32)
-    mix_grad = attn_shares[3].astype(F32)
-
-    gains_part = jnp.stack([e1, e2])
-    gains_part = gains_part + to_core(gains_part)
-    gains_part = gains_part + to_y(gains_part)
-    gains_grid = gains_part.reshape(2, Z, X, -1).transpose(1, 2, 0, 3)
-    column = lax.dynamic_index_in_dim(gains_grid, x, 1, keepdims=False)
-    for i in range(1, X):
-        column = column + to_x(lax.dynamic_index_in_dim(gains_grid, lax.rem(x + i, X), 1, keepdims=False), i)
-    gains_grad = lax.dynamic_index_in_dim(column, z, 0, keepdims=False)
-    for kk in range(1, Z):
-        gains_grad = gains_grad + to_z(lax.dynamic_index_in_dim(column, lax.rem(z + kk, Z), 0, keepdims=False), kk)
 
     step_size = step_rate / math.sqrt(total_frames)
-    grads = (qkv_grad, mix_grad, inner_grad, down_grad, gains_grad)
-    new = [
-        owner_update(w, g, m, av, step_size)
-        for w, g, m, av in zip(
-            (qkv_weight, mix_weight, inner_weight, down_weight, norm_gains),
-            grads,
-            (qkv_moment, mix_moment, inner_moment, down_moment, gains_moment),
-            (qkv_average, mix_average, inner_average, down_average, gains_average),
-        )
-    ]
-    return (
-        (layer_out, frames_grad) + grads
-        + tuple(n[0] for n in new) + tuple(n[1] for n in new) + tuple(n[2] for n in new)
+    R, R2 = qkv_weight.shape[1], down_weight.shape[1]
+    cut = min(R, 64)
+    qkv_new = update(
+        attn_shares, (1, 1, R, width), lambda p, t: (t, p, 0, 0), (2, 3), (1, R, width), lambda p, t: (p, 0, t),
+        qkv_weight, qkv_moment, qkv_average, step_size, "update_qkv",
     )
+    mix_new = update(
+        attn_shares, (1, 1, R, width), lambda p: (3, p, 0, 0), (2,), (1, R, width), lambda p: (p, 0, 0),
+        mix_weight, mix_moment, mix_average, step_size, "update_mix",
+    )
+    inner_new = update(
+        inner_shares, (1, cut, hidden), lambda p, c, r: (2 * p + c, r, 0), (2, 2, R // cut),
+        (1, cut, hidden), lambda p, c, r: (p, r, c), inner_weight, inner_moment, inner_average, step_size, "update_inner",
+    )
+    down_new = update(
+        down_shares, (1, R2, half_width), lambda p, c: (2 * p + c, 0, 0), (2, 2),
+        (1, R2, half_width), lambda p, c: (p, 0, c), down_weight, down_moment, down_average, step_size, "update_down",
+    )
+    own = norm_gains.shape[1]
+    gains_grad = lax.dynamic_slice(gains_sum, (0, fs * own), (2, own))
+    gains_new = (gains_grad,) + owner_update(norm_gains, gains_grad, gains_moment, gains_average, step_size)
+    new = (qkv_new, mix_new, inner_new, down_new, gains_new)
+    return (layer_out, frames_grad) + tuple(n[kind] for kind in range(4) for n in new)
 
 
 def solution(mesh):

time: 605 us -> 565 us (0.934)
  other arithmetic: 65.5 us -> 13.4 us
  Pallas kernels: 472 us -> 509 us
  starting transfers between devices: 19.3 us -> 0 us
    pallas_call x0 -> x4, Pallas kernels: none -> 37.9 us  [update(): pl.pallas_call(functools.partial(update_kernel, step_size), grid=grid, ou...]
    add x5 -> x1, other arithmetic: 36.5 us -> 1.26 us  [owner_update(): average_new = average_rate * average + (1.0 - average_rate) * weight_new]
    pallas_call x1, Pallas kernels: 131 us -> 152 us  [feed_forward(): pl.pallas_call(functools.partial(feed_forward_kernel, X, J), grid=(J + 3,...]
    pallas_call x1, Pallas kernels: 161 us -> 141 us  [attention_back(): pl.pallas_call(functools.partial(attention_back_kernel, X, groups, head_s...]
    ppermute x6 -> x0, starting transfers between devices: 19.3 us -> none  [permute(): return lax.ppermute(value, axes, pairs)]
    squeeze x3 -> x0, local copies, waits for them, and re-layouts: 7.3 us -> none  [the longest x1 3.71 us: per_device(): inner_grad[:, 0]]
    transpose x1, other arithmetic: 7.88 us -> 1.13 us  [per_device(): (hres + by_position(out, out_here.astype(F32))).astype(BF)]
    unnamed x68 -> x36, local copies, waits for them, and re-layouts: 13.7 us -> 16.4 us
  transfers between devices with their start and end apart: 6 -> 0, of which waited for: 1 -> 0; matrix products, arithmetic and copies ran while one was open for 10% -> 0% of each run, Pallas kernels for 0% -> 0%
where the time goes in v4:
time: 565 us; the launch traced here: 557 us
  Pallas kernels  509 us (90%)
  local copies, waits for them, and re-layouts  33.5 us (6%)
  other arithmetic  13.4 us (2%)
    pallas_call x1, Pallas kernels, forward(): pl.pallas_call(functools.partial(forward_kernel, X, groups, head_size), o...  179 us
    pallas_call x1, Pallas kernels, feed_forward(): pl.pallas_call(functools.partial(feed_forward_kernel, X, J), grid=(J + 3,...  152 us
    pallas_call x1, Pallas kernels, attention_back(): pl.pallas_call(functools.partial(attention_back_kernel, X, groups, head_s...  141 us
    pallas_call x4, Pallas kernels, update(): pl.pallas_call(functools.partial(update_kernel, step_size), grid=grid, ou...  37.9 us
    unnamed x36, local copies, waits for them, and re-layouts  16.4 us

profile of v4, /device:TPU:0, one launch (start us, length us, event | category | flops | bytes accessed | tf_op | source)
XLA Modules:
  0.0 557.1 jit_solution(17820916343464106225)
XLA Ops:
  0.7 0.9 fusion.7
  2.3 1.2 convert_dynamic-update-slice_fusion.gains_own
  3.6 1.0 slice.64
  4.6 0.8 copy.65
  5.3 0.9 copy.55.carried
  6.2 1.9 fusion.4.down_own
  8.1 1.2 slice.61
  9.2 0.9 copy.62
  11.1 1.0 copy.66
  12.9 2.3 fusion.3.inner_own
  15.2 1.0 fusion.9
  16.2 1.3 copy.60
  17.5 1.4 copy.61
  18.9 0.9 copy.59
  19.8 1.1 select_convert_fusion
  20.9 1.1 copy.54
  22.0 4.9 copy_bitcast_fusion
  27.0 178.7 %attention_forward.1 = (bf16[4,4,2,1024,256]{4,3,2,1,0:T(8,128)(2,1)}, bf16[2,1024,2816]{2,1,0:T(8,128)(2,1)}, bf16[2,2816,512]{2,1,0:T(8,128)(2,1)}, f32[8,1024...) custom-call(bf16[2,512,1024]{2,1,0:T(8,128)(2,1)} %get-tuple-element, ...), custom_call_target="tpu_custom_call" | custom-call | tf_op jit(solution)/shard_map/attention_forward/pallas_call | solution.py:451
  205.6 151.5 %feed_forward.1 = (f32[512,1024]{1,0:T(8,128)}, f32[512,1024]{1,0:T(8,128)}, bf16[512,1024]{1,0:T(8,128)(2,1)}, bf16[512,1024]{1,0:T(8,128)(2,1)}, bf16[4,128,28...) custom-call(bf16[1024,1024]{1,0:T(8,128)(2,1)} %bitcast.38, ...), custom_call_target="tpu_custom_call" | custom-call | flops 53150220288 | bytes 62914560 | tf_op jit(solution)/shard_map/feed_forward/pallas_call | solution.py:718
  357.2 0.9 slice.66
  358.0 2.7 multiply_reduce_fusion.2
  362.2 1.4 multiply_reduce_fusion
  363.7 2.3 add_convert_fusion.dhb
  366.5 141.0 %attention_back.1 = (bf16[2,512,1024]{2,1,0:T(8,128)(2,1)}, f32[8,1024]{1,0:T(8,128)}, bf16[4,2,128,1024]{3,2,1,0:T(8,128)(2,1)}, bf16[4,352,512]{2,1,0:T(8,128)(2,1)}, bf16[512,1024]{1,0:T(8,128)(2,1)}) custom-call(f32[512,1]{1,0:T(8,128)} %copy.55.carried, bf16[3,2,512,1024]{3,2,1,0:T(8,128)(2,1)} %get-tuple-element.78.q.k.v, ...), custom_call_target="tpu_custom_call" | custom-call | tf_op jit(solution)/shard_map/attention_back/pallas_call | solution.py:1193
  507.7 5.2 copy.58
  512.9 1.3 add_multiply_fusion
  514.4 1.1 fusion.2
  515.5 3.5 copy.57
  519.0 3.5 update_mix.1
  522.6 9.8 %update_qkv.1 = (f32[2,128,3072]{2,1,0:T(8,128)}, f32[2,128,3072]{2,1,0:T(8,128)}, f32[2,128,3072]{2,1,0:T(8,128)}, f32[2,128,3072]{2,1,0:T(8,128)}) custom-call(bf16[4,2,128,1024]{3,2,1,0:T(8,128)(2,1)} %get-tuple-element.90.share, f32[2,128,3072]{2,1,0:T(8,128)} %weight.4, f32[2,128,3072]{2,1,0:T(8,128)} %moment.4, f32[2,128,3072]{2,1,0:T(8,128)} %average.4), custom_call_target="tpu_custom_call" | custom-call | tf_op jit(solution)/shard_map/update_qkv/pallas_call | solution.py:1245
  532.4 8.3 %update_down.1 = (f32[2,352,1024]{2,1,0:T(8,128)}, f32[2,352,1024]{2,1,0:T(8,128)}, f32[2,352,1024]{2,1,0:T(8,128)}, f32[2,352,1024]{2,1,0:T(8,128)}) custom-call(bf16[4,352,512]{2,1,0:T(8,128)(2,1)} %get-tuple-element.95.share, f32[2,352,1024]{2,1,0:T(8,128)} %weight.7, f32[2,352,1024]{2,1,0:T(8,128)} %moment.7, f32[2,352,1024]{2,1,0:T(8,128)} %average.7), custom_call_target="tpu_custom_call" | custom-call | tf_op jit(solution)/shard_map/update_down/pallas_call | solution.py:1245
  540.7 16.2 %update_inner.1 = (f32[2,128,5632]{2,1,0:T(8,128)}, f32[2,128,5632]{2,1,0:T(8,128)}, f32[2,128,5632]{2,1,0:T(8,128)}, f32[2,128,5632]{2,1,0:T(8,128)}) custom-call(bf16[4,128,2816]{2,1,0:T(8,128)(2,1)} %get-tuple-element.93.share, f32[2,128,5632]{2,1,0:T(8,128)} %weight.6, f32[2,128,5632]{2,1,0:T(8,128)} %moment.6, f32[2,128,5632]{2,1,0:T(8,128)} %average.6), custom_call_target="tpu_custom_call" | custom-call | tf_op jit(solution)/shard_map/update_inner/pallas_call | solution.py:1245
  (38 shorter events, 4.8 us)
Async XLA Ops:
  0.7 9.5 %copy-start.4 = (f32[2,128,3072]{2,1,0:T(8,128)S(1)}, f32[2,128,3072]{2,1,0:T(8,128)}, u32[]{:S(2)}) copy-start(f32[2,128,3072]{2,1,0:T(8,128)} %weight.4) | copy-start | bytes 9437188
  16.2 4.6 copy-start.8
  16.2 4.7 copy-start.9
  17.5 4.5 copy-start.2
  357.2 3.6 copy-start.7
  358.0 3.5 copy-start
  358.0 4.2 copy-start.3
  507.6 5.3 copy-start.10
  507.6 5.3 copy-start.11
  507.6 5.3 copy-start.12
  507.6 6.5 %copy-start.6 = (bf16[512,1024]{1,0:T(8,128)(2,1)S(1)}, bf16[512,1024]{1,0:T(8,128)(2,1)}, u32[]{:S(2)}) copy-start(bf16[512,1024]{1,0:T(8,128)(2,1)} %get-tuple-element.88) | copy-start | bytes 3145732
  507.6 6.8 %copy-start.1 = (f32[2,512,1024]{2,1,0:T(8,128)S(1)}, f32[2,512,1024]{2,1,0:T(8,128)}, u32[]{:S(2)}) copy-start(f32[2,512,1024]{2,1,0:T(8,128)} %get-tuple-element.72) | copy-start | bytes 12582916
  507.6 6.8 %copy-start.5 = (f32[512,1024]{1,0:T(8,128)S(1)}, f32[512,1024]{1,0:T(8,128)}, u32[]{:S(2)}) copy-start(f32[512,1024]{1,0:T(8,128)} %get-tuple-element.77) | copy-start | bytes 6291460

commit v5 on v4

--- a/solution.py
+++ b/solution.py
@@ -91,11 +91,12 @@
 
 
 def forward_kernel(
-    X, groups, head_size, frames, carried, cot, attn_own, inner_own, down_own, gains_own,
+    X, groups, head_size, frames, carried, cot, gains_own, qkv_weight, mix_weight, inner_weight, down_weight,
     attn, inner, down, gains_out, inputs_out, rows_out, mixed_out, edge_out, hres_out, b_rows, c_rows,
+    attn_wide, inner_wide, down_wide, attn_own, inner_own, down_own,
     gains, inputs, rows_in, mixed, before, hres, b, proj, mix, edge_send, edge_recv,
     send_up, recv_up, send_down, recv_down, send_x, recv_x, send_y, recv_y, send_c, recv_c, send_r, recv_r,
-    send_g, recv_g, send_e, recv_e, send_b, recv_b, send_q, recv_q, local_sem, out_sem,
+    send_g, recv_g, send_e, recv_e, send_b, recv_b, send_q, recv_q, local_sem, out_sem, wide_sem,
 ):
     dp, fs = lax.axis_index("dp"), lax.axis_index("fsdp")
     F = Z * X
@@ -119,8 +120,43 @@
 
     UNITS = unit_list(groups, inner_own.shape[1], down_own.shape[1])
 
+    width = frames.shape[2]
+
+    def wide(slot):
+        return (attn_wide.at[slot] if slot < groups + 1 else (inner_wide, down_wide)[slot - groups - 1])
+
+    def fetch(slot, src, condition=None):
+        copy = pltpu.make_async_copy(src, wide(slot), wide_sem.at[slot])
+        if condition is None:
+            copy.start()
+        else:
+            pl.when(condition)(copy.start)
+
+    def columns_of(weight, part, block):
+        return weight.at[:, :, pl.ds(pl.multiple_of(part * width + block * STEP, STEP), STEP)]
+
+    def fetch_all():
+        for n in range(groups - 1):
+            fetch(n, columns_of(qkv_weight, jnp.minimum(dp, 2), n), dp < 3)
+            fetch(n, columns_of(mix_weight, 0, n), dp == 3)
+        fetch(groups - 1, columns_of(qkv_weight, core, groups - 1))
+        fetch(groups, columns_of(qkv_weight, 2, groups - 1), core == 0)
+        fetch(groups, columns_of(mix_weight, 0, groups - 1), core == 1)
+        half, hidden = width // 2, inner_own.shape[1]
+        fetch(groups + 1, inner_weight.at[y, :, pl.ds(pl.multiple_of(core * hidden, 128), hidden)])
+        fetch(groups + 2, down_weight.at[y, :, pl.ds(pl.multiple_of(core * half, 128), half)])
+
+    def take(slot):
+        pltpu.make_async_copy(wide(slot), wide(slot), wide_sem.at[slot]).wait()
+        if slot < groups + 1:
+            attn_own[slot] = attn_wide[slot].astype(BF)
+        elif slot == groups + 1:
+            inner_own[...] = inner_wide[...].astype(BF)
+        else:
+            down_own[...] = down_wide[...].astype(BF)
+
     def own(u):
-        kind, n, columns = UNITS[u]
+        kind, n, columns = UNITS[u][:3]
         if kind in ("quarter", "low", "high"):
             return attn_own.at[n if kind != "high" else n + 1]
         return (down_own if kind == "down" else inner_own).at[:, columns]
@@ -132,7 +168,7 @@
         return 2 + core_index if kind == "high" else core_index
 
     def whole(u, part):
-        kind, n, columns = UNITS[u]
+        kind, n, columns = UNITS[u][:3]
         if kind == "down":
             return down.at[part, :, columns]
         if kind == "inner":
@@ -140,7 +176,7 @@
         return attn.at[n, part]
 
     def place(u, source, part=None):
-        kind, n, columns = UNITS[u]
+        kind, n, columns = UNITS[u][:3]
         part = part_of(u, core, y) if part is None else part
         if kind == "down":
             R = down_own.shape[0]
@@ -151,6 +187,7 @@
         R = attn_own.shape[2]
         return attn.at[n, part, :, pl.ds(source * R, R), :]
 
+    fetch_all()
     barrier = pltpu.get_barrier_semaphore()
     peers = [z_peer(k) for k in range(1, Z)] + [x_peer(i) for i in range(1, X)]
     peers += [core_peer, y_peer, before_me, after_me]
@@ -201,7 +238,15 @@
                 lambda: (src(), place(u, source()), send_y.at[u, source()], recv_y.at[u, source()], y_peer),
             )
 
-    def start_unit(u):
+    def crossed(u):
+        return UNITS[u][3]
+
+    def block(u, row):
+        kind, n, columns = UNITS[u][:3]
+        array, R = (down, down_own.shape[0]) if kind == "down" else (inner, inner_own.shape[0])
+        return array.at[core, pl.ds(row * X * R, X * R), columns]
+
+    def send_along(u, src, dst):
         def below_top():
             return z < Z - 1
 
@@ -209,20 +254,33 @@
             return z > 0
 
         def upward():
-            return (own(u), place(u, fs), send_up.at[u, 1], recv_up.at[u, 1], up_peer)
+            return (src(), dst(), send_up.at[u, 1], recv_up.at[u, 1], up_peer)
 
         def downward():
-            return (own(u), place(u, fs), send_down.at[u, 1], recv_down.at[u, 1], down_peer)
+            return (src(), dst(), send_down.at[u, 1], recv_down.at[u, 1], down_peer)
 
         pl.when(below_top())(lambda: send(below_top, upward))
         pl.when(above_bottom())(lambda: send(above_bottom, downward))
+
+    def start_unit(u):
+        for slot in slots_of[u]:
+            take(slot)
+        if not crossed(u):
+            send_along(u, lambda: own(u), lambda: place(u, fs))
         spread(u, lambda: z, True, None)
         store(own(u), place(u, fs))
+
+    def turn(u):
+        for i in range(1, X):
+            column = lax.rem(x - i + X, X)
+            wait_recv(place(u, z * X + column), recv_x.at[u, z, i], send_x.at[u, z, i])
+        local[own_store[u]].wait()
+        send_along(u, lambda: block(u, z), lambda: block(u, z))
 
     def hop(u, k):
         def side(reached, row, further, send_sem, recv_sem, peer):
             def here():
-                return place(u, row() * X + x)
+                return block(u, row()) if crossed(u) else place(u, row() * X + x)
 
             def both():
                 return reached() & further()
@@ -235,7 +293,8 @@
                             both, lambda: (here(), here(), send_sem.at[u, k + 1], recv_sem.at[u, k + 1], peer)
                         )
                     )
-                spread(u, row, False, reached)
+                if not crossed(u):
+                    spread(u, row, False, reached)
 
             pl.when(reached())(action)
 
@@ -243,13 +302,14 @@
         side(lambda: z + k < Z, lambda: z + k, lambda: z > 0, send_down, recv_down, down_peer)
 
     def arrivals(u):
-        for row in range(Z):
+        for row in range(0 if crossed(u) else Z):
             for i in range(1, X):
                 column = lax.rem(x - i + X, X)
                 source = row * X + column
                 wait_recv(place(u, source), recv_x.at[u, row, i], send_x.at[u, row, i])
                 to_plane(u, lambda source=source: source, lambda source=source: place(u, source), None)
-        local[own_store[u]].wait()
+        if not crossed(u):
+            local[own_store[u]].wait()
         mine = whole(u, part_of(u, core, y))
         send(None, lambda: (mine, mine, send_c.at[u], recv_c.at[u], core_peer))
 
@@ -380,6 +440,11 @@
     def _():
         edge_recv[...] = jnp.zeros_like(edge_recv)
 
+    slots_of = [
+        [n] if kind in ("quarter", "low") else [n + 1] if kind == "high" else [] for kind, n, *_ in UNITS
+    ]
+    slots_of[[u[0] for u in UNITS].index("inner")] = [groups + 1]
+    slots_of[[u[0] for u in UNITS].index("down")] = [groups + 2]
     own_store = {}
     last_of = {kind_n[1]: u for u, kind_n in enumerate(UNITS) if kind_n[0] in ("quarter", "low", "high")}
     last_plane = max(u for u, kind_n in enumerate(UNITS) if kind_n[0] == "quarter")
@@ -389,9 +454,15 @@
         if tick < len(UNITS):
             own_store[tick] = len(local)
             start_unit(tick)
+        if 0 <= tick - 1 < len(UNITS) and crossed(tick - 1):
+            turn(tick - 1)
         for k in range(1, Z):
-            if 0 <= tick - k < len(UNITS):
-                hop(tick - k, k)
+            u = tick - k
+            if 0 <= u < len(UNITS) and not crossed(u):
+                hop(u, k)
+            u = tick - k - 1
+            if 0 <= u < len(UNITS) and crossed(u):
+                hop(u, k)
         if tick == 1:
             pass_gains()
         if tick == 2:
@@ -431,20 +502,23 @@
 
 
 def unit_list(groups, inner_width, down_width):
-    units = [("quarter", n, None) for n in range(groups - 1)]
-    units += [("low", groups - 1, None), ("high", groups - 1, None)]
-    units += [("down", 0, slice(0, down_width // 2)), ("down", 0, slice(down_width // 2, down_width))]
+    units = [("quarter", n, None, False) for n in range(groups - 1)]
+    units += [("low", groups - 1, None, False), ("high", groups - 1, None, False)]
+    units += [("down", 0, slice(0, down_width // 2), True), ("down", 0, slice(down_width // 2, down_width), False)]
     tiles = inner_width // 128
     cuts = [128 * (tiles * n // 4) for n in range(5)]
-    return units + [("inner", 0, slice(lo, hi)) for lo, hi in zip(cuts, cuts[1:])]
-
-
-def forward(frames, carried, cot, attn_own, inner_own, down_own, gains_own, head_size, fsdp_count):
+    return units + [("inner", 0, slice(lo, hi), n == 1) for n, (lo, hi) in enumerate(zip(cuts, cuts[1:]))]
+
+
+def forward(
+    frames, carried, cot, gains_own, qkv_weight, mix_weight, inner_weight, down_weight, head_size, fsdp_count
+):
     X = fsdp_count // Z
     _, count, width = frames.shape
-    _, _, R, _ = attn_own.shape
+    R, R2 = qkv_weight.shape[1], down_weight.shape[1]
+    hidden, half = inner_weight.shape[2] // 2, width // 2
     groups = width // STEP
-    units = len(unit_list(groups, inner_own.shape[1], down_own.shape[1]))
+    units = len(unit_list(groups, hidden, half))
     dma, vmem = pltpu.SemaphoreType.DMA, pltpu.VMEM
     whole = pl.BlockSpec(memory_space=pltpu.VMEM)
     act = jax.ShapeDtypeStruct((2, count, width), BF)
@@ -452,8 +526,8 @@
         functools.partial(forward_kernel, X, groups, head_size),
         out_shape=(
             jax.ShapeDtypeStruct((groups, 4, 2, R * fsdp_count, STEP), BF),
-            jax.ShapeDtypeStruct((2, inner_own.shape[0] * fsdp_count, inner_own.shape[1]), BF),
-            jax.ShapeDtypeStruct((2, down_own.shape[0] * fsdp_count, down_own.shape[1]), BF),
+            jax.ShapeDtypeStruct((2, R * fsdp_count, hidden), BF),
+            jax.ShapeDtypeStruct((2, R2 * fsdp_count, half), BF),
             jax.ShapeDtypeStruct(gains_own.shape, F32),
             act,
             jax.ShapeDtypeStruct((3, 2, count, width), BF),
@@ -463,9 +537,11 @@
             act,
             act,
         ),
-        in_specs=[whole] * 7,
+        in_specs=[whole] * 4 + [ANY] * 4,
         out_specs=(ANY,) * 3 + (whole,) + (ANY,) * 7,
         scratch_shapes=[
+            vmem((groups + 1, 2, R, STEP), F32), vmem((R, hidden), F32), vmem((R2, half), F32),
+            vmem((groups + 1, 2, R, STEP), BF), vmem((R, hidden), BF), vmem((R2, half), BF),
             vmem((fsdp_count,) + gains_own.shape, F32),
             vmem((2, count, width), BF), vmem((3, 2, count, width), BF), vmem((2, count, width), BF),
             vmem((4, count, STEP), F32), vmem((2, count, width), F32), vmem((2, count, width), BF),
@@ -475,13 +551,13 @@
             dma((units, Z, X)), dma((units, Z, X)), dma((groups, fsdp_count)), dma((groups, fsdp_count)),
             dma((units,)), dma((units,)), dma((groups,)), dma((groups,)),
             dma((X, Z)), dma((X, Z)), dma((groups,)), dma((groups,)), dma, dma, dma, dma,
-            dma((2,)), dma((units + 8,)),
+            dma((2,)), dma((units + 8,)), dma((groups + 3,)),
         ],
         compiler_params=pltpu.CompilerParams(
             vmem_limit_bytes=VMEM_BYTES, collective_id=0, has_side_effects=True
         ),
         name="attention_forward",
-    )(frames, carried, cot, attn_own, inner_own, down_own, gains_own)
+    )(frames, carried, cot, gains_own, qkv_weight, mix_weight, inner_weight, down_weight)
 
 
 def feed_forward_kernel(
@@ -617,7 +693,7 @@
             to_z(n, k).start()
 
     for g in range(Z):
-        @pl.when(j == ends[g] + 3)
+        @pl.when(j == min(ends[g] + 4, J + 2))
         def _():
             down_load(g).wait()
             for i in range(1, X):
@@ -1276,32 +1352,13 @@
     window = lax.dynamic_slice_in_dim(padded_ids, device * frame_count, frame_count + 1)
     carried = (window[1:] == window[:-1]).astype(F32)[:, None]
 
-    quarters = (
-        qkv_weight[:, :, :width], qkv_weight[:, :, width : 2 * width], qkv_weight[:, :, 2 * width :], mix_weight
-    )
-    last = width - STEP
-    own_rows = jnp.concatenate(
-        [
-            lax.select_n(dp, *(m[:, :, :last] for m in quarters)),
-            lax.select_n(core > 0, *(m[:, :, last:] for m in quarters[:2])),
-            lax.select_n(core > 0, *(m[:, :, last:] for m in quarters[2:])),
-        ],
-        axis=-1,
-    ).astype(BF)
-    attn_own = own_rows.reshape(positions, -1, width // STEP + 1, STEP).transpose(2, 0, 1, 3)
-    inner_own = lax.dynamic_slice(
-        inner_weight, (y, 0, core * hidden), (1, inner_weight.shape[1], hidden)
-    )[0].astype(BF)
     half_width = width // 2
-    down_own = lax.dynamic_slice(
-        down_weight, (y, 0, core * half_width), (1, down_weight.shape[1], half_width)
-    )[0].astype(BF)
     own_gains = norm_gains.astype(BF).astype(F32)
     gains_own = lax.dynamic_update_slice(jnp.zeros((8, width), F32), own_gains, (0, fs * own_gains.shape[1]))
     frames_by = frames.transpose(1, 0, 2)
     cot = cotangent.transpose(1, 0, 2)
     attn, inner, down, gains, a, qkv_rows, mixed, edge, hres, b_rows, c_rows = forward(
-        frames_by, carried, cot, attn_own, inner_own, down_own, gains_own, head_size, fsdp_count
+        frames_by, carried, cot, gains_own, qkv_weight, mix_weight, inner_weight, down_weight, head_size, fsdp_count
     )
     r2 = scale_rows(hres)
     n2 = hres * r2

time: 565 us -> 546 us (0.966)
  local copies, waits for them, and re-layouts: 33.5 us -> 16.8 us
    pallas_call x1, Pallas kernels: 152 us -> 143 us  [feed_forward(): pl.pallas_call(functools.partial(feed_forward_kernel, X, J), grid=(J + 3,...]
    unnamed x36 -> x20, local copies, waits for them, and re-layouts: 16.4 us -> 8.84 us
    pallas_call x1, Pallas kernels: 179 us -> 185 us  [forward(): pl.pallas_call(functools.partial(forward_kernel, X, groups, head_size), o...]
where the time goes in v5:
time: 546 us; the launch traced here: 538 us
  Pallas kernels  506 us (93%)
  local copies, waits for them, and re-layouts  16.8 us (3%)
  other arithmetic  13.6 us (2%)
    pallas_call x1, Pallas kernels, forward(): pl.pallas_call(functools.partial(forward_kernel, X, groups, head_size), o...  185 us
    pallas_call x1, Pallas kernels, feed_forward(): pl.pallas_call(functools.partial(feed_forward_kernel, X, J), grid=(J + 3,...  143 us
    pallas_call x1, Pallas kernels, attention_back(): pl.pallas_call(functools.partial(attention_back_kernel, X, groups, head_s...  140 us
    pallas_call x4, Pallas kernels, update(): pl.pallas_call(functools.partial(update_kernel, step_size), grid=grid, ou...  37.9 us

profile of v5, /device:TPU:0, one launch (start us, length us, event | category | flops | bytes accessed | tf_op | source)
XLA Modules:
  0.0 537.7 jit_solution(11273094925410533513)
XLA Ops:
  0.7 0.8 fusion.5
  1.5 0.1 fusion.6
  1.5 0.7 convert_dynamic-update-slice_fusion.gains_own
  2.2 0.9 copy.46.carried
  3.1 5.5 %copy_bitcast_fusion = (bf16[2,512,1024]{2,1,0:T(8,128)(2,1)}, bf16[2,512,1024]{2,1,0:T(8,128)(2,1)}) fusion(bf16[512,2,1024]{2,1,0:T(2,128)(2,1)} %param.21, bf16[512,2,1024]{2,1,0:T(2,128)(2,1)} %param.20), kind=kLoop, calls=%fused_computation.9 | loop fusion | bytes 8388608 | tf_op jit(solution)/shard_map/transpose | solution.py:1359
  8.6 0.0 copy-done.5
  8.6 184.6 %attention_forward.1 = (bf16[4,4,2,1024,256]{4,3,2,1,0:T(8,128)(2,1)}, bf16[2,1024,2816]{2,1,0:T(8,128)(2,1)}, bf16[2,2816,512]{2,1,0:T(8,128)(2,1)}, f32[8,1024...) custom-call(bf16[2,512,1024]{2,1,0:T(8,128)(2,1)} %get-tuple-element, ...), custom_call_target="tpu_custom_call" | custom-call | tf_op jit(solution)/shard_map/attention_forward/pallas_call | solution.py:525
  193.3 143.1 %feed_forward.1 = (f32[512,1024]{1,0:T(8,128)}, f32[512,1024]{1,0:T(8,128)}, bf16[512,1024]{1,0:T(8,128)(2,1)}, bf16[512,1024]{1,0:T(8,128)(2,1)}, bf16[4,128,28...) custom-call(bf16[1024,1024]{1,0:T(8,128)(2,1)} %bitcast.30, ...), custom_call_target="tpu_custom_call" | custom-call | flops 53150220288 | bytes 62914560 | tf_op jit(solution)/shard_map/feed_forward/pallas_call | solution.py:794
  336.4 0.0 copy-start
  336.4 0.0 copy-start.3
  336.4 0.9 slice.25
  337.3 3.0 multiply_reduce_fusion.2
  340.4 1.5 bitcast_convert_fusion.1
  341.8 0.0 copy-done
  341.8 0.0 copy-done.3
  341.9 0.0 copy-start.2
  341.9 1.5 multiply_reduce_fusion
  343.3 0.1 copy-done.2
  343.4 2.2 add_convert_fusion.dhb
  345.7 0.6 scatter.4.second_gain
  346.3 140.4 %attention_back.1 = (bf16[2,512,1024]{2,1,0:T(8,128)(2,1)}, f32[8,1024]{1,0:T(8,128)}, bf16[4,2,128,1024]{3,2,1,0:T(8,128)(2,1)}, bf16[4,352,512]{2,1,0:T(8,128)(2,1)}, bf16[512,1024]{1,0:T(8,128)(2,1)}) custom-call(f32[512,1]{1,0:T(8,128)} %copy.46.carried, bf16[3,2,512,1024]{3,2,1,0:T(8,128)(2,1)} %get-tuple-element.78.q.k.v, ...), custom_call_target="tpu_custom_call" | custom-call | tf_op jit(solution)/shard_map/attention_back/pallas_call | solution.py:1269
  486.7 5.2 copy.49
  491.9 0.0 copy-done.6
  491.9 0.0 copy-done.8
  491.9 1.3 add_multiply_fusion
  493.2 1.5 bitcast_convert_fusion
  494.7 1.1 fusion.2
  495.8 3.5 copy.48
  499.3 3.5 update_mix.1
  502.9 9.8 %update_qkv.1 = (f32[2,128,3072]{2,1,0:T(8,128)}, f32[2,128,3072]{2,1,0:T(8,128)}, f32[2,128,3072]{2,1,0:T(8,128)}, f32[2,128,3072]{2,1,0:T(8,128)}) custom-call(bf16[4,2,128,1024]{3,2,1,0:T(8,128)(2,1)} %get-tuple-element.90.share, f32[2,128,3072]{2,1,0:T(8,128)} %weight.4, f32[2,128,3072]{2,1,0:T(8,128)} %moment.4, f32[2,128,3072]{2,1,0:T(8,128)} %average.4), custom_call_target="tpu_custom_call" | custom-call | tf_op jit(solution)/shard_map/update_qkv/pallas_call | solution.py:1321
  512.6 8.3 %update_down.1 = (f32[2,352,1024]{2,1,0:T(8,128)}, f32[2,352,1024]{2,1,0:T(8,128)}, f32[2,352,1024]{2,1,0:T(8,128)}, f32[2,352,1024]{2,1,0:T(8,128)}) custom-call(bf16[4,352,512]{2,1,0:T(8,128)(2,1)} %get-tuple-element.95.share, f32[2,352,1024]{2,1,0:T(8,128)} %weight.7, f32[2,352,1024]{2,1,0:T(8,128)} %moment.7, f32[2,352,1024]{2,1,0:T(8,128)} %average.7), custom_call_target="tpu_custom_call" | custom-call | tf_op jit(solution)/shard_map/update_down/pallas_call | solution.py:1321
  521.0 16.2 %update_inner.1 = (f32[2,128,5632]{2,1,0:T(8,128)}, f32[2,128,5632]{2,1,0:T(8,128)}, f32[2,128,5632]{2,1,0:T(8,128)}, f32[2,128,5632]{2,1,0:T(8,128)}) custom-call(bf16[4,128,2816]{2,1,0:T(8,128)(2,1)} %get-tuple-element.93.share, f32[2,128,5632]{2,1,0:T(8,128)} %weight.6, f32[2,128,5632]{2,1,0:T(8,128)} %moment.6, f32[2,128,5632]{2,1,0:T(8,128)} %average.6), custom_call_target="tpu_custom_call" | custom-call | tf_op jit(solution)/shard_map/update_inner/pallas_call | solution.py:1321
  (12 shorter events, 0.0 us)
Async XLA Ops:
  2.2 6.4 %copy-start.5 = (f32[8,1024]{1,0:T(8,128)}, f32[8,1024]{1,0:T(8,128)S(1)}, u32[]{:S(2)}) copy-start(f32[8,1024]{1,0:T(8,128)S(1)} %convert_dynamic-update-slice_fusion.gains_own) | copy-start | bytes 98308
  336.4 5.4 %copy-start = (f32[2,512,1024]{2,1,0:T(8,128)S(1)}, f32[2,512,1024]{2,1,0:T(8,128)}, u32[]{:S(2)}) copy-start(f32[2,512,1024]{2,1,0:T(8,128)} %get-tuple-element.72) | copy-start | bytes 12582916
  336.4 5.4 %copy-start.3 = (f32[512,1024]{1,0:T(8,128)S(1)}, f32[512,1024]{1,0:T(8,128)}, u32[]{:S(2)}) copy-start(f32[512,1024]{1,0:T(8,128)} %get-tuple-element.81) | copy-start | bytes 6291460
  341.9 1.6 copy-start.2
  346.3 145.6 %copy-start.6 = (f32[2,128]{1,0:T(2,128)S(1)}, f32[2,128]{1,0:T(2,128)}, u32[]{:S(2)}) copy-start(f32[2,128]{1,0:T(2,128)} %param.27) | copy-start | bytes 3076
  346.3 145.6 %copy-start.7 = (f32[2,128]{1,0:T(2,128)S(1)}, f32[2,128]{1,0:T(2,128)}, u32[]{:S(2)}) copy-start(f32[2,128]{1,0:T(2,128)} %param.37) | copy-start | bytes 3076
  346.3 145.6 %copy-start.8 = (f32[2,128]{1,0:T(2,128)S(1)}, f32[2,128]{1,0:T(2,128)}, u32[]{:S(2)}) copy-start(f32[2,128]{1,0:T(2,128)} %param.32) | copy-start | bytes 3076
  486.7 8.0 %copy-start.1 = (f32[2,512,1024]{2,1,0:T(8,128)S(1)}, f32[2,512,1024]{2,1,0:T(8,128)}, u32[]{:S(2)}) copy-start(f32[2,512,1024]{2,1,0:T(8,128)} %get-tuple-element.72) | copy-start | bytes 12582916
  486.7 8.0 %copy-start.4 = (f32[512,1024]{1,0:T(8,128)S(1)}, f32[512,1024]{1,0:T(8,128)}, u32[]{:S(2)}) copy-start(f32[512,1024]{1,0:T(8,128)} %get-tuple-element.77) | copy-start | bytes 6291460

commit v6 on v5

--- a/solution.py
+++ b/solution.py
@@ -450,31 +450,34 @@
     last_plane = max(u for u, kind_n in enumerate(UNITS) if kind_n[0] == "quarter")
     store(cot.at[y], c_rows.at[0])
     gather_gains()
-    for tick in range(len(UNITS) + Z + 2):
-        if tick < len(UNITS):
-            own_store[tick] = len(local)
-            start_unit(tick)
-        if 0 <= tick - 1 < len(UNITS) and crossed(tick - 1):
-            turn(tick - 1)
+    starts = [unit[4] for unit in UNITS]
+    for tick in range(max(starts) + Z + 2):
+        def aged(age):
+            return [u for u, begun in enumerate(starts) if tick - begun == age]
+
+        for u in aged(0):
+            own_store[u] = len(local)
+            start_unit(u)
+        for u in aged(1):
+            if crossed(u):
+                turn(u)
         for k in range(1, Z):
-            u = tick - k
-            if 0 <= u < len(UNITS) and not crossed(u):
-                hop(u, k)
-            u = tick - k - 1
-            if 0 <= u < len(UNITS) and crossed(u):
-                hop(u, k)
+            for u in aged(k):
+                if not crossed(u):
+                    hop(u, k)
+            for u in aged(k + 1):
+                if crossed(u):
+                    hop(u, k)
         if tick == 1:
             pass_gains()
         if tick == 2:
             take_gains()
             norm_rows()
-        u = tick - Z
-        if 0 <= u < len(UNITS):
+        for u in aged(Z):
             arrivals(u)
             if u == last_plane:
                 send(None, lambda: (cot.at[1 - y], c_rows.at[1], send_q, recv_q, y_peer))
-        u = tick - Z - 1
-        if 0 <= u < len(UNITS):
+        for u in aged(Z + 1):
             relay(u)
             complete(u)
             for m in range(groups):
@@ -502,12 +505,20 @@
 
 
 def unit_list(groups, inner_width, down_width):
-    units = [("quarter", n, None, False) for n in range(groups - 1)]
-    units += [("low", groups - 1, None, False), ("high", groups - 1, None, False)]
-    units += [("down", 0, slice(0, down_width // 2), True), ("down", 0, slice(down_width // 2, down_width), False)]
-    tiles = inner_width // 128
-    cuts = [128 * (tiles * n // 4) for n in range(5)]
-    return units + [("inner", 0, slice(lo, hi), n == 1) for n, (lo, hi) in enumerate(zip(cuts, cuts[1:]))]
+    units = [("quarter", n, None, False, n) for n in range(groups - 1)]
+    units += [("low", groups - 1, None, False, groups - 1), ("high", groups - 1, None, False, groups)]
+    start = groups + 1
+    for kind, tiles, turns in (("down", down_width // 128, 2), ("inner", inner_width // 128, 6)):
+        over_x = tiles // 4 if kind == "down" else -(-tiles // 4)
+        at = 0
+        for turn in range(turns):
+            for crossed, all_tiles in ((False, tiles - over_x), (True, over_x)):
+                lo, hi = all_tiles * turn // turns, all_tiles * (turn + 1) // turns
+                if hi > lo:
+                    units.append((kind, 0, slice(128 * at, 128 * (at + hi - lo)), crossed, start))
+                    at += hi - lo
+            start += 1
+    return units
 
 
 def forward(
@@ -726,6 +737,13 @@
         hidden_grad = nt(cot[:, :half], down[0]) + nt(cot[:, half:], down[1])
         gate_grad = (hidden_grad * up * (squashed * (1.0 + gate * (1.0 - squashed)))).astype(BF)
         up_grad = (hidden_grad * active).astype(BF)
+        back[...] += nt(gate_grad, inner[0]) + nt(up_grad, inner[1])
+
+        @pl.when(j == J - 1)
+        def _():
+            staged[...] = back[rows_here:, :].astype(BF)
+            exchange.start()
+
         gate_term = tn(rows, gate_grad).astype(BF)
         up_term = tn(rows, up_grad).astype(BF)
 
@@ -744,12 +762,9 @@
         for n in range(2):
             part = slice(n * half, (n + 1) * half)
             out[:, part] += nn(hidden, down[n])
-        back[...] += nt(gate_grad, inner[0]) + nt(up_grad, inner[1])
 
     @pl.when(j == J - 1)
     def _():
-        staged[...] = back[rows_here:, :].astype(BF)
-        exchange.start()
         out_theirs[...] = out[rows_here:, :].astype(BF)
         out_mine[...] = out[:rows_here, :]
         back_mine[...] = back[:rows_here, :]

time: 546 us -> 561 us (1.027)
  Pallas kernels: 506 us -> 521 us
    pallas_call x1, Pallas kernels: 143 us -> 161 us  [feed_forward(): pl.pallas_call(functools.partial(feed_forward_kernel, X, J), grid=(J + 3,...]
where the time goes in v6:
time: 561 us; the launch traced here: 552 us
  Pallas kernels  521 us (93%)
  local copies, waits for them, and re-layouts  16.8 us (3%)
  other arithmetic  13.6 us (2%)
    pallas_call x1, Pallas kernels, forward(): pl.pallas_call(functools.partial(forward_kernel, X, groups, head_size), o...  182 us
    pallas_call x1, Pallas kernels, feed_forward(): pl.pallas_call(functools.partial(feed_forward_kernel, X, J), grid=(J + 3,...  161 us
    pallas_call x1, Pallas kernels, attention_back(): pl.pallas_call(functools.partial(attention_back_kernel, X, groups, head_s...  140 us
    pallas_call x4, Pallas kernels, update(): pl.pallas_call(functools.partial(update_kernel, step_size), grid=grid, ou...  37.9 us

profile of v6, /device:TPU:0, one launch (start us, length us, event | category | flops | bytes accessed | tf_op | source)
XLA Modules:
  0.0 552.1 jit_solution(5291820692247755975)
XLA Ops:
  0.7 0.8 fusion.5
  1.5 0.1 fusion.6
  1.5 0.7 convert_dynamic-update-slice_fusion.gains_own
  2.2 0.9 copy.46.carried
  3.1 5.5 %copy_bitcast_fusion = (bf16[2,512,1024]{2,1,0:T(8,128)(2,1)}, bf16[2,512,1024]{2,1,0:T(8,128)(2,1)}) fusion(bf16[512,2,1024]{2,1,0:T(2,128)(2,1)} %param.21, bf16[512,2,1024]{2,1,0:T(2,128)(2,1)} %param.20), kind=kLoop, calls=%fused_computation.9 | loop fusion | bytes 8388608 | tf_op jit(solution)/shard_map/transpose | solution.py:1374
  8.6 0.0 copy-done.5
  8.6 181.6 %attention_forward.1 = (bf16[4,4,2,1024,256]{4,3,2,1,0:T(8,128)(2,1)}, bf16[2,1024,2816]{2,1,0:T(8,128)(2,1)}, bf16[2,2816,512]{2,1,0:T(8,128)(2,1)}, f32[8,1024...) custom-call(bf16[2,512,1024]{2,1,0:T(8,128)(2,1)} %get-tuple-element, ...), custom_call_target="tpu_custom_call" | custom-call | tf_op jit(solution)/shard_map/attention_forward/pallas_call | solution.py:536
  190.2 161.5 %feed_forward.1 = (f32[512,1024]{1,0:T(8,128)}, f32[512,1024]{1,0:T(8,128)}, bf16[512,1024]{1,0:T(8,128)(2,1)}, bf16[512,1024]{1,0:T(8,128)(2,1)}, bf16[4,128,28...) custom-call(bf16[1024,1024]{1,0:T(8,128)(2,1)} %bitcast.30, ...), custom_call_target="tpu_custom_call" | custom-call | flops 53150220288 | bytes 62914560 | tf_op jit(solution)/shard_map/feed_forward/pallas_call | solution.py:809
  351.7 0.0 copy-start
  351.7 0.0 copy-start.3
  351.7 0.9 slice.25
  352.6 3.0 multiply_reduce_fusion.2
  355.6 1.5 bitcast_convert_fusion.1
  357.1 0.0 copy-done
  357.1 0.0 copy-done.3
  357.1 0.0 copy-start.2
  357.2 1.5 multiply_reduce_fusion
  358.6 0.1 copy-done.2
  358.7 2.2 add_convert_fusion.dhb
  361.0 0.6 scatter.4.second_gain
  361.6 139.7 %attention_back.1 = (bf16[2,512,1024]{2,1,0:T(8,128)(2,1)}, f32[8,1024]{1,0:T(8,128)}, bf16[4,2,128,1024]{3,2,1,0:T(8,128)(2,1)}, bf16[4,352,512]{2,1,0:T(8,128)(2,1)}, bf16[512,1024]{1,0:T(8,128)(2,1)}) custom-call(f32[512,1]{1,0:T(8,128)} %copy.46.carried, bf16[3,2,512,1024]{3,2,1,0:T(8,128)(2,1)} %get-tuple-element.78.q.k.v, ...), custom_call_target="tpu_custom_call" | custom-call | tf_op jit(solution)/shard_map/attention_back/pallas_call | solution.py:1284
  501.3 0.0 copy-start.1
  501.3 0.0 copy-start.4
  501.4 5.2 copy.49
  506.6 1.3 add_multiply_fusion
  507.8 1.5 bitcast_convert_fusion
  509.3 1.1 fusion.2
  510.5 3.5 copy.48
  514.0 3.5 update_mix.1
  517.5 9.8 %update_qkv.1 = (f32[2,128,3072]{2,1,0:T(8,128)}, f32[2,128,3072]{2,1,0:T(8,128)}, f32[2,128,3072]{2,1,0:T(8,128)}, f32[2,128,3072]{2,1,0:T(8,128)}) custom-call(bf16[4,2,128,1024]{3,2,1,0:T(8,128)(2,1)} %get-tuple-element.90.share, f32[2,128,3072]{2,1,0:T(8,128)} %weight.4, f32[2,128,3072]{2,1,0:T(8,128)} %moment.4, f32[2,128,3072]{2,1,0:T(8,128)} %average.4), custom_call_target="tpu_custom_call" | custom-call | tf_op jit(solution)/shard_map/update_qkv/pallas_call | solution.py:1336
  527.3 8.3 %update_down.1 = (f32[2,352,1024]{2,1,0:T(8,128)}, f32[2,352,1024]{2,1,0:T(8,128)}, f32[2,352,1024]{2,1,0:T(8,128)}, f32[2,352,1024]{2,1,0:T(8,128)}) custom-call(bf16[4,352,512]{2,1,0:T(8,128)(2,1)} %get-tuple-element.95.share, f32[2,352,1024]{2,1,0:T(8,128)} %weight.7, f32[2,352,1024]{2,1,0:T(8,128)} %moment.7, f32[2,352,1024]{2,1,0:T(8,128)} %average.7), custom_call_target="tpu_custom_call" | custom-call | tf_op jit(solution)/shard_map/update_down/pallas_call | solution.py:1336
  535.6 16.2 %update_inner.1 = (f32[2,128,5632]{2,1,0:T(8,128)}, f32[2,128,5632]{2,1,0:T(8,128)}, f32[2,128,5632]{2,1,0:T(8,128)}, f32[2,128,5632]{2,1,0:T(8,128)}) custom-call(bf16[4,128,2816]{2,1,0:T(8,128)(2,1)} %get-tuple-element.93.share, f32[2,128,5632]{2,1,0:T(8,128)} %weight.6, f32[2,128,5632]{2,1,0:T(8,128)} %moment.6, f32[2,128,5632]{2,1,0:T(8,128)} %average.6), custom_call_target="tpu_custom_call" | custom-call | tf_op jit(solution)/shard_map/update_inner/pallas_call | solution.py:1336
  (12 shorter events, 0.0 us)
Async XLA Ops:
  2.2 6.4 %copy-start.5 = (f32[8,1024]{1,0:T(8,128)}, f32[8,1024]{1,0:T(8,128)S(1)}, u32[]{:S(2)}) copy-start(f32[8,1024]{1,0:T(8,128)S(1)} %convert_dynamic-update-slice_fusion.gains_own) | copy-start | bytes 98308
  351.7 5.4 copy-start
  351.7 5.4 copy-start.3
  357.1 1.6 copy-start.2
  361.6 145.0 %copy-start.6 = (f32[2,128]{1,0:T(2,128)S(1)}, f32[2,128]{1,0:T(2,128)}, u32[]{:S(2)}) copy-start(f32[2,128]{1,0:T(2,128)} %param.27) | copy-start | bytes 3076
  361.6 145.0 %copy-start.7 = (f32[2,128]{1,0:T(2,128)S(1)}, f32[2,128]{1,0:T(2,128)}, u32[]{:S(2)}) copy-start(f32[2,128]{1,0:T(2,128)} %param.37) | copy-start | bytes 3076
  361.6 145.0 %copy-start.8 = (f32[2,128]{1,0:T(2,128)S(1)}, f32[2,128]{1,0:T(2,128)}, u32[]{:S(2)}) copy-start(f32[2,128]{1,0:T(2,128)} %param.32) | copy-start | bytes 3076
  501.3 8.0 %copy-start.1 = (f32[2,512,1024]{2,1,0:T(8,128)S(1)}, f32[2,512,1024]{2,1,0:T(8,128)}, u32[]{:S(2)}) copy-start(f32[2,512,1024]{2,1,0:T(8,128)} %get-tuple-element.72) | copy-start | bytes 12582916
  501.3 8.0 %copy-start.4 = (f32[512,1024]{1,0:T(8,128)S(1)}, f32[512,1024]{1,0:T(8,128)}, u32[]{:S(2)}) copy-start(f32[512,1024]{1,0:T(8,128)} %get-tuple-element.77) | copy-start | bytes 6291460

commit v7 on v5

--- a/solution.py
+++ b/solution.py
@@ -562,7 +562,7 @@
 
 def feed_forward_kernel(
     X, J, b, c, inner, down, out_mine, back_mine, out_theirs, back_recv, inner_all, down_columns, down_sum,
-    out, back, down_here, down_there, down_from_core, down_stage, down_column, down_from_x, mine, other, from_core, summed, from_x, column, from_z, final, staged,
+    out, back, acts, down_here, down_there, down_from_core, down_stage, down_column, down_from_x, mine, other, from_core, summed, from_x, column, from_z, final, staged,
     s1, r1, s2, r2, s3, r3, s5, r5, s6, r6, s7, r7, local_sem,
     s_stage, s_own, sdx, rdx, s_column,
 ):
@@ -645,6 +645,21 @@
         out[...] = jnp.zeros_like(out)
         back[...] = jnp.zeros_like(back)
 
+    @pl.when(j < J)
+    def _():
+        rows, cot = b[...], c[...]
+        gate = nn(rows, inner[0])
+        up = nn(rows, inner[1])
+        squashed = jax.nn.sigmoid(gate)
+        active = gate * squashed
+        hidden = (active * up).astype(BF)
+        hidden_grad = nt(cot[:, :half], down[0]) + nt(cot[:, half:], down[1])
+        gate_grad = (hidden_grad * up * (squashed * (1.0 + gate * (1.0 - squashed)))).astype(BF)
+        up_grad = (hidden_grad * active).astype(BF)
+        acts[0] = hidden
+        acts[1] = gate_grad
+        acts[2] = up_grad
+
     @pl.when((j >= 2) & (j < J + 2))
     def _():
         down_store(j - 2).wait()
@@ -718,14 +733,7 @@
     @pl.when(j < J)
     def _():
         rows, cot = b[...], c[...]
-        gate = nn(rows, inner[0])
-        up = nn(rows, inner[1])
-        squashed = jax.nn.sigmoid(gate)
-        active = gate * squashed
-        hidden = (active * up).astype(BF)
-        hidden_grad = nt(cot[:, :half], down[0]) + nt(cot[:, half:], down[1])
-        gate_grad = (hidden_grad * up * (squashed * (1.0 + gate * (1.0 - squashed)))).astype(BF)
-        up_grad = (hidden_grad * active).astype(BF)
+        hidden, gate_grad, up_grad = (acts[n] for n in range(3))
         gate_term = tn(rows, gate_grad).astype(BF)
         up_term = tn(rows, up_grad).astype(BF)
 
@@ -806,7 +814,7 @@
         in_specs=[whole, whole, inner_spec, down_spec],
         out_specs=(part, part, part, ANY, ANY, ANY, ANY),
         scratch_shapes=[
-            vmem((rows, width), F32), vmem((rows, width), F32),
+            vmem((rows, width), F32), vmem((rows, width), F32), vmem((3, rows, step), BF),
             vmem((2, step, half), BF), vmem((2, step, half), BF), vmem((J, step, half), BF),
             vmem((2, step, half), BF), vmem((Z, R2, half), BF), vmem((Z, X - 1, R2, half), BF),
             vmem((2, width, step), BF), vmem((2, width, step), BF), vmem((J, width, step), BF),

time: 546 us -> 539 us (0.987)
  Pallas kernels: 506 us -> 498 us
    pallas_call x1, Pallas kernels: 143 us -> 136 us  [feed_forward(): pl.pallas_call(functools.partial(feed_forward_kernel, X, J), grid=(J + 3,...]
where the time goes in v7:
time: 539 us; the launch traced here: 530 us
  Pallas kernels  498 us (92%)
  local copies, waits for them, and re-layouts  16.8 us (3%)
  other arithmetic  13.6 us (3%)
    pallas_call x1, Pallas kernels, forward(): pl.pallas_call(functools.partial(forward_kernel, X, groups, head_size), o...  185 us
    pallas_call x1, Pallas kernels, attention_back(): pl.pallas_call(functools.partial(attention_back_kernel, X, groups, head_s...  140 us
    pallas_call x1, Pallas kernels, feed_forward(): pl.pallas_call(functools.partial(feed_forward_kernel, X, J), grid=(J + 3,...  136 us
    pallas_call x4, Pallas kernels, update(): pl.pallas_call(functools.partial(update_kernel, step_size), grid=grid, ou...  37.9 us

profile of v7, /device:TPU:0, one launch (start us, length us, event | category | flops | bytes accessed | tf_op | source)
XLA Modules:
  0.0 529.5 jit_solution(13899620181616145090)
XLA Ops:
  0.7 0.8 fusion.5
  1.5 0.1 fusion.6
  1.5 0.7 convert_dynamic-update-slice_fusion.gains_own
  2.2 0.9 copy.46.carried
  3.1 5.5 %copy_bitcast_fusion = (bf16[2,512,1024]{2,1,0:T(8,128)(2,1)}, bf16[2,512,1024]{2,1,0:T(8,128)(2,1)}) fusion(bf16[512,2,1024]{2,1,0:T(2,128)(2,1)} %param.21, bf16[512,2,1024]{2,1,0:T(2,128)(2,1)} %param.20), kind=kLoop, calls=%fused_computation.9 | loop fusion | bytes 8388608 | tf_op jit(solution)/shard_map/transpose | solution.py:1367
  8.6 0.0 copy-done.5
  8.6 184.6 %attention_forward.1 = (bf16[4,4,2,1024,256]{4,3,2,1,0:T(8,128)(2,1)}, bf16[2,1024,2816]{2,1,0:T(8,128)(2,1)}, bf16[2,2816,512]{2,1,0:T(8,128)(2,1)}, f32[8,1024...) custom-call(bf16[2,512,1024]{2,1,0:T(8,128)(2,1)} %get-tuple-element, ...), custom_call_target="tpu_custom_call" | custom-call | tf_op jit(solution)/shard_map/attention_forward/pallas_call | solution.py:525
  193.3 135.6 %feed_forward.1 = (f32[512,1024]{1,0:T(8,128)}, f32[512,1024]{1,0:T(8,128)}, bf16[512,1024]{1,0:T(8,128)(2,1)}, bf16[512,1024]{1,0:T(8,128)(2,1)}, bf16[4,128,28...) custom-call(bf16[1024,1024]{1,0:T(8,128)(2,1)} %bitcast.30, ...), custom_call_target="tpu_custom_call" | custom-call | flops 53150220288 | bytes 62914560 | tf_op jit(solution)/shard_map/feed_forward/pallas_call | solution.py:802
  328.9 0.0 copy-start
  328.9 0.0 copy-start.3
  328.9 0.9 slice.25
  329.8 3.0 multiply_reduce_fusion.2
  332.8 1.5 bitcast_convert_fusion.1
  334.3 0.0 copy-done
  334.3 0.0 copy-done.3
  334.3 0.0 copy-start.2
  334.3 1.5 multiply_reduce_fusion
  335.8 0.1 copy-done.2
  335.9 2.2 add_convert_fusion.dhb
  338.1 0.6 scatter.4.second_gain
  338.8 139.8 %attention_back.1 = (bf16[2,512,1024]{2,1,0:T(8,128)(2,1)}, f32[8,1024]{1,0:T(8,128)}, bf16[4,2,128,1024]{3,2,1,0:T(8,128)(2,1)}, bf16[4,352,512]{2,1,0:T(8,128)(2,1)}, bf16[512,1024]{1,0:T(8,128)(2,1)}) custom-call(f32[512,1]{1,0:T(8,128)} %copy.46.carried, bf16[3,2,512,1024]{3,2,1,0:T(8,128)(2,1)} %get-tuple-element.78.q.k.v, ...), custom_call_target="tpu_custom_call" | custom-call | tf_op jit(solution)/shard_map/attention_back/pallas_call | solution.py:1277
  478.6 0.0 copy-start.1
  478.6 0.0 copy-start.4
  478.6 5.2 copy.49
  483.8 1.3 add_multiply_fusion
  485.1 1.5 bitcast_convert_fusion
  486.6 1.1 fusion.2
  487.7 3.5 copy.48
  491.2 3.5 update_mix.1
  494.7 9.8 %update_qkv.1 = (f32[2,128,3072]{2,1,0:T(8,128)}, f32[2,128,3072]{2,1,0:T(8,128)}, f32[2,128,3072]{2,1,0:T(8,128)}, f32[2,128,3072]{2,1,0:T(8,128)}) custom-call(bf16[4,2,128,1024]{3,2,1,0:T(8,128)(2,1)} %get-tuple-element.90.share, f32[2,128,3072]{2,1,0:T(8,128)} %weight.4, f32[2,128,3072]{2,1,0:T(8,128)} %moment.4, f32[2,128,3072]{2,1,0:T(8,128)} %average.4), custom_call_target="tpu_custom_call" | custom-call | tf_op jit(solution)/shard_map/update_qkv/pallas_call | solution.py:1329
  504.5 8.3 %update_down.1 = (f32[2,352,1024]{2,1,0:T(8,128)}, f32[2,352,1024]{2,1,0:T(8,128)}, f32[2,352,1024]{2,1,0:T(8,128)}, f32[2,352,1024]{2,1,0:T(8,128)}) custom-call(bf16[4,352,512]{2,1,0:T(8,128)(2,1)} %get-tuple-element.95.share, f32[2,352,1024]{2,1,0:T(8,128)} %weight.7, f32[2,352,1024]{2,1,0:T(8,128)} %moment.7, f32[2,352,1024]{2,1,0:T(8,128)} %average.7), custom_call_target="tpu_custom_call" | custom-call | tf_op jit(solution)/shard_map/update_down/pallas_call | solution.py:1329
  512.8 16.2 %update_inner.1 = (f32[2,128,5632]{2,1,0:T(8,128)}, f32[2,128,5632]{2,1,0:T(8,128)}, f32[2,128,5632]{2,1,0:T(8,128)}, f32[2,128,5632]{2,1,0:T(8,128)}) custom-call(bf16[4,128,2816]{2,1,0:T(8,128)(2,1)} %get-tuple-element.93.share, f32[2,128,5632]{2,1,0:T(8,128)} %weight.6, f32[2,128,5632]{2,1,0:T(8,128)} %moment.6, f32[2,128,5632]{2,1,0:T(8,128)} %average.6), custom_call_target="tpu_custom_call" | custom-call | tf_op jit(solution)/shard_map/update_inner/pallas_call | solution.py:1329
  (12 shorter events, 0.0 us)
Async XLA Ops:
  2.2 6.4 %copy-start.5 = (f32[8,1024]{1,0:T(8,128)}, f32[8,1024]{1,0:T(8,128)S(1)}, u32[]{:S(2)}) copy-start(f32[8,1024]{1,0:T(8,128)S(1)} %convert_dynamic-update-slice_fusion.gains_own) | copy-start | bytes 98308
  328.9 5.4 %copy-start = (f32[2,512,1024]{2,1,0:T(8,128)S(1)}, f32[2,512,1024]{2,1,0:T(8,128)}, u32[]{:S(2)}) copy-start(f32[2,512,1024]{2,1,0:T(8,128)} %get-tuple-element.72) | copy-start | bytes 12582916
  328.9 5.4 %copy-start.3 = (f32[512,1024]{1,0:T(8,128)S(1)}, f32[512,1024]{1,0:T(8,128)}, u32[]{:S(2)}) copy-start(f32[512,1024]{1,0:T(8,128)} %get-tuple-element.81) | copy-start | bytes 6291460
  334.3 1.6 copy-start.2
  338.8 145.0 %copy-start.6 = (f32[2,128]{1,0:T(2,128)S(1)}, f32[2,128]{1,0:T(2,128)}, u32[]{:S(2)}) copy-start(f32[2,128]{1,0:T(2,128)} %param.27) | copy-start | bytes 3076
  338.8 145.0 %copy-start.7 = (f32[2,128]{1,0:T(2,128)S(1)}, f32[2,128]{1,0:T(2,128)}, u32[]{:S(2)}) copy-start(f32[2,128]{1,0:T(2,128)} %param.37) | copy-start | bytes 3076
  338.8 145.0 %copy-start.8 = (f32[2,128]{1,0:T(2,128)S(1)}, f32[2,128]{1,0:T(2,128)}, u32[]{:S(2)}) copy-start(f32[2,128]{1,0:T(2,128)} %param.32) | copy-start | bytes 3076
  478.6 8.0 %copy-start.1 = (f32[2,512,1024]{2,1,0:T(8,128)S(1)}, f32[2,512,1024]{2,1,0:T(8,128)}, u32[]{:S(2)}) copy-start(f32[2,512,1024]{2,1,0:T(8,128)} %get-tuple-element.72) | copy-start | bytes 12582916
  478.6 8.0 %copy-start.4 = (f32[512,1024]{1,0:T(8,128)S(1)}, f32[512,1024]{1,0:T(8,128)}, u32[]{:S(2)}) copy-start(f32[512,1024]{1,0:T(8,128)} %get-tuple-element.77) | copy-start | bytes 6291460

commit v8 on v7

--- a/solution.py
+++ b/solution.py
@@ -958,111 +958,6 @@
         def _():
             edge_recv[...] = jnp.zeros_like(edge_recv)
 
-    def active(first):
-        return (i >= first) & (i < first + subs)
-
-    @pl.when(active(2))
-    def _():
-        n = i - 2
-        to_core(n).wait_recv()
-
-        @pl.when(n >= 2)
-        def _():
-            to_y(n - 2).wait_send()
-
-        @pl.when(n >= 3)
-        def _():
-            for j in range(1, X):
-                to_x_early(n - 3, j).wait_send()
-
-        def both(t):
-            return (mine[n % 2, t].astype(F32) + from_core[n % slots, t].astype(F32)).astype(BF)
-
-        send_y[n % 2] = both(1 - y)
-        to_y(n).start()
-        for t in range(2):
-            summed[n % 3, 1 + t] = both(2 + t).reshape(summed.shape[2:])
-        for j in range(1, X):
-            to_x_early(n, j).start()
-        keep_y[n % 2] = both(y)
-
-        @pl.when(n < subs - slots)
-        def _():
-            pl.semaphore_signal(free, inc=1, device_id=core_peer, device_id_type=MESH)
-
-    @pl.when(active(3))
-    def _():
-        n = i - 3
-        to_y(n).wait_recv()
-
-        @pl.when(n >= 3)
-        def _():
-            for j in range(1, X):
-                to_x_late(n - 3, j).wait_send()
-
-        total = (keep_y[n % 2].astype(F32) + from_y[n].astype(F32)).astype(BF)
-        summed[n % 3, 0] = total.reshape(summed.shape[2:])
-        for j in range(1, X):
-            to_x_late(n, j).start()
-
-    @pl.when(active(4))
-    def _():
-        n = i - 4
-        for j in range(1, X):
-            to_x_early(n, j).wait_recv()
-            to_x_late(n, j).wait_recv()
-
-        @pl.when(n >= 2)
-        def _():
-            for j in range(1, Z):
-                to_z(n - 2, j).wait_send()
-
-        total = summed[n % 3, :, :, x].astype(F32) + total_of([from_x[n, j].astype(F32) for j in range(X - 1)])
-        column[n % 2] = total.astype(BF)
-        for j in range(1, Z):
-            to_z(n, j).start()
-
-    @pl.when(active(5))
-    def _():
-        n = i - 5
-        for j in range(1, Z):
-            to_z(n, j).wait_recv()
-        total = column[n % 2, :, z].astype(F32) + total_of([from_z[n, j].astype(F32) for j in range(Z - 1)])
-        total = total.astype(BF)
-        final[n] = total[0]
-        plane[n] = total[1:]
-        to_plane(n).start()
-        keep(n, 0).start()
-        for d in range(1, 3):
-            share(n, d).start()
-
-    @pl.when(active(6))
-    def _():
-        n = i - 6
-        to_plane(n).wait_recv()
-        share(n, 2).wait_recv()
-        relay(n).start()
-        final_plane[n] = (plane[n].astype(F32) + from_plane[n].astype(F32)).astype(BF)
-        for t in range(2):
-            keep(n, t + 1).start()
-            share_core(n, t).start()
-
-    @pl.when(i == 4)
-    def _():
-        down_load.wait()
-        for k in range(1, Z):
-            down_to_z(k).wait_recv()
-        total = down_mine[...].astype(F32) + total_of([down_from_z[k].astype(F32) for k in range(Z - 1)])
-        down_final[...] = total.astype(BF)
-        down_keep.start()
-        for d in range(1, 3):
-            down_share(d).start()
-
-    @pl.when(i == 6)
-    def _():
-        down_share(2).wait_recv()
-        down_relay().start()
-
     @pl.when((i < subs) & (i % 2 == 0))
     def _():
         m = i // 2
@@ -1124,6 +1019,111 @@
             total = terms_here[row] + jnp.where(last, 0.0, pltpu.roll(terms_before[row], frames - 1, 0))
             grads[1 + row // 2, row % 2] = total.astype(BF)
             tails[row] = total[frames - 16 :, :]
+
+    def active(first):
+        return (i >= first) & (i < first + subs)
+
+    @pl.when(active(2))
+    def _():
+        n = i - 2
+        to_core(n).wait_recv()
+
+        @pl.when(n >= 2)
+        def _():
+            to_y(n - 2).wait_send()
+
+        @pl.when(n >= 3)
+        def _():
+            for j in range(1, X):
+                to_x_early(n - 3, j).wait_send()
+
+        def both(t):
+            return (mine[n % 2, t].astype(F32) + from_core[n % slots, t].astype(F32)).astype(BF)
+
+        send_y[n % 2] = both(1 - y)
+        to_y(n).start()
+        for t in range(2):
+            summed[n % 3, 1 + t] = both(2 + t).reshape(summed.shape[2:])
+        for j in range(1, X):
+            to_x_early(n, j).start()
+        keep_y[n % 2] = both(y)
+
+        @pl.when(n < subs - slots)
+        def _():
+            pl.semaphore_signal(free, inc=1, device_id=core_peer, device_id_type=MESH)
+
+    @pl.when(active(3))
+    def _():
+        n = i - 3
+        to_y(n).wait_recv()
+
+        @pl.when(n >= 3)
+        def _():
+            for j in range(1, X):
+                to_x_late(n - 3, j).wait_send()
+
+        total = (keep_y[n % 2].astype(F32) + from_y[n].astype(F32)).astype(BF)
+        summed[n % 3, 0] = total.reshape(summed.shape[2:])
+        for j in range(1, X):
+            to_x_late(n, j).start()
+
+    @pl.when(active(4))
+    def _():
+        n = i - 4
+        for j in range(1, X):
+            to_x_early(n, j).wait_recv()
+            to_x_late(n, j).wait_recv()
+
+        @pl.when(n >= 2)
+        def _():
+            for j in range(1, Z):
+                to_z(n - 2, j).wait_send()
+
+        total = summed[n % 3, :, :, x].astype(F32) + total_of([from_x[n, j].astype(F32) for j in range(X - 1)])
+        column[n % 2] = total.astype(BF)
+        for j in range(1, Z):
+            to_z(n, j).start()
+
+    @pl.when(active(5))
+    def _():
+        n = i - 5
+        for j in range(1, Z):
+            to_z(n, j).wait_recv()
+        total = column[n % 2, :, z].astype(F32) + total_of([from_z[n, j].astype(F32) for j in range(Z - 1)])
+        total = total.astype(BF)
+        final[n] = total[0]
+        plane[n] = total[1:]
+        to_plane(n).start()
+        keep(n, 0).start()
+        for d in range(1, 3):
+            share(n, d).start()
+
+    @pl.when(active(6))
+    def _():
+        n = i - 6
+        to_plane(n).wait_recv()
+        share(n, 2).wait_recv()
+        relay(n).start()
+        final_plane[n] = (plane[n].astype(F32) + from_plane[n].astype(F32)).astype(BF)
+        for t in range(2):
+            keep(n, t + 1).start()
+            share_core(n, t).start()
+
+    @pl.when(i == 4)
+    def _():
+        down_load.wait()
+        for k in range(1, Z):
+            down_to_z(k).wait_recv()
+        total = down_mine[...].astype(F32) + total_of([down_from_z[k].astype(F32) for k in range(Z - 1)])
+        down_final[...] = total.astype(BF)
+        down_keep.start()
+        for d in range(1, 3):
+            down_share(d).start()
+
+    @pl.when(i == 6)
+    def _():
+        down_share(2).wait_recv()
+        down_relay().start()
 
     @pl.when((i < subs) & (i % 2 == 1))
     def _():

time: 539 us -> 546 us (1.013)
  Pallas kernels: 498 us -> 506 us
    pallas_call x1, Pallas kernels: 140 us -> 148 us  [attention_back(): pl.pallas_call(functools.partial(attention_back_kernel, X, groups, head_s...]
where the time goes in v8:
time: 546 us; the launch traced here: 538 us
  Pallas kernels  506 us (93%)
  local copies, waits for them, and re-layouts  16.8 us (3%)
  other arithmetic  13.6 us (2%)
    pallas_call x1, Pallas kernels, forward(): pl.pallas_call(functools.partial(forward_kernel, X, groups, head_size), o...  185 us
    pallas_call x1, Pallas kernels, attention_back(): pl.pallas_call(functools.partial(attention_back_kernel, X, groups, head_s...  148 us
    pallas_call x1, Pallas kernels, feed_forward(): pl.pallas_call(functools.partial(feed_forward_kernel, X, J), grid=(J + 3,...  136 us
    pallas_call x4, Pallas kernels, update(): pl.pallas_call(functools.partial(update_kernel, step_size), grid=grid, ou...  37.9 us

profile of v8, /device:TPU:0, one launch (start us, length us, event | category | flops | bytes accessed | tf_op | source)
XLA Modules:
  0.0 537.6 jit_solution(8264973749666984218)
XLA Ops:
  0.7 0.8 fusion.5
  1.5 0.1 fusion.6
  1.5 0.7 convert_dynamic-update-slice_fusion.gains_own
  2.2 0.9 copy.46.carried
  3.1 5.5 %copy_bitcast_fusion = (bf16[2,512,1024]{2,1,0:T(8,128)(2,1)}, bf16[2,512,1024]{2,1,0:T(8,128)(2,1)}) fusion(bf16[512,2,1024]{2,1,0:T(2,128)(2,1)} %param.21, bf16[512,2,1024]{2,1,0:T(2,128)(2,1)} %param.20), kind=kLoop, calls=%fused_computation.9 | loop fusion | bytes 8388608 | tf_op jit(solution)/shard_map/transpose | solution.py:1367
  8.6 0.0 copy-done.5
  8.6 184.6 %attention_forward.1 = (bf16[4,4,2,1024,256]{4,3,2,1,0:T(8,128)(2,1)}, bf16[2,1024,2816]{2,1,0:T(8,128)(2,1)}, bf16[2,2816,512]{2,1,0:T(8,128)(2,1)}, f32[8,1024...) custom-call(bf16[2,512,1024]{2,1,0:T(8,128)(2,1)} %get-tuple-element, ...), custom_call_target="tpu_custom_call" | custom-call | tf_op jit(solution)/shard_map/attention_forward/pallas_call | solution.py:525
  193.3 135.6 %feed_forward.1 = (f32[512,1024]{1,0:T(8,128)}, f32[512,1024]{1,0:T(8,128)}, bf16[512,1024]{1,0:T(8,128)(2,1)}, bf16[512,1024]{1,0:T(8,128)(2,1)}, bf16[4,128,28...) custom-call(bf16[1024,1024]{1,0:T(8,128)(2,1)} %bitcast.30, ...), custom_call_target="tpu_custom_call" | custom-call | flops 53150220288 | bytes 62914560 | tf_op jit(solution)/shard_map/feed_forward/pallas_call | solution.py:802
  328.9 0.0 copy-start
  328.9 0.0 copy-start.3
  328.9 0.9 slice.25
  329.8 3.0 multiply_reduce_fusion.2
  332.8 1.5 bitcast_convert_fusion.1
  334.3 0.0 copy-done
  334.3 0.0 copy-done.3
  334.3 0.0 copy-start.2
  334.3 1.5 multiply_reduce_fusion
  335.8 0.1 copy-done.2
  335.9 2.2 add_convert_fusion.dhb
  338.1 0.6 scatter.4.second_gain
  338.8 147.8 %attention_back.1 = (bf16[2,512,1024]{2,1,0:T(8,128)(2,1)}, f32[8,1024]{1,0:T(8,128)}, bf16[4,2,128,1024]{3,2,1,0:T(8,128)(2,1)}, bf16[4,352,512]{2,1,0:T(8,128)(2,1)}, bf16[512,1024]{1,0:T(8,128)(2,1)}) custom-call(f32[512,1]{1,0:T(8,128)} %copy.46.carried, bf16[3,2,512,1024]{3,2,1,0:T(8,128)(2,1)} %get-tuple-element.78.q.k.v, ...), custom_call_target="tpu_custom_call" | custom-call | tf_op jit(solution)/shard_map/attention_back/pallas_call | solution.py:1277
  486.6 0.0 copy-start.1
  486.6 0.0 copy-start.4
  486.6 5.2 copy.49
  491.8 1.3 add_multiply_fusion
  493.1 1.5 bitcast_convert_fusion
  494.6 1.1 fusion.2
  495.7 3.5 copy.48
  499.2 3.5 update_mix.1
  502.8 9.8 %update_qkv.1 = (f32[2,128,3072]{2,1,0:T(8,128)}, f32[2,128,3072]{2,1,0:T(8,128)}, f32[2,128,3072]{2,1,0:T(8,128)}, f32[2,128,3072]{2,1,0:T(8,128)}) custom-call(bf16[4,2,128,1024]{3,2,1,0:T(8,128)(2,1)} %get-tuple-element.90.share, f32[2,128,3072]{2,1,0:T(8,128)} %weight.4, f32[2,128,3072]{2,1,0:T(8,128)} %moment.4, f32[2,128,3072]{2,1,0:T(8,128)} %average.4), custom_call_target="tpu_custom_call" | custom-call | tf_op jit(solution)/shard_map/update_qkv/pallas_call | solution.py:1329
  512.6 8.3 %update_down.1 = (f32[2,352,1024]{2,1,0:T(8,128)}, f32[2,352,1024]{2,1,0:T(8,128)}, f32[2,352,1024]{2,1,0:T(8,128)}, f32[2,352,1024]{2,1,0:T(8,128)}) custom-call(bf16[4,352,512]{2,1,0:T(8,128)(2,1)} %get-tuple-element.95.share, f32[2,352,1024]{2,1,0:T(8,128)} %weight.7, f32[2,352,1024]{2,1,0:T(8,128)} %moment.7, f32[2,352,1024]{2,1,0:T(8,128)} %average.7), custom_call_target="tpu_custom_call" | custom-call | tf_op jit(solution)/shard_map/update_down/pallas_call | solution.py:1329
  520.9 16.2 %update_inner.1 = (f32[2,128,5632]{2,1,0:T(8,128)}, f32[2,128,5632]{2,1,0:T(8,128)}, f32[2,128,5632]{2,1,0:T(8,128)}, f32[2,128,5632]{2,1,0:T(8,128)}) custom-call(bf16[4,128,2816]{2,1,0:T(8,128)(2,1)} %get-tuple-element.93.share, f32[2,128,5632]{2,1,0:T(8,128)} %weight.6, f32[2,128,5632]{2,1,0:T(8,128)} %moment.6, f32[2,128,5632]{2,1,0:T(8,128)} %average.6), custom_call_target="tpu_custom_call" | custom-call | tf_op jit(solution)/shard_map/update_inner/pallas_call | solution.py:1329
  (12 shorter events, 0.0 us)
Async XLA Ops:
  2.2 6.4 %copy-start.5 = (f32[8,1024]{1,0:T(8,128)}, f32[8,1024]{1,0:T(8,128)S(1)}, u32[]{:S(2)}) copy-start(f32[8,1024]{1,0:T(8,128)S(1)} %convert_dynamic-update-slice_fusion.gains_own) | copy-start | bytes 98308
  328.9 5.4 %copy-start = (f32[2,512,1024]{2,1,0:T(8,128)S(1)}, f32[2,512,1024]{2,1,0:T(8,128)}, u32[]{:S(2)}) copy-start(f32[2,512,1024]{2,1,0:T(8,128)} %get-tuple-element.72) | copy-start | bytes 12582916
  328.9 5.4 %copy-start.3 = (f32[512,1024]{1,0:T(8,128)S(1)}, f32[512,1024]{1,0:T(8,128)}, u32[]{:S(2)}) copy-start(f32[512,1024]{1,0:T(8,128)} %get-tuple-element.81) | copy-start | bytes 6291460
  334.3 1.6 copy-start.2
  338.8 153.1 %copy-start.6 = (f32[2,128]{1,0:T(2,128)S(1)}, f32[2,128]{1,0:T(2,128)}, u32[]{:S(2)}) copy-start(f32[2,128]{1,0:T(2,128)} %param.27) | copy-start | bytes 3076
  338.8 153.1 %copy-start.7 = (f32[2,128]{1,0:T(2,128)S(1)}, f32[2,128]{1,0:T(2,128)}, u32[]{:S(2)}) copy-start(f32[2,128]{1,0:T(2,128)} %param.37) | copy-start | bytes 3076
  338.8 153.1 %copy-start.8 = (f32[2,128]{1,0:T(2,128)S(1)}, f32[2,128]{1,0:T(2,128)}, u32[]{:S(2)}) copy-start(f32[2,128]{1,0:T(2,128)} %param.32) | copy-start | bytes 3076
  486.6 8.0 %copy-start.1 = (f32[2,512,1024]{2,1,0:T(8,128)S(1)}, f32[2,512,1024]{2,1,0:T(8,128)}, u32[]{:S(2)}) copy-start(f32[2,512,1024]{2,1,0:T(8,128)} %get-tuple-element.72) | copy-start | bytes 12582916
  486.6 8.0 %copy-start.4 = (f32[512,1024]{1,0:T(8,128)S(1)}, f32[512,1024]{1,0:T(8,128)}, u32[]{:S(2)}) copy-start(f32[512,1024]{1,0:T(8,128)} %get-tuple-element.77) | copy-start | bytes 6291460
